TPU v7x, 32 devices: a whole 2x2x4 slice. The times are simulated.
32 devices in a mesh: src: 8 (over z, y), rcv: 4 (over x, core).
Axes of the slice: x: 2, y: 2, z: 4, core: 2. Of those that a mesh axis runs over, the one named last changes fastest.
Arguments:
- history: bfloat16 [12, 24576], P(None, 'src'), may hold values from 0.19921875 to 2
- kernel: bfloat16 [12, 8, 4, 24, 64, 128], P(None, 'src', 'rcv'), may hold values from -0.15625 to 0.15625
- scales: float32 [12, 8, 4, 24], P(None, 'src', 'rcv'), may hold values from 0.25 to 4
- block_rows: int32 [12, 8, 4, 24], P(None, 'src', 'rcv'), may hold values from 0 to 95
- block_cols: int32 [12, 8, 4, 24], P(None, 'src', 'rcv'), may hold values from 0 to 47
- shear_pre: float32 [24576], P(('src', 'rcv')), may hold values from 0.5 to 2
- sigma_pre: float32 [24576], P(('src', 'rcv')), may hold values from 2 to 4
- friction_a: float32 [24576], P(('src', 'rcv')), may hold values from 0.15 to 0.5
- state_rate: float32 [24576], P(('src', 'rcv')), may hold values from 0.5 to 2
- state_init: float32 [24576], P(('src', 'rcv')), may hold values from -1 to 1
Outputs:
- slip_rates: float32 [4, 24576], P(None, ('src', 'rcv'))
- state_final: float32 [24576], P(('src', 'rcv'))
All inputs are finite; a program needn't handle non-finite values.
Results may differ from a plain program's by a relative error of at most 0.0022.
Values may be sent and summed in bfloat16 or wider, within the bound.
No kernel may reach another device: no remote copies, remote signals or barrier semaphores. Data moves between devices by JAX's collectives and lax.ppermute only.
A program may use at most 64 MiB of HBM per device.

v0:
```python
import jax
import jax.numpy as jnp
from jax import lax
from jax.sharding import PartitionSpec as P

STEPS = 4
NEWTON_ITERS = 4


DAMPING = 1.0
LOADING = 0.05
TIME_STEP = 0.2


def inverse_sinh(value):
    magnitude = jnp.abs(value)
    result = jnp.log(magnitude + jnp.sqrt(1.0 + magnitude * magnitude))
    return jnp.where(value < 0.0, -result, result)


def friction_solve(stress, step_no, guess, state_now, shear_pre, sigma_pre, friction_a, state_rate):
    comp_width = stress.shape[1] // 2
    shear_total = stress[:, :comp_width].reshape(-1) + shear_pre + LOADING * (step_no + 1)
    normal = sigma_pre * (1.0 + 0.5 * jnp.tanh(stress[:, comp_width:].reshape(-1)))
    strength = friction_a * normal
    factor = 0.5 * jnp.exp(state_now)
    slip_rate = guess
    for attempt in range(NEWTON_ITERS):
        scaled = slip_rate * factor
        misfit = shear_total - DAMPING * slip_rate - strength * inverse_sinh(scaled)
        derivative = -DAMPING - strength * factor / jnp.sqrt(1.0 + scaled * scaled)
        slip_rate = slip_rate - misfit / derivative
    next_state = state_now + TIME_STEP * state_rate * jnp.tanh(
        jnp.exp(-state_now) - jnp.abs(slip_rate)
    )
    return (slip_rate, next_state)


def recent_terms(panels, weights, row_ids, col_ids, newest_first, recv_blocks):
    lag_count = len(newest_first)
    stacked = jnp.stack(newest_first)
    picked = stacked[jnp.arange(lag_count)[:, None], col_ids[:lag_count]]
    partial_terms = jnp.einsum(
        "lkj,lkjm->lkm", picked, panels[:lag_count], preferred_element_type=jnp.float32
    )
    partial_terms = partial_terms * weights[:lag_count, :, None]
    flat_terms = partial_terms.reshape(-1, partial_terms.shape[-1])
    return jax.ops.segment_sum(
        flat_terms, row_ids[:lag_count].reshape(-1), num_segments=recv_blocks
    )


def per_device(
    history,
    kernel,
    scales,
    block_rows,
    block_cols,
    shear_pre,
    sigma_pre,
    friction_a,
    state_rate,
    state_init,
):
    lag_count = kernel.shape[0]
    slot_count = kernel.shape[3]
    block_width = kernel.shape[4]
    panels = kernel.reshape(lag_count, slot_count, block_width, 2 * block_width)
    weights = scales.reshape(lag_count, slot_count)
    row_ids = block_rows.reshape(lag_count, slot_count)
    col_ids = block_cols.reshape(lag_count, slot_count)
    src_blocks = history.shape[1] // block_width
    recv_blocks = src_blocks * lax.axis_size("src") // lax.axis_size("rcv")
    own_count = shear_pre.shape[0]
    hist_blocks = history.reshape(lag_count, src_blocks, block_width)
    lag_index = jnp.arange(lag_count)[:, None]
    step_index = jnp.arange(STEPS)[None, :]
    hist_rows = jnp.clip(lag_count - 1 - lag_index + step_index, 0, lag_count - 1)
    picked = hist_blocks[hist_rows[:, None, :], col_ids[:, :, None]]
    picked = jnp.where((step_index <= lag_index)[:, None, :, None], picked, jnp.zeros_like(picked))
    older = jnp.einsum("lksj,lkjm->lksm", picked, panels, preferred_element_type=jnp.float32)
    older = older * weights[:, :, None, None]
    older_part = jax.ops.segment_sum(
        older.reshape(lag_count * slot_count, STEPS, 2 * block_width),
        row_ids.reshape(-1),
        num_segments=recv_blocks,
    )
    guess = lax.dynamic_slice_in_dim(
        history[lag_count - 1], lax.axis_index("rcv") * own_count, own_count
    ).astype(jnp.float32)
    state_now = state_init
    recent_rates = []
    outputs = []
    older_sum = lax.psum_scatter(older_part, "src", scatter_dimension=0, tiled=True)
    for step_no in range(STEPS):
        if step_no > 0:
            fresh = recent_terms(panels, weights, row_ids, col_ids, recent_rates[::-1], recv_blocks)
        stress = older_sum[:, step_no]
        if step_no > 0:
            stress = stress + lax.psum_scatter(fresh, "src", scatter_dimension=0, tiled=True)
        slip_rate, state_now = friction_solve(
            stress, step_no, guess, state_now, shear_pre, sigma_pre, friction_a, state_rate
        )
        outputs.append(slip_rate)
        if step_no + 1 < STEPS:
            rounded = slip_rate.astype(jnp.bfloat16)
            source_rates = lax.all_gather(rounded, "rcv", axis=0, tiled=True)
            recent_rates.append(source_rates.reshape(src_blocks, block_width))
        guess = slip_rate
    return (jnp.stack(outputs), state_now)


def solution(mesh):
    return jax.shard_map(
        per_device,
        mesh=mesh,
        in_specs=(
            P(None, "src"),
            P(None, "src", "rcv", None, None, None),
            P(None, "src", "rcv", None),
            P(None, "src", "rcv", None),
            P(None, "src", "rcv", None),
            P(("src", "rcv")),
            P(("src", "rcv")),
            P(("src", "rcv")),
            P(("src", "rcv")),
            P(("src", "rcv")),
        ),
        out_specs=(P(None, ("src", "rcv")), P(("src", "rcv"))),
        check_vma=False,
    )
```

profile of v0, /device:TPU:0, one launch (start us, length us, event | category | flops | bytes accessed | tf_op | source)
XLA Modules:
  0.0 223.3 jit_solution(8065364403526946603)
XLA Ops:
  8.3 1.1 reshape.254
  10.0 0.7 reduce.1
  10.8 7.1 %gather_fusion = bf16[1152,64]{1,0:T(8,128)(2,1)S(1)} fusion(bf16[12,48,64]{2,1,0:T(8,128)(2,1)S(1)} %reshape.254, s32[1152]{0:T(1024)S(1)} %reshape.266), kind=kCustom, calls=%fused_computation | custom fusion | bytes 304128 | tf_op jit(solution)/shard_map/gather | solution.py:79
  18.1 3.8 %fusion.5 = f32[12,24,4,128]{3,2,1,0:T(4,128)S(1)} fusion(bf16[12,1,1,24,64,128]{5,4,3,2,1,0:T(8,128)(2,1)} %param.11, f32[12,24]{1,0:T(8,128)S(1)} %bitcast.94, bf16[12,24,4,64]{3,2,1,0:T(4,128)(2,1)S(1)} %bitcast.82, pred[12,4]{1,0:T(8,128)(4,1)S(1)} %iota_compare_fusion), kind=kOutput, calls=%fused_computation.10 | convolution fusion | flops 19095552 | bytes 5457072 | tf_op jit(solution)/shard_map/lksj,lkjm->lksm/dot_general | solution.py:81
  21.9 10.9 %scatter_fusion = f32[96,4,128]{2,1,0:T(4,128)S(1)} fusion(f32[96,4,128]{2,1,0:T(4,128)S(1)} %broadcast_in_dim.20, s32[288]{0:T(512)S(1)} %reshape.294, f32[288,4,128]{2,1,0:T(4,128)S(1)} %bitcast.81), kind=kCustom, calls=%fused_computation.4 | custom fusion | flops 147456 | bytes 1770624 | tf_op jit(solution)/shard_map/scatter-add | solution.py:83
  33.4 0.8 slice.97
  35.7 70.6 %all-reduce.10.cloned.1.call-done = f32[96,4,128]{2,1,0:T(4,128)} async-done(((f32[96,4,128]{2,1,0:T(4,128)}), f32[96,4,128]{2,1,0:T(4,128)}) %all-reduce.10.cloned.1.call-update) | async-done | bytes 196624
  106.3 0.9 constant_dynamic-slice_fusion.3
  107.6 5.2 %all-gather = bf16[4,1,768]{2,1,0:T(2,128)(2,1)S(1)} all-gather(bf16[1,1,768]{2,1,0:T(2,128)(2,1)S(1)} %reshape.329), channel_id=1, replica_groups=mesh['src'=8,'rcv'=4] {'rcv'}, dimensions={0}, use_global_device_ids=true | all-gather | bytes 7680 | tf_op jit(solution)/shard_map/all_gather | solution.py:107
  112.9 0.7 gather_fusion.1
  113.6 1.2 fusion.14
  114.8 0.8 scatter_custom_fusion.1
  115.6 22.1 %fusion = f32[16,128]{1,0:T(8,128)S(1)} fusion(f32[96,128]{1,0:T(8,128)S(1)} %scatter_custom_fusion.1), kind=kCustom, calls=%all-reduce-scatter | all-reduce-scatter fusion | flops 16385 | bytes 57856
  137.7 1.4 collective-permute-start
  139.1 1.3 collective-permute-start.1
  142.3 5.2 %all-gather.1 = bf16[4,1,768]{2,1,0:T(2,128)(2,1)S(1)} all-gather(bf16[1,1,768]{2,1,0:T(2,128)(2,1)S(1)} %reshape.331), channel_id=1, replica_groups=mesh['src'=8,'rcv'=4] {'rcv'}, dimensions={0}, use_global_device_ids=true | all-gather | bytes 7680 | tf_op jit(solution)/shard_map/all_gather | solution.py:107
  147.6 1.0 gather_fusion.2
  148.7 1.4 fusion.11
  150.2 0.8 scatter_custom_fusion.2
  151.0 22.5 %fusion.1 = f32[16,128]{1,0:T(8,128)S(1)} fusion(f32[96,128]{1,0:T(8,128)S(1)} %scatter_custom_fusion.2), kind=kCustom, calls=%all-reduce-scatter.1 | all-reduce-scatter fusion | flops 16385 | bytes 57856
  173.5 1.8 collective-permute-start.2
  175.4 1.3 collective-permute-start.3
  176.8 1.2 collective-permute-done.3
  178.6 5.2 %all-gather.2 = bf16[4,1,768]{2,1,0:T(2,128)(2,1)S(1)} all-gather(bf16[1,1,768]{2,1,0:T(2,128)(2,1)S(1)} %reshape.333), channel_id=1, replica_groups=mesh['src'=8,'rcv'=4] {'rcv'}, dimensions={0}, use_global_device_ids=true | all-gather | bytes 7680 | tf_op jit(solution)/shard_map/all_gather | solution.py:107
  183.9 1.5 gather_fusion.3
  185.5 1.7 fusion.8
  187.2 0.8 scatter_custom_fusion.3
  188.1 22.3 %fusion.2 = f32[16,128]{1,0:T(8,128)S(1)} fusion(f32[96,128]{1,0:T(8,128)S(1)} %scatter_custom_fusion.3), kind=kCustom, calls=%all-reduce-scatter.2 | all-reduce-scatter fusion | flops 16385 | bytes 57856
  210.4 1.6 collective-permute-start.4
  212.0 1.3 collective-permute-start.5
  213.4 1.3 collective-permute-done.5
  215.1 0.7 multiply_add_fusion
  (100 shorter events, 7.3 us)
Async XLA Ops:
  7.2 99.2 %all-reduce.10.cloned.1.call-start = ((), (), s32[]{:S(2)}) async-start(), calls=%async_computation | async-start | bytes 393216
  17.9 16.4 %copy-start.6 = (s32[12,1,1,24]{3,2,1,0:T(1,128)S(1)}, s32[12,1,1,24]{3,2,1,0:T(1,128)}, u32[]{:S(2)}) copy-start(s32[12,1,1,24]{3,2,1,0:T(1,128)} %param.14) | copy-start | bytes 3460
  17.9 16.4 %copy-start.7 = (f32[12,1,1,24]{3,2,1,0:T(1,128)S(1)}, f32[12,1,1,24]{3,2,1,0:T(1,128)}, u32[]{:S(2)}) copy-start(f32[12,1,1,24]{3,2,1,0:T(1,128)} %param.12) | copy-start | bytes 3460
  17.9 16.4 %slice-start = ((s32[12,1,1,24]{3,2,1,0:T(1,128)}), s32[2,1,1,24]{3,2,1,0:T(1,128)S(1)}, s32[]{:S(2)}) async-start(s32[12,1,1,24]{3,2,1,0:T(1,128)} %param.14), calls=%async_computation.1 | async-start | bytes 2048 | tf_op jit(solution)/shard_map/slice | solution.py:42
  17.9 16.5 %copy-start.9 = (u32[32]{0:T(128)S(1)}, u32[32]{0:T(128)}, u32[]{:S(2)}) copy-start(u32[32]{0:T(128)} %constant.113) | copy-start | bytes 388
  18.0 17.7 %copy-start.8 = (s32[12,1,1,24]{3,2,1,0:T(1,128)S(1)}, s32[12,1,1,24]{3,2,1,0:T(1,128)}, u32[]{:S(2)}) copy-start(s32[12,1,1,24]{3,2,1,0:T(1,128)} %param.13) | copy-start | bytes 3460
  18.0 89.5 %copy-start.1 = (f32[768]{0:T(1024)S(1)}, f32[768]{0:T(1024)}, u32[]{:S(2)}) copy-start(f32[768]{0:T(1024)} %param.17) | copy-start | bytes 9220
  18.0 89.5 %copy-start.2 = (f32[768]{0:T(1024)S(1)}, f32[768]{0:T(1024)}, u32[]{:S(2)}) copy-start(f32[768]{0:T(1024)} %param.16) | copy-start | bytes 9220
  18.0 89.5 %copy-start.3 = (f32[768]{0:T(1024)S(1)}, f32[768]{0:T(1024)}, u32[]{:S(2)}) copy-start(f32[768]{0:T(1024)} %param.15) | copy-start | bytes 9220
  18.0 89.5 %copy-start.4 = (f32[768]{0:T(1024)S(1)}, f32[768]{0:T(1024)}, u32[]{:S(2)}) copy-start(f32[768]{0:T(1024)} %param.19) | copy-start | bytes 9220
  18.0 124.2 %copy-start.5 = (f32[768]{0:T(1024)S(1)}, f32[768]{0:T(1024)}, u32[]{:S(2)}) copy-start(f32[768]{0:T(1024)} %param.18) | copy-start | bytes 9220
  18.0 132.1 %slice-start.1 = ((f32[12,1,1,24]{3,2,1,0:T(1,128)}), f32[2,1,1,24]{3,2,1,0:T(1,128)S(1)}, s32[]{:S(2)}) async-start(f32[12,1,1,24]{3,2,1,0:T(1,128)} %param.12), calls=%async_computation.2 | async-start | bytes 2048 | tf_op jit(solution)/shard_map/slice | solution.py:46
  18.0 158.7 %slice-start.2 = ((f32[12,1,1,24]{3,2,1,0:T(1,128)}), f32[3,1,1,24]{3,2,1,0:T(1,128)S(1)}, s32[]{:S(2)}) async-start(f32[12,1,1,24]{3,2,1,0:T(1,128)} %param.12), calls=%async_computation.3 | async-start | bytes 3072 | tf_op jit(solution)/shard_map/slice | solution.py:46
  32.7 0.7 copy-start
  137.7 4.1 %collective-permute-start = (f32[16,128]{1,0:T(8,128)S(1)}, f32[16,128]{1,0:T(8,128)S(1)}, u32[]{:S(2)}, u32[]{:S(2)}) collective-permute-start(f32[16,128]{1,0:T(8,128)S(1)} %fusion), channel_id=1, source_target_pairs={{0,4},{4,8},{8,12},{12,16},{16,20},{20,24},{24,28},{1,5},{5,9},{9,... | collective-permute-start | bytes 24584
  139.1 2.6 %collective-permute-start.1 = (f32[12,128]{1,0:T(8,128)S(1)}, f32[12,128]{1,0:T(8,128)S(1)}, u32[]{:S(2)}, u32[]{:S(2)}) collective-permute-start(f32[12,128]{1,0:T(8,128)S(1)} %slice.143), channel_id=1, source_target_pairs={{0,8},{4,12},{8,16},{12,20},{16,24},{20,28},{1,9},{5,13},{9,17},{1... | collective-permute-start | bytes 18440
  173.5 4.5 %collective-permute-start.2 = (f32[16,128]{1,0:T(8,128)S(1)}, f32[16,128]{1,0:T(8,128)S(1)}, u32[]{:S(2)}, u32[]{:S(2)}) collective-permute-start(f32[16,128]{1,0:T(8,128)S(1)} %fusion.1), channel_id=1, source_target_pairs={{0,4},{4,8},{8,12},{12,16},{16,20},{20,24},{24,28},{1,5},{5,9},{9,... | collective-permute-start | bytes 24584
  175.4 2.6 %collective-permute-start.3 = (f32[12,128]{1,0:T(8,128)S(1)}, f32[12,128]{1,0:T(8,128)S(1)}, u32[]{:S(2)}, u32[]{:S(2)}) collective-permute-start(f32[12,128]{1,0:T(8,128)S(1)} %slice.144), channel_id=1, source_target_pairs={{0,8},{4,12},{8,16},{12,20},{16,24},{20,28},{1,9},{5,13},{9,17},{1... | collective-permute-start | bytes 18440
  210.4 4.3 %collective-permute-start.4 = (f32[16,128]{1,0:T(8,128)S(1)}, f32[16,128]{1,0:T(8,128)S(1)}, u32[]{:S(2)}, u32[]{:S(2)}) collective-permute-start(f32[16,128]{1,0:T(8,128)S(1)} %fusion.2), channel_id=1, source_target_pairs={{0,4},{4,8},{8,12},{12,16},{16,20},{20,24},{24,28},{1,5},{5,9},{9,... | collective-permute-start | bytes 24584
  212.0 2.6 %collective-permute-start.5 = (f32[12,128]{1,0:T(8,128)S(1)}, f32[12,128]{1,0:T(8,128)S(1)}, u32[]{:S(2)}, u32[]{:S(2)}) collective-permute-start(f32[12,128]{1,0:T(8,128)S(1)} %slice.145), channel_id=1, source_target_pairs={{0,8},{4,12},{8,16},{12,20},{16,24},{20,28},{1,9},{5,13},{9,17},{1... | collective-permute-start | bytes 18440
Sparse Core Ops, SparseCore 0:
  33.6 72.7 all-reduce.9
where the time goes:
time: 224 us; the launch traced here: 223 us
  blocking collectives  82.4 us (37%)
  waiting for transfers between devices  73.6 us (33%)
  local copies, waits for them, and re-layouts  17.3 us (8%)
  other arithmetic  17.2 us (8%)
  between operations  15.9 us (7%)
  starting transfers between devices  8.81 us (4%)
  matrix products  8.08 us (4%)
    unnamed x8, waiting for transfers between devices  73.6 us
    unnamed x3, blocking collectives  66.9 us
    all_gather x3, blocking collectives, per_device(): source_rates = lax.all_gather(rounded, 'rcv', axis=0, tiled=True)  15.5 us
    scatter-add x1, other arithmetic, per_device(): jax.ops.segment_sum(older.reshape(lag_count * slot_count, STEPS, 2 * bloc...  10.9 us
    unnamed x7, starting transfers between devices  8.81 us
    gather x1, local copies, waits for them, and re-layouts, per_device(): picked = hist_blocks[hist_rows[:, None, :], col_ids[:, :, None]]  7.09 us
  transfers between devices with their start and end apart: 7, of which 4 were waited for; matrix products, arithmetic and copies ran while one was open for 1% of the time, Pallas kernels for 0%

commit v1 on v0

v1 whole, which is shorter than its diff:
```python
import jax
import jax.numpy as jnp
from jax import lax
from jax.experimental import pallas as pl
from jax.experimental.pallas import tpu as pltpu
from jax.sharding import PartitionSpec as P

STEPS = 4
NEWTON_ITERS = 4
DAMPING = 1.0
LOADING = 0.05
TIME_STEP = 0.2
LANES = 128
SPLIT = 3


def inverse_sinh(value):
    magnitude = jnp.abs(value)
    result = jnp.log(magnitude + jnp.sqrt(1.0 + magnitude * magnitude))
    return jnp.where(value < 0.0, -result, result)


def friction_solve(stress, step_no, guess, state_now, shear_sigma, rate_a):
    axis = stress.ndim - 1
    half = LANES // 2
    shear_total = stress + shear_sigma + LOADING * (step_no + 1)
    strength = rate_a * (shear_sigma * (1.0 + 0.5 * jnp.tanh(stress)))
    strength = pltpu.roll(strength, half, axis)
    factor = 0.5 * jnp.exp(state_now)
    slip_rate = guess
    for attempt in range(NEWTON_ITERS):
        scaled = slip_rate * factor
        misfit = shear_total - DAMPING * slip_rate - strength * inverse_sinh(scaled)
        derivative = -DAMPING - strength * factor / jnp.sqrt(1.0 + scaled * scaled)
        slip_rate = slip_rate - misfit / derivative
    next_state = state_now + TIME_STEP * rate_a * jnp.tanh(
        jnp.exp(-state_now) - jnp.abs(slip_rate)
    )
    low = lax.broadcasted_iota(jnp.int32, stress.shape, axis) < half
    return jnp.where(low, slip_rate, 0.0), jnp.where(low, next_state, 0.0)


def older_kernel(
    panels, history, rows, cols, scales, send, rest, guess, panel_buf, sources, acc, sems,
    *, lags, slots, width, n_src, n_rcv, own_blocks,
):
    src_blocks = n_rcv * own_blocks
    recv_blocks = n_src * own_blocks
    per_tile = own_blocks // SPLIT
    pad_rows = 24

    def panel_copy(lag):
        return pltpu.make_async_copy(panels.at[lag], panel_buf.at[lag], sems.at[lag])

    for lag in range(lags):
        panel_copy(lag).start()
    tail = jnp.zeros((pad_rows - lags, LANES), jnp.float32)
    for pair in range(src_blocks // 2):
        tile = history[:, pair * LANES:(pair + 1) * LANES].astype(jnp.float32)
        sources[2 * pair * pad_rows:2 * pair * pad_rows + lags, :] = tile
        sources[2 * pair * pad_rows + lags:(2 * pair + 1) * pad_rows, :] = tail
        sources[(2 * pair + 1) * pad_rows:(2 * pair + 1) * pad_rows + lags, :] = pltpu.roll(tile, width, 1)
        sources[(2 * pair + 1) * pad_rows + lags:(2 * pair + 2) * pad_rows, :] = tail
    acc[...] = jnp.zeros_like(acc)

    def one_lag(lag, carry):
        panel_copy(lag).wait()
        for slot in range(slots):
            col = cols[lag, slot]
            picked = sources[pl.ds(col * pad_rows + (lags - 1) - lag, 8), :]
            picked = picked[:, :width].astype(jnp.bfloat16)
            term = jnp.dot(picked, panel_buf[lag, slot], preferred_element_type=jnp.float32)
            at = pl.ds(pl.multiple_of(rows[lag, slot] * 8, 8), 8)
            acc[at, :] = acc[at, :] + term * scales[lag, slot]
        return carry

    lax.fori_loop(0, lags, one_lag, 0)
    for dest in range(n_src):
        for tile in range(SPLIT):
            piece = acc[pl.ds((dest * own_blocks + tile) * 8, per_tile, stride=8 * SPLIT), :]
            for dup in range(n_rcv):
                send[dest * n_rcv + dup, :, tile * LANES:(tile + 1) * LANES] = piece
    for step in range(1, STEPS):
        rest[step - 1] = acc[pl.ds(step, recv_blocks, stride=8), :]
    for tile in range(SPLIT):
        guess[tile] = sources[pl.ds(tile * pad_rows + lags - 1, src_blocks // SPLIT, stride=pad_rows * SPLIT), :]


def step_kernel(
    recv, params, guess, state_in, rest, panels, rows, cols, scales,
    send, rest_out, slip_out, state_out, total, fields, sources, acc,
    *, step_no, lags_now, slots, width, n_src, n_rcv, own_blocks, dups, first,
):
    per_tile = own_blocks // SPLIT
    for tile in range(SPLIT):
        lanes = slice(tile * LANES, (tile + 1) * LANES)
        for owner in range(n_rcv):
            part = recv[owner, :, lanes]
            for src in range(1, n_src):
                part = part + recv[src * n_rcv + owner, :, lanes]
            at = slice(owner * per_tile, (owner + 1) * per_tile)
            total[tile, at, :] = part
            for kind in range(3):
                fields[kind, tile, at, :] = params[owner, kind, :, lanes]
    state_now = fields[2] if first else state_in[...]
    slip_rate, next_state = friction_solve(
        total[...], step_no, guess[...], state_now, fields[0], fields[1]
    )
    slip_out[...] = slip_rate
    state_out[...] = next_state
    for tile in range(SPLIT):
        sources[pl.ds(tile, n_rcv * per_tile, stride=SPLIT), :] = slip_rate[tile]
    acc[...] = rest[...]
    for lag in range(lags_now):
        for slot in range(slots):
            picked = sources[pl.ds(cols[lag, slot], 1), :]
            picked = jnp.broadcast_to(picked[:, :width], (8, width)).astype(jnp.bfloat16)
            term = jnp.dot(picked, panels[lag, slot], preferred_element_type=jnp.float32)
            at = pl.ds(rows[lag, slot], 1)
            acc[lag, at, :] = acc[lag, at, :] + term[:1] * scales[lag, slot]
    for dest in range(n_src):
        for tile in range(SPLIT):
            piece = acc[0, pl.ds(dest * own_blocks + tile, per_tile, stride=SPLIT), :]
            for dup in range(dups):
                send[dest * dups + dup, :, tile * LANES:(tile + 1) * LANES] = piece
    for later in range(1, lags_now):
        rest_out[later - 1] = acc[later]


def last_kernel(recv, params, guess, state_in, slip_out, state_out, *, step_no, n_src):
    for tile in range(SPLIT):
        lanes = slice(tile * LANES, (tile + 1) * LANES)
        part = recv[0, :, lanes]
        for src in range(1, n_src):
            part = part + recv[src, :, lanes]
        slip_rate, next_state = friction_solve(
            part, step_no, guess[tile], state_in[tile], params[0, :, lanes], params[1, :, lanes]
        )
        slip_out[tile] = slip_rate
        state_out[tile] = next_state


def per_device(
    history, kernel, scales, block_rows, block_cols,
    shear_pre, sigma_pre, friction_a, state_rate, state_init,
):
    lags = kernel.shape[0]
    slots = kernel.shape[3]
    width = kernel.shape[4]
    n_src = lax.axis_size("src")
    n_rcv = lax.axis_size("rcv")
    own_blocks = shear_pre.shape[0] // width
    src_blocks = n_rcv * own_blocks
    recv_blocks = n_src * own_blocks
    per_tile = own_blocks // SPLIT
    wide = SPLIT * LANES
    panels = kernel.reshape(lags, slots, width, 2 * width)
    weights = scales.reshape(lags, slots)
    row_ids = block_rows.reshape(lags, slots)
    col_ids = block_cols.reshape(lags, slots)
    sizes = dict(slots=slots, width=width, n_src=n_src, n_rcv=n_rcv, own_blocks=own_blocks)
    vmem = pl.BlockSpec(memory_space=pltpu.VMEM)
    smem = pl.BlockSpec(memory_space=pltpu.SMEM)
    f32 = jnp.float32

    def shape(*dims):
        return jax.ShapeDtypeStruct(dims, f32)

    def paired(low, high):
        both = jnp.stack([low.reshape(-1, width), high.reshape(-1, width)], axis=1)
        return both.reshape(per_tile, wide)

    own_params = jnp.stack(
        [paired(shear_pre, sigma_pre), paired(state_rate, friction_a), paired(state_init, state_init)]
    )
    params = lax.all_gather(own_params, "rcv", axis=0)

    send, rest, guess = pl.pallas_call(
        lambda *refs: older_kernel(*refs, lags=lags, **sizes),
        in_specs=[pl.BlockSpec(memory_space=pl.ANY), vmem, smem, smem, smem],
        out_specs=[vmem] * 3,
        out_shape=[
            shape(n_src * n_rcv, per_tile, wide),
            shape(STEPS - 1, recv_blocks, LANES),
            shape(SPLIT, src_blocks // SPLIT, LANES),
        ],
        scratch_shapes=[
            pltpu.VMEM((lags, slots, width, 2 * width), jnp.bfloat16),
            pltpu.VMEM((src_blocks * 24, LANES), f32),
            pltpu.VMEM((recv_blocks * 8, LANES), f32),
            pltpu.SemaphoreType.DMA((lags,)),
        ],
        compiler_params=pltpu.CompilerParams(vmem_limit_bytes=32 * 1024 * 1024),
        name="older",
    )(panels, history, row_ids, col_ids, weights)

    state = guess
    outputs = []
    recent = panels[:STEPS - 1]
    for step_no in range(STEPS - 1):
        recv = lax.all_to_all(send, ("src", "rcv"), 0, 0, tiled=True)
        lags_now = STEPS - 1 - step_no
        dups = n_rcv if lags_now > 1 else 1
        u_shape = shape(SPLIT, src_blocks // SPLIT, LANES)
        outs = pl.pallas_call(
            lambda *refs, step_no=step_no, lags_now=lags_now, dups=dups: step_kernel(
                *refs, step_no=step_no, lags_now=lags_now, dups=dups, first=step_no == 0, **sizes
            ),
            in_specs=[vmem] * 6 + [smem] * 3,
            out_specs=[vmem] * 4,
            out_shape=[
                shape(n_src * dups, per_tile, wide),
                shape(max(lags_now - 1, 1), recv_blocks, LANES),
                u_shape,
                u_shape,
            ],
            scratch_shapes=[
                pltpu.VMEM((SPLIT, src_blocks // SPLIT, LANES), f32),
                pltpu.VMEM((3, SPLIT, src_blocks // SPLIT, LANES), f32),
                pltpu.VMEM((src_blocks, LANES), f32),
                pltpu.VMEM((lags_now, recv_blocks, LANES), f32),
            ],
            compiler_params=pltpu.CompilerParams(vmem_limit_bytes=32 * 1024 * 1024),
            name="step",
        )(recv, params, guess, state, rest, recent, row_ids, col_ids, weights)
        send, rest, guess, state = outs
        outputs.append(guess)

    recv = lax.all_to_all(send, "src", 0, 0, tiled=True)
    mine = lax.axis_index("rcv") * per_tile

    def own(field):
        return lax.dynamic_slice_in_dim(field, mine, per_tile, 1)

    small = shape(SPLIT, per_tile, LANES)
    slip_rate, state = pl.pallas_call(
        lambda *refs: last_kernel(*refs, step_no=STEPS - 1, n_src=n_src),
        in_specs=[vmem] * 4,
        out_specs=[vmem] * 2,
        out_shape=[small, small],
        name="last",
    )(recv, own_params, own(guess), own(state))

    def flat(field):
        return jnp.swapaxes(field[:, :, :width], 0, 1).reshape(-1)

    rates = [flat(own(field)) for field in outputs] + [flat(slip_rate)]
    return (jnp.stack(rates), flat(state))


def solution(mesh):
    return jax.shard_map(
        per_device,
        mesh=mesh,
        in_specs=(
            P(None, "src"),
            P(None, "src", "rcv", None, None, None),
            P(None, "src", "rcv", None),
            P(None, "src", "rcv", None),
            P(None, "src", "rcv", None),
            P(("src", "rcv")),
            P(("src", "rcv")),
            P(("src", "rcv")),
            P(("src", "rcv")),
            P(("src", "rcv")),
        ),
        out_specs=(P(None, ("src", "rcv")), P(("src", "rcv"))),
        check_vma=False,
    )
```

time: 224 us -> 75.7 us (0.34)
  blocking collectives: 82.4 us -> 18.5 us
  waiting for transfers between devices: 73.6 us -> 16.2 us
  other arithmetic: 17.2 us -> 0.67 us
  between operations: 15.9 us -> 0.79 us
  Pallas kernels: 0 us -> 14.6 us
  matrix products: 8.08 us -> 0 us
  local copies, waits for them, and re-layouts: 17.3 us -> 10.9 us
  starting transfers between devices: 8.81 us -> 13.4 us
    unnamed x8 -> x0, waiting for transfers between devices: 73.6 us -> none
    unnamed x3 -> x0, blocking collectives: 66.9 us -> none
    all_to_all x0 -> x3, waiting for transfers between devices: none -> 16.2 us  [the longest x2 10.1 us: per_device(): recv = lax.all_to_all(send, ('src', 'rcv'), 0, 0, tiled=True)]
    pallas_call x0 -> x5, Pallas kernels: none -> 14.6 us  [the longest x1 6.99 us: per_device(): pl.pallas_call(lambda *refs: older_kernel(*refs, lags=lags, **sizes), in_...]
    all_to_all x0 -> x3, starting transfers between devices: none -> 13.4 us  [the longest x2 10 us: per_device(): recv = lax.all_to_all(send, ('src', 'rcv'), 0, 0, tiled=True)]
    scatter-add x4 -> x0, other arithmetic: 13.2 us -> none  [the longest x1 10.9 us: per_device(): jax.ops.segment_sum(older.reshape(lag_count * slot_count, STEPS, 2 * bloc...]
    all_to_all x0 -> x1, blocking collectives: none -> 13.2 us  [per_device(): recv = lax.all_to_all(send, ('src', 'rcv'), 0, 0, tiled=True)]
    gather x4 -> x0, local copies, waits for them, and re-layouts: 10.4 us -> none  [the longest x1 7.09 us: per_device(): picked = hist_blocks[hist_rows[:, None, :], col_ids[:, :, None]]]
  transfers between devices with their start and end apart: 7 -> 3, of which waited for: 4 -> 3; matrix products, arithmetic and copies ran while one was open for 1% -> 4% of each run, Pallas kernels for 0% -> 0%
where the time goes in v1:
time: 75.7 us; the launch traced here: 75 us
  blocking collectives  18.5 us (24%)
  waiting for transfers between devices  16.2 us (21%)
  Pallas kernels  14.6 us (19%)
  starting transfers between devices  13.4 us (18%)
  local copies, waits for them, and re-layouts  10.9 us (14%)
  between operations  0.79 us (1%)
    all_to_all x1, blocking collectives, per_device(): recv = lax.all_to_all(send, ('src', 'rcv'), 0, 0, tiled=True)  13.2 us
    all_to_all x2, waiting for transfers between devices, per_device(): recv = lax.all_to_all(send, ('src', 'rcv'), 0, 0, tiled=True)  10.1 us
    all_to_all x2, starting transfers between devices, per_device(): recv = lax.all_to_all(send, ('src', 'rcv'), 0, 0, tiled=True)  10 us
    pallas_call x1, Pallas kernels, per_device(): pl.pallas_call(lambda *refs: older_kernel(*refs, lags=lags, **sizes), in_...  6.99 us
    all_to_all x1, waiting for transfers between devices, per_device(): recv = lax.all_to_all(send, 'src', 0, 0, tiled=True)  6.06 us
    pallas_call x3, Pallas kernels, per_device(): pl.pallas_call(lambda *refs, step_no=step_no, lags_now=lags_now, dups=dup...  5.95 us
    all_gather x1, blocking collectives, per_device(): params = lax.all_gather(own_params, 'rcv', axis=0)  5.32 us
    unnamed x22, local copies, waits for them, and re-layouts  5.31 us
  transfers between devices with their start and end apart: 3, of which 3 were waited for; matrix products, arithmetic and copies ran while one was open for 4% of the time, Pallas kernels for 0%

profile of v1, /device:TPU:0, one launch (start us, length us, event | category | flops | bytes accessed | tf_op | source)
XLA Modules:
  0.0 75.0 jit_solution(6152511682141697829)
XLA Ops:
  0.7 0.7 copy.31
  1.4 0.7 copy_bitcast_fusion.1
  2.1 2.3 %copy-done = bf16[12,1,1,24,64,128]{5,4,3,2,1,0:T(8,128)(2,1)S(1)} copy-done((bf16[12,1,1,24,64,128]{5,4,3,2,1,0:T(8,128)(2,1)S(1)}, bf16[12,1,1,24,64,128]{5,4,3,2,1,0:T(8,128)(2,1)}, u32[]{:S(2)}) %copy-start) | copy-done | bytes 4718616
  4.5 0.9 %copy-done.1 = bf16[12,3072]{1,0:T(8,128)(2,1)S(1)} copy-done((bf16[12,3072]{1,0:T(8,128)(2,1)S(1)}, bf16[12,3072]{1,0:T(8,128)(2,1)}, u32[]{:S(2)}) %copy-start.1) | copy-done | bytes 73752
  5.3 7.0 %older.1 = (f32[32,4,384]{2,1,0:T(4,128)}, f32[3,96,128]{2,1,0:T(8,128)S(1)}, f32[3,16,128]{2,1,0:T(8,128)S(1)}) custom-call(bf16[12,24,64,128]{3,2,1,0:T(8,128)(2,1)S(1)} %bitcast.23, bf16[12,3072]{1,0:T(8,128)(2,1)S(1)} %copy-done.1, s32[12,24]{1,0:T(8,128)S(1)} %get-tuple-element.35.refs_2_.refs_6_, s32[12,24]{1,0:T(8,128)S(1)} %get-tuple-element.34.refs_3_.refs_7_, ...), custom_call_target="tpu_custom_call" | custom-call | tf_op jit(solution)/shard_map/older/pallas_call | solution.py:178
  12.3 7.3 %all-to-all-start = ((f32[32,4,384]{2,1,0:T(4,128)}), f32[32,4,384]{2,1,0:T(4,128)S(1)}, u32[]{:S(2)}, u32[]{:S(2)}) async-start(f32[32,4,384]{2,1,0:T(4,128)} %get-tuple-element.18), calls=%async_computation | async-start | bytes 393216 | tf_op jit(solution)/shard_map/all_to_all | solution.py:201
  19.9 0.1 stack_reshape.39
  20.1 0.1 stack_reshape.42
  20.3 0.1 stack_reshape.44
  20.4 5.3 %all-gather = f32[12,4,384]{2,1,0:T(4,128)S(1)} all-gather(f32[3,4,384]{2,1,0:T(4,128)S(1)} %constant_dynamic-update-slice_fusion.refs_1_), channel_id=2, replica_groups=mesh['src'=8,'rcv'=4] {'rcv'}, dimensions={0}, use_global_device_ids=true | all-gather | bytes 92160 | tf_op jit(solution)/shard_map/all_gather | solution.py:176
  25.7 1.4 %slice_bitcast_fusion.refs_5_ = bf16[3,24,64,128]{3,2,1,0:T(8,128)(2,1)S(1)} fusion(bf16[12,1,1,24,64,128]{5,4,3,0,2,1:T(8,128)(2,1)} %bitcast.22), kind=kLoop, calls=%fused_computation | loop fusion | bytes 2359296 | tf_op jit(solution)/shard_map/slice | solution.py:199
  27.1 1.4 %all-to-all-done.refs_0_ = f32[32,4,384]{2,1,0:T(4,128)S(1)} async-done(((f32[32,4,384]{2,1,0:T(4,128)}), f32[32,4,384]{2,1,0:T(4,128)S(1)}, u32[]{:S(2)}, u32[]{:S(2)}) %all-to-all-start) | async-done | bytes 196640 | tf_op jit(solution)/shard_map/all_to_all | solution.py:201
  28.5 1.7 %step.3 = (f32[32,4,384]{2,1,0:T(4,128)S(1)}, f32[2,96,128]{2,1,0:T(8,128)S(1)}, f32[3,16,128]{2,1,0:T(8,128)S(1)}, f32[3,16,128]{2,1,0:T(8,128)S(1)}) custom-call(f32[32,4,384]{2,1,0:T(4,128)S(1)} %all-to-all-done.refs_0_, f32[4,3,4,384]{3,2,1,0:T(4,128)S(1)} %bitcast.24, f32[3,16,128]{2,1,0:T(8,128)S(1)} %get-tuple-element.19.refs_2_.refs_3_, ...), custom_call_target="tpu_custom_call" | custom-call | tf_op jit(solution)/shard_map/step/pallas_call | solution.py:205
  30.2 13.2 %all_to_all.20.refs_0_ = f32[32,4,384]{2,1,0:T(4,128)S(1)} all-to-all(f32[32,4,384]{2,1,0:T(4,128)S(1)} %get-tuple-element.22), channel_id=1, replica_groups=mesh['src'=8,'rcv'=4] {'src','rcv'}, dimensions={0} | all-to-all | bytes 393216 | tf_op jit(solution)/shard_map/all_to_all | solution.py:201
  43.4 2.2 %step.4 = (f32[32,4,384]{2,1,0:T(4,128)}, f32[1,96,128]{2,1,0:T(8,128)S(1)}, f32[3,16,128]{2,1,0:T(8,128)S(1)}, f32[3,16,128]{2,1,0:T(8,128)S(1)}) custom-call(f32[32,4,384]{2,1,0:T(4,128)S(1)} %all_to_all.20.refs_0_, f32[4,3,4,384]{3,2,1,0:T(4,128)S(1)} %bitcast.25, f32[3,16,128]{2,1,0:T(8,128)S(1)} %get-tuple-element.21.refs_2_, ...), custom_call_target="tpu_custom_call" | custom-call | tf_op jit(solution)/shard_map/step/pallas_call | solution.py:205
  45.7 2.7 %all-to-all-start.2 = ((f32[32,4,384]{2,1,0:T(4,128)}), f32[32,4,384]{2,1,0:T(4,128)S(1)}, u32[]{:S(2)}, u32[]{:S(2)}) async-start(f32[32,4,384]{2,1,0:T(4,128)} %get-tuple-element.26), calls=%async_computation.2 | async-start | bytes 393216 | tf_op jit(solution)/shard_map/all_to_all | solution.py:201
  48.4 0.1 stack_reshape.45
  48.5 0.1 stack_reshape.46
  48.6 8.7 %all-to-all-done.2.refs_0_ = f32[32,4,384]{2,1,0:T(4,128)S(1)} async-done(((f32[32,4,384]{2,1,0:T(4,128)}), f32[32,4,384]{2,1,0:T(4,128)S(1)}, u32[]{:S(2)}, u32[]{:S(2)}) %all-to-all-start.2) | async-done | bytes 196640 | tf_op jit(solution)/shard_map/all_to_all | solution.py:201
  57.3 2.0 %step.5 = (f32[8,4,384]{2,1,0:T(4,128)}, f32[1,96,128]{2,1,0:T(8,128)}, f32[3,16,128]{2,1,0:T(8,128)S(1)}, f32[3,16,128]{2,1,0:T(8,128)S(1)}) custom-call(f32[32,4,384]{2,1,0:T(4,128)S(1)} %all-to-all-done.2.refs_0_, f32[4,3,4,384]{3,2,1,0:T(4,128)S(1)} %bitcast.26, f32[3,16,128]{2,1,0:T(8,128)S(1)} %get-tuple-element.25.refs_2_, ...), custom_call_target="tpu_custom_call" | custom-call | tf_op jit(solution)/shard_map/step/pallas_call | solution.py:205
  59.3 0.6 constant_dynamic-slice_fusion.1.refs_2_
  59.9 3.3 %all-to-all-start.3 = ((f32[8,4,384]{2,1,0:T(4,128)}), f32[8,4,384]{2,1,0:T(4,128)S(1)}, u32[]{:S(2)}, u32[]{:S(2)}) async-start(f32[8,4,384]{2,1,0:T(4,128)} %get-tuple-element.30), calls=%async_computation.3 | async-start | bytes 98304 | tf_op jit(solution)/shard_map/all_to_all | solution.py:229
  63.3 0.1 stack_reshape.47
  63.4 0.6 constant_dynamic-slice_fusion.refs_3_
  63.9 6.1 %all-to-all-done.3.refs_0_ = f32[8,4,384]{2,1,0:T(4,128)S(1)} async-done(((f32[8,4,384]{2,1,0:T(4,128)}), f32[8,4,384]{2,1,0:T(4,128)S(1)}, u32[]{:S(2)}, u32[]{:S(2)}) %all-to-all-start.3) | async-done | bytes 49184 | tf_op jit(solution)/shard_map/all_to_all | solution.py:229
  70.0 0.6 copy-done.2
  70.6 1.6 %last.1 = (f32[3,4,128]{2,1,0:T(4,128)}, f32[3,4,128]{2,1,0:T(4,128)}) custom-call(f32[8,4,384]{2,1,0:T(4,128)} %copy-done.2, f32[3,4,384]{2,1,0:T(4,128)} %copy-done.3, f32[3,4,128]{2,1,0:T(4,128)} %constant_dynamic-slice_fusion.1.refs_2_, f32[3,4,128]{2,1,0:T(4,128)} %constant_dynamic-slice_fusion.refs_3_), custom_call_target="tpu_custom_call" | custom-call | tf_op jit(solution)/shard_map/last/pallas_call | solution.py:236
  72.2 0.7 slice_bitcast_fusion.2
  72.9 0.1 stack_reshape.48
  73.0 0.7 slice_bitcast_fusion.1
  73.7 0.7 reshape.24
  74.4 0.6 pad_maximum_fusion.3
  (34 shorter events, 0.5 us)
Async XLA Ops:
  0.6 19.0 %copy-start.4 = (f32[768]{0:T(1024)S(1)}, f32[768]{0:T(1024)}, u32[]{:S(2)}) copy-start(f32[768]{0:T(1024)} %param.15) | copy-start | bytes 9220
  0.6 19.1 %copy-start.5 = (f32[768]{0:T(1024)S(1)}, f32[768]{0:T(1024)}, u32[]{:S(2)}) copy-start(f32[768]{0:T(1024)} %param.16) | copy-start | bytes 9220
  0.7 19.3 %copy-start.6 = (f32[768]{0:T(1024)S(1)}, f32[768]{0:T(1024)}, u32[]{:S(2)}) copy-start(f32[768]{0:T(1024)} %param.18) | copy-start | bytes 9220
  0.7 19.4 %copy-start.7 = (f32[768]{0:T(1024)S(1)}, f32[768]{0:T(1024)}, u32[]{:S(2)}) copy-start(f32[768]{0:T(1024)} %param.17) | copy-start | bytes 9220
  0.7 19.5 %copy-start.8 = (f32[768]{0:T(1024)S(1)}, f32[768]{0:T(1024)}, u32[]{:S(2)}) copy-start(f32[768]{0:T(1024)} %param.19) | copy-start | bytes 9220
  2.1 2.3 %copy-start = (bf16[12,1,1,24,64,128]{5,4,3,2,1,0:T(8,128)(2,1)S(1)}, bf16[12,1,1,24,64,128]{5,4,3,2,1,0:T(8,128)(2,1)}, u32[]{:S(2)}) copy-start(bf16[12,1,1,24,64,128]{5,4,3,2,1,0:T(8,128)(2,1)} %param.11) | copy-start | bytes 14155780
  4.5 0.9 %copy-start.1 = (bf16[12,3072]{1,0:T(8,128)(2,1)S(1)}, bf16[12,3072]{1,0:T(8,128)(2,1)}, u32[]{:S(2)}) copy-start(bf16[12,3072]{1,0:T(8,128)(2,1)} %refs_1_.1) | copy-start | bytes 221188
  12.3 16.2 %all-to-all-start = ((f32[32,4,384]{2,1,0:T(4,128)}), f32[32,4,384]{2,1,0:T(4,128)S(1)}, u32[]{:S(2)}, u32[]{:S(2)}) async-start(f32[32,4,384]{2,1,0:T(4,128)} %get-tuple-element.18), calls=%async_computation | async-start | bytes 393216 | tf_op jit(solution)/shard_map/all_to_all | solution.py:201
  20.4 49.6 %copy-start.3 = (f32[3,4,384]{2,1,0:T(4,128)}, f32[3,4,384]{2,1,0:T(4,128)S(1)}, u32[]{:S(2)}) copy-start(f32[3,4,384]{2,1,0:T(4,128)S(1)} %constant_dynamic-update-slice_fusion.refs_1_) | copy-start | bytes 55300
  45.7 11.6 %all-to-all-start.2 = ((f32[32,4,384]{2,1,0:T(4,128)}), f32[32,4,384]{2,1,0:T(4,128)S(1)}, u32[]{:S(2)}, u32[]{:S(2)}) async-start(f32[32,4,384]{2,1,0:T(4,128)} %get-tuple-element.26), calls=%async_computation.2 | async-start | bytes 393216 | tf_op jit(solution)/shard_map/all_to_all | solution.py:201
  59.9 10.1 %all-to-all-start.3 = ((f32[8,4,384]{2,1,0:T(4,128)}), f32[8,4,384]{2,1,0:T(4,128)S(1)}, u32[]{:S(2)}, u32[]{:S(2)}) async-start(f32[8,4,384]{2,1,0:T(4,128)} %get-tuple-element.30), calls=%async_computation.3 | async-start | bytes 98304 | tf_op jit(solution)/shard_map/all_to_all | solution.py:229
  70.0 0.6 copy-start.2

commit v2 on v0

v2 whole, which is shorter than its diff:
```python
import functools

import jax
import jax.numpy as jnp
from jax import lax
from jax.experimental import pallas as pl
from jax.experimental.pallas import tpu as pltpu
from jax.sharding import PartitionSpec as P

STEPS = 4
NEWTON_ITERS = 4
DAMPING = 1.0
LOADING = 0.05
TIME_STEP = 0.2
LANES = 128
HALF = LANES // 2
ROWS = 4
IN_FLIGHT = 3
TAPS = 24
VMEM_LIMIT = 16 * 1024 * 1024


def inverse_sinh(value):
    magnitude = jnp.abs(value)
    result = jnp.log(magnitude + jnp.sqrt(1.0 + magnitude * magnitude))
    return jnp.where(value < 0.0, -result, result)


def friction_solve(shear, normal_stress, step_no, guess, state_now, fields):
    shear_pre, sigma_pre, friction_a, state_rate = fields
    shear_total = shear + shear_pre + LOADING * (step_no + 1)
    normal = sigma_pre * (1.0 + 0.5 * jnp.tanh(normal_stress))
    strength = friction_a * normal
    factor = 0.5 * jnp.exp(state_now)
    slip_rate = guess
    for attempt in range(NEWTON_ITERS):
        scaled = slip_rate * factor
        misfit = shear_total - DAMPING * slip_rate - strength * inverse_sinh(scaled)
        derivative = -DAMPING - strength * factor / jnp.sqrt(1.0 + scaled * scaled)
        slip_rate = slip_rate - misfit / derivative
    next_state = state_now + TIME_STEP * state_rate * jnp.tanh(
        jnp.exp(-state_now) - jnp.abs(slip_rate)
    )
    return slip_rate, next_state


def split_stress(even, odd):
    low = lax.broadcasted_iota(jnp.int32, even.shape, 1) < HALF
    shear = jnp.where(low, even, pltpu.roll(odd, HALF, 1))
    normal = jnp.where(low, pltpu.roll(even, HALF, 1), odd)
    return shear, normal


def pack_messages(send, acc, own_blocks, n_dest, dups, stride):
    for dest in range(n_dest):
        for tile in range(own_blocks // ROWS):
            first = (dest * own_blocks + tile * ROWS) * stride
            rows = pl.ds(first, ROWS, stride=stride) if stride > 1 else pl.ds(first, ROWS)
            piece = acc[rows, :]
            for dup in range(dups):
                send[dest * dups + dup, :, tile * LANES:(tile + 1) * LANES] = piece


def sum_messages(recv, total, own_blocks, n_src, owners):
    for owner in range(owners):
        part = recv[owner]
        for src in range(1, n_src):
            part = part + recv[src * owners + owner]
        for tile in range(own_blocks // ROWS):
            first = owner * own_blocks + tile * ROWS
            total[first:first + ROWS, :] = part[:, tile * LANES:(tile + 1) * LANES]
    pairs = owners * own_blocks // 2
    return total[pl.ds(0, pairs, stride=2), :], total[pl.ds(1, pairs, stride=2), :]


def older_kernel(
    panels, history, rows_in, cols_in, scales_in, send, rest, guess, recent,
    panel_buf, history_buf, rows, cols, scales, sources, acc, sems, small_sems, out_sem,
    *, lags, slots, n_src, n_rcv, own_blocks,
):
    src_blocks = n_rcv * own_blocks
    recv_blocks = n_src * own_blocks
    smalls = [
        pltpu.make_async_copy(source, target, small_sems.at[at])
        for at, (source, target) in enumerate(
            [(history, history_buf), (cols_in, cols), (rows_in, rows), (scales_in, scales)]
        )
    ]

    def panel_copy(lag):
        return pltpu.make_async_copy(panels.at[lag], panel_buf.at[lag], sems.at[lag])

    for copy in smalls:
        copy.start()
    for lag in range(IN_FLIGHT):
        panel_copy(lag).start()
    acc[...] = jnp.zeros_like(acc)
    tail = jnp.zeros((TAPS - lags, LANES), jnp.float32)
    smalls[0].wait()
    for pair in range(src_blocks // 2):
        tile = history_buf[:, pair * LANES:(pair + 1) * LANES].astype(jnp.float32)
        for half in range(2):
            base = (2 * pair + half) * TAPS
            sources[base:base + lags, :] = tile if half == 0 else pltpu.roll(tile, HALF, 1)
            sources[base + lags:base + TAPS, :] = tail
    for copy in smalls[1:]:
        copy.wait()

    def one_lag(lag, carry):
        panel_copy(lag).wait()

        @pl.when(lag + IN_FLIGHT < lags)
        def _():
            panel_copy(lag + IN_FLIGHT).start()

        for slot in range(slots):
            col = cols[lag, 0, 0, slot]
            picked = sources[pl.ds(col * TAPS + (lags - 1) - lag, 8), :]
            picked = picked[:, :HALF].astype(jnp.bfloat16)
            term = jnp.dot(picked, panel_buf[lag, slot], preferred_element_type=jnp.float32)
            at = pl.ds(pl.multiple_of(rows[lag, 0, 0, slot] * 8, 8), 8)
            acc[at, :] = acc[at, :] + term * scales[lag, 0, 0, slot]
        return carry

    lax.fori_loop(0, lags, one_lag, 0)
    handed_on = pltpu.make_async_copy(panel_buf.at[pl.ds(0, STEPS - 1)], recent, out_sem)
    handed_on.start()
    pack_messages(send, acc, own_blocks, n_src, n_rcv, 8)
    for step in range(1, STEPS):
        rest[step - 1] = acc[pl.ds(step, recv_blocks, stride=8), :]
    guess[...] = sources[pl.ds(lags - 1, src_blocks // 2, stride=2 * TAPS), :]
    handed_on.wait()


def small_copies(sources, targets, sems):
    return [
        pltpu.make_async_copy(source, target, sems.at[at])
        for at, (source, target) in enumerate(zip(sources, targets))
    ]


def spread_sources(slip_rate, sources):
    pairs = slip_rate.shape[0]
    sources[pl.ds(0, pairs, stride=2), :] = slip_rate
    sources[pl.ds(1, pairs, stride=2), :] = pltpu.roll(slip_rate, HALF, 1)


def add_terms(acc_at, lag, panels, sources, rows, cols, scales, slots):
    for slot in range(slots):
        picked = sources[pl.ds(cols[lag, 0, 0, slot], 1), :]
        picked = jnp.broadcast_to(picked[:, :HALF], (8, HALF)).astype(jnp.bfloat16)
        term = jnp.dot(picked, panels[lag, slot], preferred_element_type=jnp.float32)
        at = pl.ds(rows[lag, 0, 0, slot], 1)
        acc_at[at, :] = acc_at[at, :] + term[:1] * scales[lag, 0, 0, slot]


def step_kernel(
    recv, fields, guess, state_in, rest, panels, rows_in, cols_in, scales_in,
    send, slip_out, state_out,
    rows, cols, scales, total, sources, acc, sems,
    *, step_no, rest_at, slots, n_src, n_rcv, own_blocks, dups,
):
    copies = small_copies((cols_in, rows_in, scales_in), (cols, rows, scales), sems)
    for copy in copies:
        copy.start()
    shear, normal = split_stress(*sum_messages(recv, total, own_blocks, n_src, n_rcv))
    slip_rate, next_state = friction_solve(
        shear, normal, step_no, guess[...], state_in[...], [fields[kind] for kind in range(4)]
    )
    slip_out[...] = slip_rate
    state_out[...] = next_state
    spread_sources(slip_rate, sources)
    acc[...] = rest[rest_at]
    for copy in copies:
        copy.wait()
    add_terms(acc, 0, panels, sources, rows, cols, scales, slots)
    pack_messages(send, acc, own_blocks, n_src, dups, 1)


def later_kernel(
    slip_rate, rest, panels, rows_in, cols_in, scales_in, rest_out,
    rows, cols, scales, sources, sems, *, later, slots,
):
    copies = small_copies((cols_in, rows_in, scales_in), (cols, rows, scales), sems)
    for copy in copies:
        copy.start()
    spread_sources(slip_rate[...], sources)
    for at in range(later):
        rest_out[at] = rest[at + 1]
    for copy in copies:
        copy.wait()
    for at in range(later):
        add_terms(rest_out.at[at], at + 1, panels, sources, rows, cols, scales, slots)


def last_kernel(
    recv, shear_pre, sigma_pre, friction_a, state_rate, state_in, *refs, step_no, n_src,
):
    slips, (slip_out, state_out, total) = refs[:step_no], refs[step_no:]
    pairs = slip_out.shape[1] // LANES
    mine = pl.ds(lax.axis_index("rcv") * pairs, pairs)
    shear, normal = split_stress(*sum_messages(recv, total, 2 * pairs, n_src, 1))
    fields = [ref[...] for ref in (shear_pre, sigma_pre, friction_a, state_rate)]
    slip_rate, next_state = friction_solve(
        shear, normal, step_no, slips[-1][mine, :], state_in[mine, :], fields
    )
    for step, field in enumerate([ref[mine, :] for ref in slips] + [slip_rate]):
        for row in range(pairs):
            slip_out[step:step + 1, row * LANES:(row + 1) * LANES] = field[row:row + 1]
    state_out[...] = next_state


def per_device(
    history, kernel, scales, block_rows, block_cols,
    shear_pre, sigma_pre, friction_a, state_rate, state_init,
):
    lags = kernel.shape[0]
    slots = kernel.shape[3]
    width = kernel.shape[4]
    n_src = lax.axis_size("src")
    n_rcv = lax.axis_size("rcv")
    own = shear_pre.shape[0]
    own_blocks = own // width
    pairs = own // LANES
    src_blocks = n_rcv * own_blocks
    recv_rows = n_src * own_blocks
    message = (ROWS, own_blocks // ROWS * LANES)
    panels = kernel.reshape(lags, slots, width, 2 * width)
    f32 = jnp.float32
    hbm = pl.BlockSpec(memory_space=pltpu.HBM)
    vmem = pl.BlockSpec(memory_space=pltpu.VMEM)
    sizes = dict(slots=slots, n_src=n_src, n_rcv=n_rcv, own_blocks=own_blocks)
    index_bufs = [
        pltpu.SMEM(block_rows.shape, jnp.int32),
        pltpu.SMEM(block_cols.shape, jnp.int32),
        pltpu.SMEM(scales.shape, f32),
    ]

    def shape(*dims, dtype=f32):
        return jax.ShapeDtypeStruct(dims, dtype)

    def call(body, ins, outs, scratch, name, args, flops, limit=VMEM_LIMIT):
        return pl.pallas_call(
            body, in_specs=ins, out_specs=[vmem] * len(outs), out_shape=outs, scratch_shapes=scratch,
            compiler_params=pltpu.CompilerParams(vmem_limit_bytes=limit), name=name,
            cost_estimate=pl.CostEstimate(flops=flops, bytes_accessed=flops // 64, transcendentals=0),
        )(*args)

    own_fields = [
        field.reshape(pairs, LANES)
        for field in (shear_pre, sigma_pre, friction_a, state_rate, state_init)
    ]
    fields = lax.all_gather(jnp.stack(own_fields), "rcv", axis=1, tiled=True)

    panels, history, *table = [
        pltpu.with_memory_space_constraint(array, pltpu.HBM)
        for array in (panels, history, block_rows, block_cols, scales)
    ]
    one_lag = 2 * slots * width * 2 * width * 8
    send, rest, guess, recent = call(
        functools.partial(older_kernel, lags=lags, **sizes),
        [hbm] * 5,
        [
            shape(n_src * n_rcv, *message),
            shape(STEPS - 1, recv_rows, LANES),
            shape(src_blocks // 2, LANES),
            shape(STEPS - 1, slots, width, 2 * width, dtype=panels.dtype),
        ],
        [
            pltpu.VMEM(panels.shape, panels.dtype),
            pltpu.VMEM(history.shape, history.dtype),
            *index_bufs,
            pltpu.VMEM((src_blocks * TAPS, LANES), f32),
            pltpu.VMEM((recv_rows * 8, LANES), f32),
            pltpu.SemaphoreType.DMA((lags,)),
            pltpu.SemaphoreType.DMA((4,)),
            pltpu.SemaphoreType.DMA,
        ],
        "older", [panels, history, *table], 60 * one_lag, limit=32 * 1024 * 1024,
    )

    state = fields[4]
    slips = []
    for step_no in range(STEPS - 1):
        recv = lax.all_to_all(send, ("src", "rcv"), 0, 0, tiled=True) if step_no == 0 else recv
        last = step_no == STEPS - 2
        dups = 1 if last else n_rcv
        send, slip_rate, state = call(
            functools.partial(step_kernel, step_no=step_no, rest_at=0, dups=dups, **sizes),
            [vmem] * 6 + [hbm] * 3,
            [
                shape(n_src * dups, *message),
                shape(src_blocks // 2, LANES),
                shape(src_blocks // 2, LANES),
            ],
            index_bufs + [
                pltpu.VMEM((src_blocks, LANES), f32),
                pltpu.VMEM((src_blocks, LANES), f32),
                pltpu.VMEM((recv_rows, LANES), f32),
                pltpu.SemaphoreType.DMA((3,)),
            ],
            "step", [recv, fields, guess, state, rest, recent, *table], one_lag,
        )
        guess = slip_rate
        slips.append(slip_rate)
        recv = lax.all_to_all(send, "src" if last else ("src", "rcv"), 0, 0, tiled=True)
        later = STEPS - 2 - step_no
        if later:
            rest, = call(
                functools.partial(later_kernel, later=later, slots=slots),
                [vmem] * 3 + [hbm] * 3,
                [shape(later, recv_rows, LANES)],
                index_bufs + [
                    pltpu.VMEM((src_blocks, LANES), f32),
                    pltpu.SemaphoreType.DMA((3,)),
                ],
                "later", [slip_rate, rest, recent, *table], later * one_lag,
            )

    slip_rates, state = call(
        functools.partial(last_kernel, step_no=STEPS - 1, n_src=n_src),
        [vmem] * (6 + len(slips)),
        [shape(STEPS, own), shape(pairs, LANES)],
        [pltpu.VMEM((own_blocks, LANES), f32)],
        "last", [recv, *own_fields[:4], state, *slips], 10 ** 6,
    )
    return (slip_rates, state.reshape(own))


def solution(mesh):
    return jax.shard_map(
        per_device,
        mesh=mesh,
        in_specs=(
            P(None, "src"),
            P(None, "src", "rcv", None, None, None),
            P(None, "src", "rcv", None),
            P(None, "src", "rcv", None),
            P(None, "src", "rcv", None),
            P(("src", "rcv")),
            P(("src", "rcv")),
            P(("src", "rcv")),
            P(("src", "rcv")),
            P(("src", "rcv")),
        ),
        out_specs=(P(None, ("src", "rcv")), P(("src", "rcv"))),
        check_vma=False,
    )
```

time: 224 us -> 62.9 us (0.28)
  blocking collectives: 82.4 us -> 15.6 us
  waiting for transfers between devices: 73.6 us -> 18.1 us
  other arithmetic: 17.2 us -> 0 us
  local copies, waits for them, and re-layouts: 17.3 us -> 0.13 us
  between operations: 15.9 us -> 0.81 us
  Pallas kernels: 0 us -> 14.6 us
  matrix products: 8.08 us -> 0 us
  starting transfers between devices: 8.81 us -> 12.7 us
    unnamed x8 -> x0, waiting for transfers between devices: 73.6 us -> none
    unnamed x3 -> x0, blocking collectives: 66.9 us -> none
    all_to_all x0 -> x3, waiting for transfers between devices: none -> 18.1 us  [the longest x2 15.2 us: per_device(): lax.all_to_all(send, 'src' if last else ('src', 'rcv'), 0, 0, tiled=True)]
    pallas_call x0 -> x7, Pallas kernels: none -> 14.6 us  [call(): pl.pallas_call(body, in_specs=ins, out_specs=[vmem] * len(outs), out_shap...]
    scatter-add x4 -> x0, other arithmetic: 13.2 us -> none  [the longest x1 10.9 us: per_device(): jax.ops.segment_sum(older.reshape(lag_count * slot_count, STEPS, 2 * bloc...]
    all_to_all x0 -> x3, starting transfers between devices: none -> 12.7 us  [the longest x1 7.3 us: per_device(): lax.all_to_all(send, ('src', 'rcv'), 0, 0, tiled=True)]
    gather x4 -> x0, local copies, waits for them, and re-layouts: 10.4 us -> none  [the longest x1 7.09 us: per_device(): picked = hist_blocks[hist_rows[:, None, :], col_ids[:, :, None]]]
    all_to_all x0 -> x1, blocking collectives: none -> 9.88 us  [per_device(): lax.all_to_all(send, 'src' if last else ('src', 'rcv'), 0, 0, tiled=True)]
  transfers between devices with their start and end apart: 7 -> 3, of which waited for: 4 -> 3; matrix products, arithmetic and copies ran while one was open for 1% -> 0% of each run, Pallas kernels for 0% -> 4%
where the time goes in v2:
time: 62.9 us; the launch traced here: 62.1 us
  waiting for transfers between devices  18.1 us (29%)
  blocking collectives  15.6 us (25%)
  Pallas kernels  14.6 us (23%)
  starting transfers between devices  12.7 us (20%)
  between operations  0.81 us (1%)
    all_to_all x2, waiting for transfers between devices, per_device(): lax.all_to_all(send, 'src' if last else ('src', 'rcv'), 0, 0, tiled=True)  15.2 us
    pallas_call x7, Pallas kernels, call(): pl.pallas_call(body, in_specs=ins, out_specs=[vmem] * len(outs), out_shap...  14.6 us
    all_to_all x1, blocking collectives, per_device(): lax.all_to_all(send, 'src' if last else ('src', 'rcv'), 0, 0, tiled=True)  9.88 us
    all_to_all x1, starting transfers between devices, per_device(): lax.all_to_all(send, ('src', 'rcv'), 0, 0, tiled=True)  7.3 us
    all_gather x1, blocking collectives, per_device(): fields = lax.all_gather(jnp.stack(own_fields), 'rcv', axis=1, tiled=True)  5.75 us
    all_to_all x2, starting transfers between devices, per_device(): lax.all_to_all(send, 'src' if last else ('src', 'rcv'), 0, 0, tiled=True)  5.44 us
    all_to_all x1, waiting for transfers between devices, per_device(): lax.all_to_all(send, ('src', 'rcv'), 0, 0, tiled=True)  2.95 us
  transfers between devices with their start and end apart: 3, of which 3 were waited for; matrix products, arithmetic and copies ran while one was open for 0% of the time, Pallas kernels for 4%

profile of v2, /device:TPU:0, one launch (start us, length us, event | category | flops | bytes accessed | tf_op | source)
XLA Modules:
  0.0 62.1 jit_solution(2444614434170791914)
XLA Ops:
  0.6 0.0 copy-start.4
  0.6 0.0 copy-start
  0.7 0.0 copy-start.1
  0.7 0.0 copy-start.2
  0.7 0.0 copy-start.3
  0.7 6.2 %older.1 = (f32[32,4,384]{2,1,0:T(4,128)}, f32[3,96,128]{2,1,0:T(8,128)S(1)}, f32[24,128]{1,0:T(8,128)S(1)}, bf16[3,24,64,128]{3,2,1,0:T(8,128)(2,1)S(1)}) custom-call(bf16[12,24,64,128]{3,2,1,0:T(8,128)(2,1)} %bitcast.12, bf16[12,3072]{1,0:T(8,128)(2,1)} %history.1, s32[12,1,1,24]{3,2,1,0:T(1,128)} %rows_in.11, s32[12,1,1,24]{3,2,1,0:T(1,128)} %cols_in.11, ...), custom_call_target="tpu_custom_call" | custom-call | flops 188743680 | bytes 2949120 | tf_op jit(solution)/shard_map/older/pallas_call | solution.py:243
  6.9 7.3 %all-to-all-start = ((f32[32,4,384]{2,1,0:T(4,128)}), f32[32,4,384]{2,1,0:T(4,128)S(1)}, u32[]{:S(2)}, u32[]{:S(2)}) async-start(f32[32,4,384]{2,1,0:T(4,128)} %get-tuple-element.17), calls=%async_computation | async-start | bytes 393216 | tf_op jit(solution)/shard_map/all_to_all | solution.py:285
  14.2 0.0 copy-done.4
  14.2 0.0 copy-done
  14.2 0.0 copy-done.1
  14.2 0.0 copy-done.2
  14.3 0.0 copy-done.3
  14.3 5.8 %all_gather.3 = f32[5,24,128]{2,0,1:T(8,128)S(1)} all-gather(f32[5,6,128]{2,0,1:T(8,128)S(1)} %stack.3), channel_id=1, replica_groups=mesh['src'=8,'rcv'=4] {'rcv'}, dimensions={1}, use_global_device_ids=true | all-gather | bytes 76800 | tf_op jit(solution)/shard_map/all_gather | solution.py:253
  20.1 3.0 %all-to-all-done.recv = f32[32,4,384]{2,1,0:T(4,128)S(1)} async-done(((f32[32,4,384]{2,1,0:T(4,128)}), f32[32,4,384]{2,1,0:T(4,128)S(1)}, u32[]{:S(2)}, u32[]{:S(2)}) %all-to-all-start) | async-done | bytes 196640 | tf_op jit(solution)/shard_map/all_to_all | solution.py:285
  23.0 1.9 %step.3 = (f32[32,4,384]{2,1,0:T(4,128)}, f32[24,128]{1,0:T(8,128)S(1)}, f32[24,128]{1,0:T(8,128)S(1)}) custom-call(f32[32,4,384]{2,1,0:T(4,128)S(1)} %all-to-all-done.recv, f32[5,24,128]{2,1,0:T(8,128)S(1)} %copy.13.fields, f32[24,128]{1,0:T(8,128)S(1)} %get-tuple-element.18.guess, f32[24,128]{1,0:T(8,128)S(1)} %slice_bitcast_fusion.state_in, ...), custom_call_target="tpu_custom_call" | custom-call | flops 3145728 | bytes 49152 | tf_op jit(solution)/shard_map/step/pallas_call | solution.py:243
  25.0 2.7 %all-to-all-start.1 = ((f32[32,4,384]{2,1,0:T(4,128)}), f32[32,4,384]{2,1,0:T(4,128)S(1)}, u32[]{:S(2)}, u32[]{:S(2)}) async-start(f32[32,4,384]{2,1,0:T(4,128)} %get-tuple-element.21), calls=%async_computation.1 | async-start | bytes 393216 | tf_op jit(solution)/shard_map/all_to_all | solution.py:306
  27.7 1.3 %later.2.rest = f32[2,96,128]{2,1,0:T(8,128)S(1)} custom-call(f32[24,128]{1,0:T(8,128)S(1)} %get-tuple-element.22.slip_rate.guess.refs_0_, f32[3,96,128]{2,1,0:T(8,128)S(1)} %get-tuple-element.19.rest, bf16[3,24,64,128]{3,2,1,0:T(8,128)(2,1)S(1)} %get-tuple-element.20.panels, s32[12,1,1,24]{3,2,1,0:T(1,128)} %rows_in.11, s32[12,1,1,24]{3,2,1,0:T(1,128)} %cols_in.11, ...), custom_call_target="tpu_custom_call" | custom-call | flops 6291456 | bytes 98304 | tf_op jit(solution)/shard_map/later/pallas_call | solution.py:243
  29.1 7.5 %all-to-all-done.1.recv = f32[32,4,384]{2,1,0:T(4,128)S(1)} async-done(((f32[32,4,384]{2,1,0:T(4,128)}), f32[32,4,384]{2,1,0:T(4,128)S(1)}, u32[]{:S(2)}, u32[]{:S(2)}) %all-to-all-start.1) | async-done | bytes 196640 | tf_op jit(solution)/shard_map/all_to_all | solution.py:306
  36.6 1.9 %step.4 = (f32[32,4,384]{2,1,0:T(4,128)}, f32[24,128]{1,0:T(8,128)S(1)}, f32[24,128]{1,0:T(8,128)S(1)}) custom-call(f32[32,4,384]{2,1,0:T(4,128)S(1)} %all-to-all-done.1.recv, f32[5,24,128]{2,1,0:T(8,128)S(1)} %copy.13.fields, f32[24,128]{1,0:T(8,128)S(1)} %get-tuple-element.22.slip_rate.guess.refs_0_, f32[24,128]{1,0:T(8,128)S(1)} %get-tuple-element.23.state_in, ...), custom_call_target="tpu_custom_call" | custom-call | flops 3145728 | bytes 49152 | tf_op jit(solution)/shard_map/step/pallas_call | solution.py:243
  38.6 2.7 %all-to-all-start.2 = ((f32[32,4,384]{2,1,0:T(4,128)}), f32[32,4,384]{2,1,0:T(4,128)S(1)}, u32[]{:S(2)}, u32[]{:S(2)}) async-start(f32[32,4,384]{2,1,0:T(4,128)} %get-tuple-element.24), calls=%async_computation.2 | async-start | bytes 393216 | tf_op jit(solution)/shard_map/all_to_all | solution.py:306
  41.3 1.2 %later.3.rest = f32[1,96,128]{2,1,0:T(8,128)S(1)} custom-call(f32[24,128]{1,0:T(8,128)S(1)} %get-tuple-element.25.slip_rate.guess.refs_1_, f32[2,96,128]{2,1,0:T(8,128)S(1)} %later.2.rest, bf16[3,24,64,128]{3,2,1,0:T(8,128)(2,1)S(1)} %get-tuple-element.20.panels, s32[12,1,1,24]{3,2,1,0:T(1,128)} %rows_in.11, s32[12,1,1,24]{3,2,1,0:T(1,128)} %cols_in.11, ...), custom_call_target="tpu_custom_call" | custom-call | flops 3145728 | bytes 49152 | tf_op jit(solution)/shard_map/later/pallas_call | solution.py:243
  42.5 7.7 %all-to-all-done.2.recv = f32[32,4,384]{2,1,0:T(4,128)S(1)} async-done(((f32[32,4,384]{2,1,0:T(4,128)}), f32[32,4,384]{2,1,0:T(4,128)S(1)}, u32[]{:S(2)}, u32[]{:S(2)}) %all-to-all-start.2) | async-done | bytes 196640 | tf_op jit(solution)/shard_map/all_to_all | solution.py:306
  50.2 1.2 %step.5 = (f32[8,4,384]{2,1,0:T(4,128)S(1)}, f32[24,128]{1,0:T(8,128)S(1)}, f32[24,128]{1,0:T(8,128)S(1)}) custom-call(f32[32,4,384]{2,1,0:T(4,128)S(1)} %all-to-all-done.2.recv, f32[5,24,128]{2,1,0:T(8,128)S(1)} %copy.13.fields, f32[24,128]{1,0:T(8,128)S(1)} %get-tuple-element.25.slip_rate.guess.refs_1_, f32[24,128]{1,0:T(8,128)S(1)} %get-tuple-element.26.state_in, ...), custom_call_target="tpu_custom_call" | custom-call | flops 3145728 | bytes 49152 | tf_op jit(solution)/shard_map/step/pallas_call | solution.py:243
  51.4 9.9 %all_to_all.20.recv = f32[8,4,384]{2,1,0:T(4,128)S(1)} all-to-all(f32[8,4,384]{2,1,0:T(4,128)S(1)} %get-tuple-element.27), channel_id=1, replica_groups=mesh['src'=8,'rcv'=4] {'src'}, dimensions={0} | all-to-all | bytes 98304 | tf_op jit(solution)/shard_map/all_to_all | solution.py:306
  61.3 0.8 %last.1 = (f32[4,768]{1,0:T(4,128)}, f32[6,128]{1,0:T(8,128)}) custom-call(f32[8,4,384]{2,1,0:T(4,128)S(1)} %all_to_all.20.recv, f32[6,128]{1,0:T(8,128)S(1)} %bitcast.8, f32[6,128]{1,0:T(8,128)S(1)} %bitcast.9, f32[6,128]{1,0:T(8,128)S(1)} %bitcast.10, f32[6,128]{1,0:T(8,128)S(1)} %bitcast.11, f32[24,128]{1,0:T(8,128)S(1)} %get-tuple-element.28.state_in, ...), custom_call_target="tpu_custom_call" | custom-call | flops 1000000 | bytes 15625 | tf_op jit(solution)/shard_map/last/pallas_call | solution.py:243
  (8 shorter events, 0.1 us)
Async XLA Ops:
  0.6 13.5 %copy-start.4 = (f32[768]{0:T(1024)S(1)}, f32[768]{0:T(1024)}, u32[]{:S(2)}) copy-start(f32[768]{0:T(1024)} %param.19) | copy-start | bytes 9220
  0.6 13.5 %copy-start = (f32[768]{0:T(1024)S(1)}, f32[768]{0:T(1024)}, u32[]{:S(2)}) copy-start(f32[768]{0:T(1024)} %param.15) | copy-start | bytes 9220
  0.7 13.6 %copy-start.1 = (f32[768]{0:T(1024)S(1)}, f32[768]{0:T(1024)}, u32[]{:S(2)}) copy-start(f32[768]{0:T(1024)} %param.16) | copy-start | bytes 9220
  0.7 13.6 %copy-start.2 = (f32[768]{0:T(1024)S(1)}, f32[768]{0:T(1024)}, u32[]{:S(2)}) copy-start(f32[768]{0:T(1024)} %param.17) | copy-start | bytes 9220
  0.7 13.6 %copy-start.3 = (f32[768]{0:T(1024)S(1)}, f32[768]{0:T(1024)}, u32[]{:S(2)}) copy-start(f32[768]{0:T(1024)} %param.18) | copy-start | bytes 9220
  6.9 16.2 %all-to-all-start = ((f32[32,4,384]{2,1,0:T(4,128)}), f32[32,4,384]{2,1,0:T(4,128)S(1)}, u32[]{:S(2)}, u32[]{:S(2)}) async-start(f32[32,4,384]{2,1,0:T(4,128)} %get-tuple-element.17), calls=%async_computation | async-start | bytes 393216 | tf_op jit(solution)/shard_map/all_to_all | solution.py:285
  25.0 11.6 %all-to-all-start.1 = ((f32[32,4,384]{2,1,0:T(4,128)}), f32[32,4,384]{2,1,0:T(4,128)S(1)}, u32[]{:S(2)}, u32[]{:S(2)}) async-start(f32[32,4,384]{2,1,0:T(4,128)} %get-tuple-element.21), calls=%async_computation.1 | async-start | bytes 393216 | tf_op jit(solution)/shard_map/all_to_all | solution.py:306
  38.6 11.6 %all-to-all-start.2 = ((f32[32,4,384]{2,1,0:T(4,128)}), f32[32,4,384]{2,1,0:T(4,128)S(1)}, u32[]{:S(2)}, u32[]{:S(2)}) async-start(f32[32,4,384]{2,1,0:T(4,128)} %get-tuple-element.24), calls=%async_computation.2 | async-start | bytes 393216 | tf_op jit(solution)/shard_map/all_to_all | solution.py:306

commit v3 on v2

--- a/solution.py
+++ b/solution.py
@@ -15,8 +15,12 @@
 LANES = 128
 HALF = LANES // 2
 ROWS = 4
-IN_FLIGHT = 3
+IN_FLIGHT = 5
+GROUP = 4
+SLOT_ROWS = 32
+PARTS = 3
 TAPS = 24
+LEAD = 8
 VMEM_LIMIT = 16 * 1024 * 1024
 
 
@@ -51,12 +55,10 @@
     return shear, normal
 
 
-def pack_messages(send, acc, own_blocks, n_dest, dups, stride):
+def pack_messages(send, partials, own_blocks, n_dest, dups):
     for dest in range(n_dest):
         for tile in range(own_blocks // ROWS):
-            first = (dest * own_blocks + tile * ROWS) * stride
-            rows = pl.ds(first, ROWS, stride=stride) if stride > 1 else pl.ds(first, ROWS)
-            piece = acc[rows, :]
+            piece = partials(dest * own_blocks + tile * ROWS, ROWS)
             for dup in range(dups):
                 send[dest * dups + dup, :, tile * LANES:(tile + 1) * LANES] = piece
 
@@ -73,18 +75,50 @@
     return total[pl.ds(0, pairs, stride=2), :], total[pl.ds(1, pairs, stride=2), :]
 
 
+def make_tables(rows, cols, scales, gather, scatter, weights):
+    slots = rows.shape[-1]
+    lane = lax.broadcasted_iota(jnp.int32, (SLOT_ROWS, LANES), 1)
+    diagonal = lax.broadcasted_iota(jnp.int32, (SLOT_ROWS, LANES), 0) == lane
+    rest = jnp.full((1, LANES - slots), -1.0, jnp.float32)
+
+    def widened(values):
+        return jnp.concatenate([values.astype(jnp.float32), rest], axis=1)
+
+    def column(values):
+        spread = jnp.where(diagonal, jnp.broadcast_to(values, diagonal.shape), 0.0)
+        return jnp.sum(spread, axis=1, keepdims=True)
+
+    one_row = lax.broadcasted_iota(jnp.int32, (1, LANES), 1)
+    block = lax.broadcasted_iota(jnp.int32, (scatter.shape[1], LANES), 0).astype(jnp.float32)
+    for lag in range(STEPS - 1):
+        row_ids = widened(rows[lag, 0])
+        for part in range(1, PARTS):
+            at = one_row >= part * SLOT_ROWS
+            row_ids = jnp.where(at, pltpu.roll(widened(rows[lag, 0]), part * SLOT_ROWS, 1), row_ids)
+        row_ids = jnp.where(one_row < PARTS * SLOT_ROWS, row_ids, -1.0)
+        scatter[lag] = (block == row_ids).astype(jnp.float32).astype(jnp.bfloat16)
+        picks = column(widened(cols[lag, 0])) == lane.astype(jnp.float32)
+        gather[lag] = picks.astype(jnp.float32).astype(jnp.bfloat16)
+        weights[lag] = jnp.broadcast_to(column(widened(scales[lag, 0])), weights.shape[1:])
+
+
 def older_kernel(
-    panels, history, rows_in, cols_in, scales_in, send, rest, guess, recent,
-    panel_buf, history_buf, rows, cols, scales, sources, acc, sems, small_sems, out_sem,
+    panels, history, rows_in, cols_in, scales_in,
+    send, rest, guess, recent, gather, scatter, weights,
+    panel_buf, history_buf, rows, cols, scales, rows_now, cols_now, scales_now, sources, acc,
+    sems, small_sems, out_sem,
     *, lags, slots, n_src, n_rcv, own_blocks,
 ):
     src_blocks = n_rcv * own_blocks
     recv_blocks = n_src * own_blocks
+    recent_lags = pl.ds(0, STEPS - 1)
     smalls = [
         pltpu.make_async_copy(source, target, small_sems.at[at])
-        for at, (source, target) in enumerate(
-            [(history, history_buf), (cols_in, cols), (rows_in, rows), (scales_in, scales)]
-        )
+        for at, (source, target) in enumerate([
+            (history, history_buf), (cols_in, cols), (rows_in, rows), (scales_in, scales),
+            (rows_in.at[recent_lags], rows_now), (cols_in.at[recent_lags], cols_now),
+            (scales_in.at[recent_lags], scales_now),
+        ])
     ]
 
     def panel_copy(lag):
@@ -96,15 +130,21 @@
         panel_copy(lag).start()
     acc[...] = jnp.zeros_like(acc)
     tail = jnp.zeros((TAPS - lags, LANES), jnp.float32)
+    sources[0:LEAD, :] = jnp.zeros((LEAD, LANES), jnp.float32)
     smalls[0].wait()
     for pair in range(src_blocks // 2):
         tile = history_buf[:, pair * LANES:(pair + 1) * LANES].astype(jnp.float32)
         for half in range(2):
-            base = (2 * pair + half) * TAPS
+            base = LEAD + (2 * pair + half) * TAPS
             sources[base:base + lags, :] = tile if half == 0 else pltpu.roll(tile, HALF, 1)
             sources[base + lags:base + TAPS, :] = tail
     for copy in smalls[1:]:
         copy.wait()
+    make_tables(rows_now, cols_now, scales_now, gather, scatter, weights)
+
+    top = lax.broadcasted_iota(jnp.int32, (8, LANES), 0) < STEPS
+    match = top == (lax.broadcasted_iota(jnp.int32, (8, LANES), 1) < HALF)
+    zero = jnp.zeros((8, LANES), jnp.float32)
 
     def one_lag(lag, carry):
         panel_copy(lag).wait()
@@ -113,84 +153,96 @@
         def _():
             panel_copy(lag + IN_FLIGHT).start()
 
-        for slot in range(slots):
-            col = cols[lag, 0, 0, slot]
-            picked = sources[pl.ds(col * TAPS + (lags - 1) - lag, 8), :]
-            picked = picked[:, :HALF].astype(jnp.bfloat16)
-            term = jnp.dot(picked, panel_buf[lag, slot], preferred_element_type=jnp.float32)
-            at = pl.ds(pl.multiple_of(rows[lag, 0, 0, slot] * 8, 8), 8)
-            acc[at, :] = acc[at, :] + term * scales[lag, 0, 0, slot]
+        first_tap = LEAD + (lags - 1) - lag
+        for group in range(0, slots, GROUP):
+            pairs = []
+            for slot in range(group, group + GROUP, 2):
+                low = sources[pl.ds(cols[lag, 0, 0, slot] * TAPS + first_tap, 8), :]
+                partner = cols[lag, 0, 0, slot + 1] ^ 1
+                high = sources[pl.ds(partner * TAPS + first_tap - STEPS, 8), :]
+                pairs.append(jnp.where(match, jnp.where(top, low, high), 0.0))
+            columns = [
+                jnp.concatenate([pair if at == to else zero for at in range(len(pairs))], axis=0)
+                for to, pair in enumerate(pairs)
+            ]
+            picked = jnp.concatenate(columns, axis=1).astype(jnp.bfloat16)
+            panel = panel_buf[lag, group:group + GROUP].reshape(GROUP * HALF, LANES)
+            terms = jnp.dot(picked, panel, preferred_element_type=jnp.float32)
+            for pair in range(len(pairs)):
+                slot = group + 2 * pair
+                scale = jnp.where(top, scales[lag, 0, 0, slot], scales[lag, 0, 0, slot + 1])
+                term = terms[8 * pair:8 * pair + 8] * scale
+                for part, addend in enumerate([jnp.where(top, term, 0.0), jnp.where(top, 0.0, term)]):
+                    at = pl.ds(pl.multiple_of(rows[lag, 0, 0, slot + part] * 8, 8), 8)
+                    acc[at, :] = acc[at, :] + addend
         return carry
 
     lax.fori_loop(0, lags, one_lag, 0)
-    handed_on = pltpu.make_async_copy(panel_buf.at[pl.ds(0, STEPS - 1)], recent, out_sem)
+    handed_on = pltpu.make_async_copy(panel_buf.at[recent_lags], recent, out_sem)
     handed_on.start()
-    pack_messages(send, acc, own_blocks, n_src, n_rcv, 8)
+
+    def partials(first_row, count, step):
+        low, high = [
+            acc[pl.ds(first_row * 8 + start, count, stride=8), :] for start in (step, STEPS + step)
+        ]
+        return low + high
+
+    pack_messages(send, lambda first, count: partials(first, count, 0), own_blocks, n_src, n_rcv)
     for step in range(1, STEPS):
-        rest[step - 1] = acc[pl.ds(step, recv_blocks, stride=8), :]
-    guess[...] = sources[pl.ds(lags - 1, src_blocks // 2, stride=2 * TAPS), :]
+        rest[step - 1] = partials(0, recv_blocks, step)
+    guess[...] = sources[pl.ds(LEAD + lags - 1, src_blocks // 2, stride=2 * TAPS), :]
     handed_on.wait()
-
-
-def small_copies(sources, targets, sems):
-    return [
-        pltpu.make_async_copy(source, target, sems.at[at])
-        for at, (source, target) in enumerate(zip(sources, targets))
-    ]
 
 
 def spread_sources(slip_rate, sources):
     pairs = slip_rate.shape[0]
-    sources[pl.ds(0, pairs, stride=2), :] = slip_rate
-    sources[pl.ds(1, pairs, stride=2), :] = pltpu.roll(slip_rate, HALF, 1)
-
-
-def add_terms(acc_at, lag, panels, sources, rows, cols, scales, slots):
-    for slot in range(slots):
-        picked = sources[pl.ds(cols[lag, 0, 0, slot], 1), :]
-        picked = jnp.broadcast_to(picked[:, :HALF], (8, HALF)).astype(jnp.bfloat16)
-        term = jnp.dot(picked, panels[lag, slot], preferred_element_type=jnp.float32)
-        at = pl.ds(rows[lag, 0, 0, slot], 1)
-        acc_at[at, :] = acc_at[at, :] + term[:1] * scales[lag, 0, 0, slot]
+    low = lax.broadcasted_iota(jnp.int32, slip_rate.shape, 1) < HALF
+    turned = pltpu.roll(slip_rate, HALF, 1)
+    sources[pl.ds(0, pairs, stride=2), :] = jnp.where(low, slip_rate, turned)
+    sources[pl.ds(1, pairs, stride=2), :] = jnp.where(low, turned, slip_rate)
+
+
+def new_terms(lag, panels, sources, gather, scatter, weights):
+    slots, width, wide = panels.shape[1:]
+    rounded = sources[...].astype(jnp.bfloat16)
+    picked = jnp.dot(gather[lag][:, :rounded.shape[0]], rounded, preferred_element_type=jnp.float32)
+    lane = lax.broadcasted_iota(jnp.int32, picked.shape, 1)
+    row = lax.broadcasted_iota(jnp.int32, picked.shape, 0)
+    first = row - jnp.where(lane < HALF, 0, 1)
+    tiles = [
+        jnp.where(first == slot, picked, 0.0).astype(jnp.bfloat16) for slot in range(0, slots, 2)
+    ]
+    panel = panels[lag].reshape(slots * width, wide)
+    terms = jnp.dot(jnp.concatenate(tiles, axis=1), panel, preferred_element_type=jnp.float32)
+    left = terms * weights[lag]
+    parts = []
+    for part in range(PARTS):
+        parts.append(left.astype(jnp.bfloat16))
+        left = left - parts[-1].astype(jnp.float32)
+    stacked = jnp.concatenate(parts, axis=0)
+    return jnp.dot(scatter[lag][:, :stacked.shape[0]], stacked, preferred_element_type=jnp.float32)
 
 
 def step_kernel(
-    recv, fields, guess, state_in, rest, panels, rows_in, cols_in, scales_in,
-    send, slip_out, state_out,
-    rows, cols, scales, total, sources, acc, sems,
-    *, step_no, rest_at, slots, n_src, n_rcv, own_blocks, dups,
+    recv, fields, guess, state_in, rest, panels, gather, scatter, weights,
+    send, slip_out, state_out, total, sources, acc,
+    *, step_no, n_src, n_rcv, own_blocks, dups,
 ):
-    copies = small_copies((cols_in, rows_in, scales_in), (cols, rows, scales), sems)
-    for copy in copies:
-        copy.start()
     shear, normal = split_stress(*sum_messages(recv, total, own_blocks, n_src, n_rcv))
     slip_rate, next_state = friction_solve(
         shear, normal, step_no, guess[...], state_in[...], [fields[kind] for kind in range(4)]
     )
+    spread_sources(slip_rate, sources)
+    acc[...] = rest[0] + new_terms(0, panels, sources, gather, scatter, weights)
+    pack_messages(send, lambda first, count: acc[pl.ds(first, count), :], own_blocks, n_src, dups)
     slip_out[...] = slip_rate
     state_out[...] = next_state
-    spread_sources(slip_rate, sources)
-    acc[...] = rest[rest_at]
-    for copy in copies:
-        copy.wait()
-    add_terms(acc, 0, panels, sources, rows, cols, scales, slots)
-    pack_messages(send, acc, own_blocks, n_src, dups, 1)
-
-
-def later_kernel(
-    slip_rate, rest, panels, rows_in, cols_in, scales_in, rest_out,
-    rows, cols, scales, sources, sems, *, later, slots,
-):
-    copies = small_copies((cols_in, rows_in, scales_in), (cols, rows, scales), sems)
-    for copy in copies:
-        copy.start()
+
+
+def later_kernel(slip_rate, rest, panels, gather, scatter, weights, rest_out, sources):
     spread_sources(slip_rate[...], sources)
-    for at in range(later):
-        rest_out[at] = rest[at + 1]
-    for copy in copies:
-        copy.wait()
-    for at in range(later):
-        add_terms(rest_out.at[at], at + 1, panels, sources, rows, cols, scales, slots)
+    for at in range(rest_out.shape[0]):
+        rest_out[at] = rest[at + 1] + new_terms(at + 1, panels, sources, gather, scatter, weights)
 
 
 def last_kernel(
@@ -230,12 +282,6 @@
     hbm = pl.BlockSpec(memory_space=pltpu.HBM)
     vmem = pl.BlockSpec(memory_space=pltpu.VMEM)
     sizes = dict(slots=slots, n_src=n_src, n_rcv=n_rcv, own_blocks=own_blocks)
-    index_bufs = [
-        pltpu.SMEM(block_rows.shape, jnp.int32),
-        pltpu.SMEM(block_cols.shape, jnp.int32),
-        pltpu.SMEM(scales.shape, f32),
-    ]
-
     def shape(*dims, dtype=f32):
         return jax.ShapeDtypeStruct(dims, dtype)
 
@@ -257,7 +303,7 @@
         for array in (panels, history, block_rows, block_cols, scales)
     ]
     one_lag = 2 * slots * width * 2 * width * 8
-    send, rest, guess, recent = call(
+    send, rest, guess, recent, *tables = call(
         functools.partial(older_kernel, lags=lags, **sizes),
         [hbm] * 5,
         [
@@ -265,15 +311,19 @@
             shape(STEPS - 1, recv_rows, LANES),
             shape(src_blocks // 2, LANES),
             shape(STEPS - 1, slots, width, 2 * width, dtype=panels.dtype),
+            shape(STEPS - 1, SLOT_ROWS, LANES, dtype=jnp.bfloat16),
+            shape(STEPS - 1, recv_rows, LANES, dtype=jnp.bfloat16),
+            shape(STEPS - 1, SLOT_ROWS, LANES),
         ],
         [
             pltpu.VMEM(panels.shape, panels.dtype),
             pltpu.VMEM(history.shape, history.dtype),
-            *index_bufs,
-            pltpu.VMEM((src_blocks * TAPS, LANES), f32),
+            *[pltpu.SMEM(array.shape, array.dtype) for array in table],
+            *[pltpu.VMEM((STEPS - 1, *array.shape[1:]), array.dtype) for array in table],
+            pltpu.VMEM((LEAD + src_blocks * TAPS, LANES), f32),
             pltpu.VMEM((recv_rows * 8, LANES), f32),
             pltpu.SemaphoreType.DMA((lags,)),
-            pltpu.SemaphoreType.DMA((4,)),
+            pltpu.SemaphoreType.DMA((7,)),
             pltpu.SemaphoreType.DMA,
         ],
         "older", [panels, history, *table], 60 * one_lag, limit=32 * 1024 * 1024,
@@ -281,25 +331,26 @@
 
     state = fields[4]
     slips = []
+    recv = lax.all_to_all(send, ("src", "rcv"), 0, 0, tiled=True)
     for step_no in range(STEPS - 1):
-        recv = lax.all_to_all(send, ("src", "rcv"), 0, 0, tiled=True) if step_no == 0 else recv
         last = step_no == STEPS - 2
         dups = 1 if last else n_rcv
         send, slip_rate, state = call(
-            functools.partial(step_kernel, step_no=step_no, rest_at=0, dups=dups, **sizes),
-            [vmem] * 6 + [hbm] * 3,
+            functools.partial(
+                step_kernel, step_no=step_no, dups=dups, n_src=n_src, n_rcv=n_rcv, own_blocks=own_blocks
+            ),
+            [vmem] * 9,
             [
                 shape(n_src * dups, *message),
                 shape(src_blocks // 2, LANES),
                 shape(src_blocks // 2, LANES),
             ],
-            index_bufs + [
+            [
                 pltpu.VMEM((src_blocks, LANES), f32),
                 pltpu.VMEM((src_blocks, LANES), f32),
                 pltpu.VMEM((recv_rows, LANES), f32),
-                pltpu.SemaphoreType.DMA((3,)),
             ],
-            "step", [recv, fields, guess, state, rest, recent, *table], one_lag,
+            "step", [recv, fields, guess, state, rest, recent, *tables], one_lag,
         )
         guess = slip_rate
         slips.append(slip_rate)
@@ -307,14 +358,11 @@
         later = STEPS - 2 - step_no
         if later:
             rest, = call(
-                functools.partial(later_kernel, later=later, slots=slots),
-                [vmem] * 3 + [hbm] * 3,
+                later_kernel,
+                [vmem] * 6,
                 [shape(later, recv_rows, LANES)],
-                index_bufs + [
-                    pltpu.VMEM((src_blocks, LANES), f32),
-                    pltpu.SemaphoreType.DMA((3,)),
-                ],
-                "later", [slip_rate, rest, recent, *table], later * one_lag,
+                [pltpu.VMEM((src_blocks, LANES), f32)],
+                "later", [slip_rate, rest, recent, *tables], later * one_lag,
             )
 
     slip_rates, state = call(

time: 62.9 us -> 60 us (0.954)
  Pallas kernels: 14.6 us -> 10.8 us
  waiting for transfers between devices: 18.1 us -> 19.5 us
    pallas_call x7, Pallas kernels: 14.6 us -> 10.8 us  [call(): pl.pallas_call(body, in_specs=ins, out_specs=[vmem] * len(outs), out_shap...]
    all_to_all x2, waiting for transfers between devices: 15.2 us -> 16.6 us  [per_device(): lax.all_to_all(send, 'src' if last else ('src', 'rcv'), 0, 0, tiled=True)]
  transfers between devices with their start and end apart: 3 -> 3, of which waited for: 3 -> 3; matrix products, arithmetic and copies ran while one was open for 0% -> 0% of each run, Pallas kernels for 4% -> 2%
where the time goes in v3:
time: 60 us; the launch traced here: 59.6 us
  waiting for transfers between devices  19.5 us (32%)
  blocking collectives  15.6 us (26%)
  starting transfers between devices  12.7 us (21%)
  Pallas kernels  10.8 us (18%)
  between operations  0.79 us (1%)
    all_to_all x2, waiting for transfers between devices, per_device(): lax.all_to_all(send, 'src' if last else ('src', 'rcv'), 0, 0, tiled=True)  16.6 us
    pallas_call x7, Pallas kernels, call(): pl.pallas_call(body, in_specs=ins, out_specs=[vmem] * len(outs), out_shap...  10.8 us
    all_to_all x1, blocking collectives, per_device(): lax.all_to_all(send, 'src' if last else ('src', 'rcv'), 0, 0, tiled=True)  9.88 us
    all_to_all x1, starting transfers between devices, per_device(): recv = lax.all_to_all(send, ('src', 'rcv'), 0, 0, tiled=True)  7.31 us
    all_gather x1, blocking collectives, per_device(): fields = lax.all_gather(jnp.stack(own_fields), 'rcv', axis=1, tiled=True)  5.75 us
    all_to_all x2, starting transfers between devices, per_device(): lax.all_to_all(send, 'src' if last else ('src', 'rcv'), 0, 0, tiled=True)  5.42 us
    all_to_all x1, waiting for transfers between devices, per_device(): recv = lax.all_to_all(send, ('src', 'rcv'), 0, 0, tiled=True)  2.95 us
  transfers between devices with their start and end apart: 3, of which 3 were waited for; matrix products, arithmetic and copies ran while one was open for 0% of the time, Pallas kernels for 2%

profile of v3, /device:TPU:0, one launch (start us, length us, event | category | flops | bytes accessed | tf_op | source)
XLA Modules:
  0.0 59.6 jit_solution(159817954792119768)
XLA Ops:
  0.6 0.0 copy-start.4
  0.6 0.0 copy-start
  0.7 0.0 copy-start.1
  0.7 0.0 copy-start.2
  0.7 0.0 copy-start.3
  0.7 5.3 %older.1 = (f32[32,4,384]{2,1,0:T(4,128)}, f32[3,96,128]{2,1,0:T(8,128)S(1)}, f32[24,128]{1,0:T(8,128)S(1)}, bf16[3,24,64,128]{3,2,1,0:T(8,128)(2,1)S(1)}, bf16[...) custom-call(bf16[12,24,64,128]{3,2,1,0:T(8,128)(2,1)} %bitcast.12, ...), custom_call_target="tpu_custom_call" | custom-call | flops 188743680 | bytes 2949120 | tf_op jit(solution)/shard_map/older/pallas_call | solution.py:289
  6.0 7.3 %all-to-all-start = ((f32[32,4,384]{2,1,0:T(4,128)}), f32[32,4,384]{2,1,0:T(4,128)S(1)}, u32[]{:S(2)}, u32[]{:S(2)}) async-start(f32[32,4,384]{2,1,0:T(4,128)} %get-tuple-element.20), calls=%async_computation | async-start | bytes 393216 | tf_op jit(solution)/shard_map/all_to_all | solution.py:334
  13.3 0.0 copy-done.4
  13.3 0.0 copy-done
  13.3 0.0 copy-done.1
  13.4 0.0 copy-done.2
  13.4 0.0 copy-done.3
  13.5 5.8 %all_gather.3 = f32[5,24,128]{2,0,1:T(8,128)S(1)} all-gather(f32[5,6,128]{2,0,1:T(8,128)S(1)} %stack.3), channel_id=1, replica_groups=mesh['src'=8,'rcv'=4] {'rcv'}, dimensions={1}, use_global_device_ids=true | all-gather | bytes 76800 | tf_op jit(solution)/shard_map/all_gather | solution.py:299
  19.2 3.0 %all-to-all-done.recv = f32[32,4,384]{2,1,0:T(4,128)S(1)} async-done(((f32[32,4,384]{2,1,0:T(4,128)}), f32[32,4,384]{2,1,0:T(4,128)S(1)}, u32[]{:S(2)}, u32[]{:S(2)}) %all-to-all-start) | async-done | bytes 196640 | tf_op jit(solution)/shard_map/all_to_all | solution.py:334
  22.2 1.4 %step.3 = (f32[32,4,384]{2,1,0:T(4,128)}, f32[24,128]{1,0:T(8,128)S(1)}, f32[24,128]{1,0:T(8,128)S(1)}) custom-call(f32[32,4,384]{2,1,0:T(4,128)S(1)} %all-to-all-done.recv, f32[5,24,128]{2,1,0:T(8,128)S(1)} %copy.13.fields, f32[24,128]{1,0:T(8,128)S(1)} %get-tuple-element.21.guess, f32[24,128]{1,0:T(8,128)S(1)} %slice_bitcast_fusion.state_in, ...), custom_call_target="tpu_custom_call" | custom-call | flops 3145728 | bytes 49152 | tf_op jit(solution)/shard_map/step/pallas_call | solution.py:289
  23.6 2.7 %all-to-all-start.1 = ((f32[32,4,384]{2,1,0:T(4,128)}), f32[32,4,384]{2,1,0:T(4,128)S(1)}, u32[]{:S(2)}, u32[]{:S(2)}) async-start(f32[32,4,384]{2,1,0:T(4,128)} %get-tuple-element.27), calls=%async_computation.1 | async-start | bytes 393216 | tf_op jit(solution)/shard_map/all_to_all | solution.py:357
  26.3 0.7 %later.2.rest = f32[2,96,128]{2,1,0:T(8,128)S(1)} custom-call(f32[24,128]{1,0:T(8,128)S(1)} %get-tuple-element.28.slip_rate.guess.refs_0_, f32[3,96,128]{2,1,0:T(8,128)S(1)} %get-tuple-element.22.rest, bf16[3,24,64,128]{3,2,1,0:T(8,128)(2,1)S(1)} %get-tuple-element.23.panels, bf16[3,32,128]{2,1,0:T(8,128)(2,1)S(1)} %get-tuple-element.24.gather, ...), custom_call_target="tpu_custom_call" | custom-call | flops 6291456 | bytes 98304 | tf_op jit(solution)/shard_map/later/pallas_call | solution.py:289
  27.0 8.2 %all-to-all-done.1.recv = f32[32,4,384]{2,1,0:T(4,128)S(1)} async-done(((f32[32,4,384]{2,1,0:T(4,128)}), f32[32,4,384]{2,1,0:T(4,128)S(1)}, u32[]{:S(2)}, u32[]{:S(2)}) %all-to-all-start.1) | async-done | bytes 196640 | tf_op jit(solution)/shard_map/all_to_all | solution.py:357
  35.2 1.4 %step.4 = (f32[32,4,384]{2,1,0:T(4,128)}, f32[24,128]{1,0:T(8,128)S(1)}, f32[24,128]{1,0:T(8,128)S(1)}) custom-call(f32[32,4,384]{2,1,0:T(4,128)S(1)} %all-to-all-done.1.recv, f32[5,24,128]{2,1,0:T(8,128)S(1)} %copy.13.fields, f32[24,128]{1,0:T(8,128)S(1)} %get-tuple-element.28.slip_rate.guess.refs_0_, f32[24,128]{1,0:T(8,128)S(1)} %get-tuple-element.29.state_in, ...), custom_call_target="tpu_custom_call" | custom-call | flops 3145728 | bytes 49152 | tf_op jit(solution)/shard_map/step/pallas_call | solution.py:289
  36.6 2.7 %all-to-all-start.2 = ((f32[32,4,384]{2,1,0:T(4,128)}), f32[32,4,384]{2,1,0:T(4,128)S(1)}, u32[]{:S(2)}, u32[]{:S(2)}) async-start(f32[32,4,384]{2,1,0:T(4,128)} %get-tuple-element.30), calls=%async_computation.2 | async-start | bytes 393216 | tf_op jit(solution)/shard_map/all_to_all | solution.py:357
  39.3 0.5 later.3.rest
  39.8 8.4 %all-to-all-done.2.recv = f32[32,4,384]{2,1,0:T(4,128)S(1)} async-done(((f32[32,4,384]{2,1,0:T(4,128)}), f32[32,4,384]{2,1,0:T(4,128)S(1)}, u32[]{:S(2)}, u32[]{:S(2)}) %all-to-all-start.2) | async-done | bytes 196640 | tf_op jit(solution)/shard_map/all_to_all | solution.py:357
  48.2 0.7 %step.5 = (f32[8,4,384]{2,1,0:T(4,128)S(1)}, f32[24,128]{1,0:T(8,128)S(1)}, f32[24,128]{1,0:T(8,128)S(1)}) custom-call(f32[32,4,384]{2,1,0:T(4,128)S(1)} %all-to-all-done.2.recv, f32[5,24,128]{2,1,0:T(8,128)S(1)} %copy.13.fields, f32[24,128]{1,0:T(8,128)S(1)} %get-tuple-element.31.slip_rate.guess.refs_1_, f32[24,128]{1,0:T(8,128)S(1)} %get-tuple-element.32.state_in, ...), custom_call_target="tpu_custom_call" | custom-call | flops 3145728 | bytes 49152 | tf_op jit(solution)/shard_map/step/pallas_call | solution.py:289
  48.9 9.9 %all_to_all.20.recv = f32[8,4,384]{2,1,0:T(4,128)S(1)} all-to-all(f32[8,4,384]{2,1,0:T(4,128)S(1)} %get-tuple-element.33), channel_id=1, replica_groups=mesh['src'=8,'rcv'=4] {'src'}, dimensions={0} | all-to-all | bytes 98304 | tf_op jit(solution)/shard_map/all_to_all | solution.py:357
  58.8 0.8 %last.1 = (f32[4,768]{1,0:T(4,128)}, f32[6,128]{1,0:T(8,128)}) custom-call(f32[8,4,384]{2,1,0:T(4,128)S(1)} %all_to_all.20.recv, f32[6,128]{1,0:T(8,128)S(1)} %bitcast.8, f32[6,128]{1,0:T(8,128)S(1)} %bitcast.9, f32[6,128]{1,0:T(8,128)S(1)} %bitcast.10, f32[6,128]{1,0:T(8,128)S(1)} %bitcast.11, f32[24,128]{1,0:T(8,128)S(1)} %get-tuple-element.34.state_in, ...), custom_call_target="tpu_custom_call" | custom-call | flops 1000000 | bytes 15625 | tf_op jit(solution)/shard_map/last/pallas_call | solution.py:289
  (8 shorter events, 0.1 us)
Async XLA Ops:
  0.6 12.7 %copy-start.4 = (f32[768]{0:T(1024)S(1)}, f32[768]{0:T(1024)}, u32[]{:S(2)}) copy-start(f32[768]{0:T(1024)} %param.19) | copy-start | bytes 9220
  0.6 12.7 %copy-start = (f32[768]{0:T(1024)S(1)}, f32[768]{0:T(1024)}, u32[]{:S(2)}) copy-start(f32[768]{0:T(1024)} %param.15) | copy-start | bytes 9220
  0.7 12.7 %copy-start.1 = (f32[768]{0:T(1024)S(1)}, f32[768]{0:T(1024)}, u32[]{:S(2)}) copy-start(f32[768]{0:T(1024)} %param.16) | copy-start | bytes 9220
  0.7 12.7 %copy-start.2 = (f32[768]{0:T(1024)S(1)}, f32[768]{0:T(1024)}, u32[]{:S(2)}) copy-start(f32[768]{0:T(1024)} %param.17) | copy-start | bytes 9220
  0.7 12.7 %copy-start.3 = (f32[768]{0:T(1024)S(1)}, f32[768]{0:T(1024)}, u32[]{:S(2)}) copy-start(f32[768]{0:T(1024)} %param.18) | copy-start | bytes 9220
  6.0 16.2 %all-to-all-start = ((f32[32,4,384]{2,1,0:T(4,128)}), f32[32,4,384]{2,1,0:T(4,128)S(1)}, u32[]{:S(2)}, u32[]{:S(2)}) async-start(f32[32,4,384]{2,1,0:T(4,128)} %get-tuple-element.20), calls=%async_computation | async-start | bytes 393216 | tf_op jit(solution)/shard_map/all_to_all | solution.py:334
  23.6 11.6 %all-to-all-start.1 = ((f32[32,4,384]{2,1,0:T(4,128)}), f32[32,4,384]{2,1,0:T(4,128)S(1)}, u32[]{:S(2)}, u32[]{:S(2)}) async-start(f32[32,4,384]{2,1,0:T(4,128)} %get-tuple-element.27), calls=%async_computation.1 | async-start | bytes 393216 | tf_op jit(solution)/shard_map/all_to_all | solution.py:357
  36.6 11.6 %all-to-all-start.2 = ((f32[32,4,384]{2,1,0:T(4,128)}), f32[32,4,384]{2,1,0:T(4,128)S(1)}, u32[]{:S(2)}, u32[]{:S(2)}) async-start(f32[32,4,384]{2,1,0:T(4,128)} %get-tuple-element.30), calls=%async_computation.2 | async-start | bytes 393216 | tf_op jit(solution)/shard_map/all_to_all | solution.py:357

commit v4 on v3

--- a/solution.py
+++ b/solution.py
@@ -19,6 +19,7 @@
 GROUP = 4
 SLOT_ROWS = 32
 PARTS = 3
+MESSAGE_SCALE = 2.0 ** 22
 TAPS = 24
 LEAD = 8
 VMEM_LIMIT = 16 * 1024 * 1024
@@ -55,19 +56,32 @@
     return shear, normal
 
 
+def encode(partial):
+    scaled = partial * (1.0 / MESSAGE_SCALE)
+    return (scaled * scaled * scaled).astype(jnp.bfloat16)
+
+
+def decode(message):
+    cube = message.astype(jnp.float32)
+    magnitude = jnp.abs(cube)
+    root = jnp.exp2(jnp.log2(jnp.maximum(magnitude, 1e-38)) * (1.0 / 3.0)) * MESSAGE_SCALE
+    root = jnp.where(cube < 0.0, -root, root)
+    return jnp.where(magnitude > 0.0, root, 0.0)
+
+
 def pack_messages(send, partials, own_blocks, n_dest, dups):
     for dest in range(n_dest):
         for tile in range(own_blocks // ROWS):
-            piece = partials(dest * own_blocks + tile * ROWS, ROWS)
+            piece = encode(partials(dest * own_blocks + tile * ROWS, ROWS))
             for dup in range(dups):
                 send[dest * dups + dup, :, tile * LANES:(tile + 1) * LANES] = piece
 
 
 def sum_messages(recv, total, own_blocks, n_src, owners):
     for owner in range(owners):
-        part = recv[owner]
+        part = decode(recv[owner])
         for src in range(1, n_src):
-            part = part + recv[src * owners + owner]
+            part = part + decode(recv[src * owners + owner])
         for tile in range(own_blocks // ROWS):
             first = owner * own_blocks + tile * ROWS
             total[first:first + ROWS, :] = part[:, tile * LANES:(tile + 1) * LANES]
@@ -307,7 +321,7 @@
         functools.partial(older_kernel, lags=lags, **sizes),
         [hbm] * 5,
         [
-            shape(n_src * n_rcv, *message),
+            shape(n_src * n_rcv, *message, dtype=jnp.bfloat16),
             shape(STEPS - 1, recv_rows, LANES),
             shape(src_blocks // 2, LANES),
             shape(STEPS - 1, slots, width, 2 * width, dtype=panels.dtype),
@@ -341,7 +355,7 @@
             ),
             [vmem] * 9,
             [
-                shape(n_src * dups, *message),
+                shape(n_src * dups, *message, dtype=jnp.bfloat16),
                 shape(src_blocks // 2, LANES),
                 shape(src_blocks // 2, LANES),
             ],

time: 60 us -> 56.8 us (0.947)
  waiting for transfers between devices: 19.5 us -> 16.6 us
  blocking collectives: 15.6 us -> 14.5 us
  starting transfers between devices: 12.7 us -> 13.4 us
    all_to_all x2, waiting for transfers between devices: 16.6 us -> 14.4 us  [per_device(): lax.all_to_all(send, 'src' if last else ('src', 'rcv'), 0, 0, tiled=True)]
    all_to_all x1, blocking collectives: 9.88 us -> 9 us  [per_device(): lax.all_to_all(send, 'src' if last else ('src', 'rcv'), 0, 0, tiled=True)]
    all_to_all x1, waiting for transfers between devices: 2.95 us -> 2.16 us  [per_device(): recv = lax.all_to_all(send, ('src', 'rcv'), 0, 0, tiled=True)]
    all_to_all x2, starting transfers between devices: 5.42 us -> 6.11 us  [per_device(): lax.all_to_all(send, 'src' if last else ('src', 'rcv'), 0, 0, tiled=True)]
where the time goes in v4:
time: 56.8 us; the launch traced here: 56.4 us
  waiting for transfers between devices  16.6 us (29%)
  blocking collectives  14.5 us (26%)
  starting transfers between devices  13.4 us (24%)
  Pallas kernels  11 us (19%)
  between operations  0.79 us (1%)
    all_to_all x2, waiting for transfers between devices, per_device(): lax.all_to_all(send, 'src' if last else ('src', 'rcv'), 0, 0, tiled=True)  14.4 us
    pallas_call x7, Pallas kernels, call(): pl.pallas_call(body, in_specs=ins, out_specs=[vmem] * len(outs), out_shap...  11 us
    all_to_all x1, blocking collectives, per_device(): lax.all_to_all(send, 'src' if last else ('src', 'rcv'), 0, 0, tiled=True)  9 us
    all_to_all x1, starting transfers between devices, per_device(): recv = lax.all_to_all(send, ('src', 'rcv'), 0, 0, tiled=True)  7.31 us
    all_to_all x2, starting transfers between devices, per_device(): lax.all_to_all(send, 'src' if last else ('src', 'rcv'), 0, 0, tiled=True)  6.11 us
    all_gather x1, blocking collectives, per_device(): fields = lax.all_gather(jnp.stack(own_fields), 'rcv', axis=1, tiled=True)  5.47 us
    all_to_all x1, waiting for transfers between devices, per_device(): recv = lax.all_to_all(send, ('src', 'rcv'), 0, 0, tiled=True)  2.16 us
  transfers between devices with their start and end apart: 3, of which 3 were waited for; matrix products, arithmetic and copies ran while one was open for 0% of the time, Pallas kernels for 2%

profile of v4, /device:TPU:0, one launch (start us, length us, event | category | flops | bytes accessed | tf_op | source)
XLA Modules:
  0.0 56.4 jit_solution(9494571457905150311)
XLA Ops:
  0.6 0.0 copy-start.4
  0.6 0.0 copy-start
  0.7 0.0 copy-start.1
  0.7 0.0 copy-start.2
  0.7 0.0 copy-start.3
  0.7 5.3 %older.1 = (bf16[32,4,384]{2,1,0:T(4,128)(2,1)}, f32[3,96,128]{2,1,0:T(8,128)S(1)}, f32[24,128]{1,0:T(8,128)S(1)}, bf16[3,24,64,128]{3,2,1,0:T(8,128)(2,1)S(1)},...) custom-call(bf16[12,24,64,128]{3,2,1,0:T(8,128)(2,1)} %bitcast.12, ...), custom_call_target="tpu_custom_call" | custom-call | flops 188743680 | bytes 2949120 | tf_op jit(solution)/shard_map/older/pallas_call | solution.py:303
  6.0 7.3 %all-to-all-start = ((bf16[32,4,384]{2,1,0:T(4,128)(2,1)}), bf16[32,4,384]{2,1,0:T(4,128)(2,1)S(1)}, u32[]{:S(2)}, u32[]{:S(2)}) async-start(bf16[32,4,384]{2,1,0:T(4,128)(2,1)} %get-tuple-element.20), calls=%async_computation | async-start | bytes 196608 | tf_op jit(solution)/shard_map/all_to_all | solution.py:348
  13.3 0.0 copy-done.4
  13.3 0.0 copy-done
  13.3 0.0 copy-done.1
  13.3 0.0 copy-done.2
  13.4 0.0 copy-done.3
  13.4 5.5 %all_gather.3 = f32[5,24,128]{2,0,1:T(8,128)S(1)} all-gather(f32[5,6,128]{2,0,1:T(8,128)S(1)} %stack.3), channel_id=1, replica_groups=mesh['src'=8,'rcv'=4] {'rcv'}, dimensions={1}, use_global_device_ids=true | all-gather | bytes 76800 | tf_op jit(solution)/shard_map/all_gather | solution.py:313
  18.9 2.2 %all-to-all-done.recv = bf16[32,4,384]{2,1,0:T(4,128)(2,1)S(1)} async-done(((bf16[32,4,384]{2,1,0:T(4,128)(2,1)}), bf16[32,4,384]{2,1,0:T(4,128)(2,1)S(1)}, u32[]{:S(2)}, u32[]{:S(2)}) %all-to-all-start) | async-done | bytes 98336 | tf_op jit(solution)/shard_map/all_to_all | solution.py:348
  21.1 1.5 %step.3 = (bf16[32,4,384]{2,1,0:T(4,128)(2,1)}, f32[24,128]{1,0:T(8,128)S(1)}, f32[24,128]{1,0:T(8,128)S(1)}) custom-call(bf16[32,4,384]{2,1,0:T(4,128)(2,1)S(1)} %all-to-all-done.recv, f32[5,24,128]{2,1,0:T(8,128)S(1)} %copy.13.fields, f32[24,128]{1,0:T(8,128)S(1)} %get-tuple-element.21.guess, f32[24,128]{1,0:T(8,128)S(1)} %slice_bitcast_fusion.state_in, ...), custom_call_target="tpu_custom_call" | custom-call | flops 3145728 | bytes 49152 | tf_op jit(solution)/shard_map/step/pallas_call | solution.py:303
  22.6 3.6 %all-to-all-start.1 = ((bf16[32,4,384]{2,1,0:T(4,128)(2,1)}), bf16[32,4,384]{2,1,0:T(4,128)(2,1)S(1)}, u32[]{:S(2)}, u32[]{:S(2)}) async-start(bf16[32,4,384]{2,1,0:T(4,128)(2,1)} %get-tuple-element.27), calls=%async_computation.1 | async-start | bytes 196608 | tf_op jit(solution)/shard_map/all_to_all | solution.py:371
  26.1 0.7 %later.2.rest = f32[2,96,128]{2,1,0:T(8,128)S(1)} custom-call(f32[24,128]{1,0:T(8,128)S(1)} %get-tuple-element.28.slip_rate.guess.refs_0_, f32[3,96,128]{2,1,0:T(8,128)S(1)} %get-tuple-element.22.rest, bf16[3,24,64,128]{3,2,1,0:T(8,128)(2,1)S(1)} %get-tuple-element.23.panels, bf16[3,32,128]{2,1,0:T(8,128)(2,1)S(1)} %get-tuple-element.24.gather, ...), custom_call_target="tpu_custom_call" | custom-call | flops 6291456 | bytes 98304 | tf_op jit(solution)/shard_map/later/pallas_call | solution.py:303
  26.8 7.1 %all-to-all-done.1.recv = bf16[32,4,384]{2,1,0:T(4,128)(2,1)S(1)} async-done(((bf16[32,4,384]{2,1,0:T(4,128)(2,1)}), bf16[32,4,384]{2,1,0:T(4,128)(2,1)S(1)}, u32[]{:S(2)}, u32[]{:S(2)}) %all-to-all-start.1) | async-done | bytes 98336 | tf_op jit(solution)/shard_map/all_to_all | solution.py:371
  33.9 1.5 %step.4 = (bf16[32,4,384]{2,1,0:T(4,128)(2,1)}, f32[24,128]{1,0:T(8,128)S(1)}, f32[24,128]{1,0:T(8,128)S(1)}) custom-call(bf16[32,4,384]{2,1,0:T(4,128)(2,1)S(1)} %all-to-all-done.1.recv, f32[5,24,128]{2,1,0:T(8,128)S(1)} %copy.13.fields, f32[24,128]{1,0:T(8,128)S(1)} %get-tuple-element.28.slip_rate.guess.refs_0_, f32[24,128]{1,0:T(8,128)S(1)} %get-tuple-element.29.state_in, ...), custom_call_target="tpu_custom_call" | custom-call | flops 3145728 | bytes 49152 | tf_op jit(solution)/shard_map/step/pallas_call | solution.py:303
  35.4 2.6 %all-to-all-start.2 = ((bf16[32,4,384]{2,1,0:T(4,128)(2,1)}), bf16[32,4,384]{2,1,0:T(4,128)(2,1)S(1)}, u32[]{:S(2)}, u32[]{:S(2)}) async-start(bf16[32,4,384]{2,1,0:T(4,128)(2,1)} %get-tuple-element.30), calls=%async_computation.2 | async-start | bytes 196608 | tf_op jit(solution)/shard_map/all_to_all | solution.py:371
  38.0 0.5 later.3.rest
  38.5 7.3 %all-to-all-done.2.recv = bf16[32,4,384]{2,1,0:T(4,128)(2,1)S(1)} async-done(((bf16[32,4,384]{2,1,0:T(4,128)(2,1)}), bf16[32,4,384]{2,1,0:T(4,128)(2,1)S(1)}, u32[]{:S(2)}, u32[]{:S(2)}) %all-to-all-start.2) | async-done | bytes 98336 | tf_op jit(solution)/shard_map/all_to_all | solution.py:371
  45.8 0.8 %step.5 = (bf16[8,4,384]{2,1,0:T(4,128)(2,1)S(1)}, f32[24,128]{1,0:T(8,128)S(1)}, f32[24,128]{1,0:T(8,128)S(1)}) custom-call(bf16[32,4,384]{2,1,0:T(4,128)(2,1)S(1)} %all-to-all-done.2.recv, f32[5,24,128]{2,1,0:T(8,128)S(1)} %copy.13.fields, f32[24,128]{1,0:T(8,128)S(1)} %get-tuple-element.31.slip_rate.guess.refs_1_, ...), custom_call_target="tpu_custom_call" | custom-call | flops 3145728 | bytes 49152 | tf_op jit(solution)/shard_map/step/pallas_call | solution.py:303
  46.6 9.0 %all_to_all.20.recv = bf16[8,4,384]{2,1,0:T(4,128)(2,1)S(1)} all-to-all(bf16[8,4,384]{2,1,0:T(4,128)(2,1)S(1)} %get-tuple-element.33), channel_id=1, replica_groups=mesh['src'=8,'rcv'=4] {'src'}, dimensions={0} | all-to-all | bytes 49152 | tf_op jit(solution)/shard_map/all_to_all | solution.py:371
  55.6 0.8 %last.1 = (f32[4,768]{1,0:T(4,128)}, f32[6,128]{1,0:T(8,128)}) custom-call(bf16[8,4,384]{2,1,0:T(4,128)(2,1)S(1)} %all_to_all.20.recv, f32[6,128]{1,0:T(8,128)S(1)} %bitcast.8, f32[6,128]{1,0:T(8,128)S(1)} %bitcast.9, f32[6,128]{1,0:T(8,128)S(1)} %bitcast.10, f32[6,128]{1,0:T(8,128)S(1)} %bitcast.11, f32[24,128]{1,0:T(8,128)S(1)} %get-tuple-element.34.state_in, ...), custom_call_target="tpu_custom_call" | custom-call | flops 1000000 | bytes 15625 | tf_op jit(solution)/shard_map/last/pallas_call | solution.py:303
  (8 shorter events, 0.1 us)
Async XLA Ops:
  0.6 12.6 %copy-start.4 = (f32[768]{0:T(1024)S(1)}, f32[768]{0:T(1024)}, u32[]{:S(2)}) copy-start(f32[768]{0:T(1024)} %param.19) | copy-start | bytes 9220
  0.6 12.6 %copy-start = (f32[768]{0:T(1024)S(1)}, f32[768]{0:T(1024)}, u32[]{:S(2)}) copy-start(f32[768]{0:T(1024)} %param.15) | copy-start | bytes 9220
  0.7 12.7 %copy-start.1 = (f32[768]{0:T(1024)S(1)}, f32[768]{0:T(1024)}, u32[]{:S(2)}) copy-start(f32[768]{0:T(1024)} %param.16) | copy-start | bytes 9220
  0.7 12.7 %copy-start.2 = (f32[768]{0:T(1024)S(1)}, f32[768]{0:T(1024)}, u32[]{:S(2)}) copy-start(f32[768]{0:T(1024)} %param.17) | copy-start | bytes 9220
  0.7 12.7 %copy-start.3 = (f32[768]{0:T(1024)S(1)}, f32[768]{0:T(1024)}, u32[]{:S(2)}) copy-start(f32[768]{0:T(1024)} %param.18) | copy-start | bytes 9220
  6.0 15.1 %all-to-all-start = ((bf16[32,4,384]{2,1,0:T(4,128)(2,1)}), bf16[32,4,384]{2,1,0:T(4,128)(2,1)S(1)}, u32[]{:S(2)}, u32[]{:S(2)}) async-start(bf16[32,4,384]{2,1,0:T(4,128)(2,1)} %get-tuple-element.20), calls=%async_computation | async-start | bytes 196608 | tf_op jit(solution)/shard_map/all_to_all | solution.py:348
  22.6 11.4 %all-to-all-start.1 = ((bf16[32,4,384]{2,1,0:T(4,128)(2,1)}), bf16[32,4,384]{2,1,0:T(4,128)(2,1)S(1)}, u32[]{:S(2)}, u32[]{:S(2)}) async-start(bf16[32,4,384]{2,1,0:T(4,128)(2,1)} %get-tuple-element.27), calls=%async_computation.1 | async-start | bytes 196608 | tf_op jit(solution)/shard_map/all_to_all | solution.py:371
  35.4 10.4 %all-to-all-start.2 = ((bf16[32,4,384]{2,1,0:T(4,128)(2,1)}), bf16[32,4,384]{2,1,0:T(4,128)(2,1)S(1)}, u32[]{:S(2)}, u32[]{:S(2)}) async-start(bf16[32,4,384]{2,1,0:T(4,128)(2,1)} %get-tuple-element.30), calls=%async_computation.2 | async-start | bytes 196608 | tf_op jit(solution)/shard_map/all_to_all | solution.py:371

commit v5 on v4

--- a/solution.py
+++ b/solution.py
@@ -239,9 +239,9 @@
 
 def step_kernel(
     recv, fields, guess, state_in, rest, panels, gather, scatter, weights,
-    send, slip_out, state_out, total, sources, acc,
-    *, step_no, n_src, n_rcv, own_blocks, dups,
+    send, slip_out, state_out, *refs, step_no, n_src, n_rcv, own_blocks, dups, later,
 ):
+    rest_out, (total, sources, acc) = refs[:-3], refs[-3:]
     shear, normal = split_stress(*sum_messages(recv, total, own_blocks, n_src, n_rcv))
     slip_rate, next_state = friction_solve(
         shear, normal, step_no, guess[...], state_in[...], [fields[kind] for kind in range(4)]
@@ -251,12 +251,9 @@
     pack_messages(send, lambda first, count: acc[pl.ds(first, count), :], own_blocks, n_src, dups)
     slip_out[...] = slip_rate
     state_out[...] = next_state
-
-
-def later_kernel(slip_rate, rest, panels, gather, scatter, weights, rest_out, sources):
-    spread_sources(slip_rate[...], sources)
-    for at in range(rest_out.shape[0]):
-        rest_out[at] = rest[at + 1] + new_terms(at + 1, panels, sources, gather, scatter, weights)
+    for at in range(later):
+        terms = new_terms(at + 1, panels, sources, gather, scatter, weights)
+        rest_out[0][at] = rest[at + 1] + terms
 
 
 def last_kernel(
@@ -349,16 +346,18 @@
     for step_no in range(STEPS - 1):
         last = step_no == STEPS - 2
         dups = 1 if last else n_rcv
-        send, slip_rate, state = call(
+        later = STEPS - 2 - step_no
+        send, slip_rate, state, *rest_out = call(
             functools.partial(
-                step_kernel, step_no=step_no, dups=dups, n_src=n_src, n_rcv=n_rcv, own_blocks=own_blocks
+                step_kernel, step_no=step_no, dups=dups, later=later,
+                n_src=n_src, n_rcv=n_rcv, own_blocks=own_blocks,
             ),
             [vmem] * 9,
             [
                 shape(n_src * dups, *message, dtype=jnp.bfloat16),
                 shape(src_blocks // 2, LANES),
                 shape(src_blocks // 2, LANES),
-            ],
+            ] + [shape(later, recv_rows, LANES)] * bool(later),
             [
                 pltpu.VMEM((src_blocks, LANES), f32),
                 pltpu.VMEM((src_blocks, LANES), f32),
@@ -367,17 +366,9 @@
             "step", [recv, fields, guess, state, rest, recent, *tables], one_lag,
         )
         guess = slip_rate
+        rest = rest_out[0] if later else rest
         slips.append(slip_rate)
         recv = lax.all_to_all(send, "src" if last else ("src", "rcv"), 0, 0, tiled=True)
-        later = STEPS - 2 - step_no
-        if later:
-            rest, = call(
-                later_kernel,
-                [vmem] * 6,
-                [shape(later, recv_rows, LANES)],
-                [pltpu.VMEM((src_blocks, LANES), f32)],
-                "later", [slip_rate, rest, recent, *tables], later * one_lag,
-            )
 
     slip_rates, state = call(
         functools.partial(last_kernel, step_no=STEPS - 1, n_src=n_src),

time: 56.8 us -> 54.9 us (0.967)
  blocking collectives: 14.5 us -> 35.1 us
  waiting for transfers between devices: 16.6 us -> 2.16 us
  starting transfers between devices: 13.4 us -> 7.31 us
  Pallas kernels: 11 us -> 9.03 us
    all_to_all x1 -> x3, blocking collectives: 9 us -> 29.7 us  [per_device(): lax.all_to_all(send, 'src' if last else ('src', 'rcv'), 0, 0, tiled=True)]
    all_to_all x2 -> x0, waiting for transfers between devices: 14.4 us -> none  [per_device(): lax.all_to_all(send, 'src' if last else ('src', 'rcv'), 0, 0, tiled=True)]
    all_to_all x2 -> x0, starting transfers between devices: 6.11 us -> none  [per_device(): lax.all_to_all(send, 'src' if last else ('src', 'rcv'), 0, 0, tiled=True)]
    pallas_call x7 -> x5, Pallas kernels: 11 us -> 9.03 us  [call(): pl.pallas_call(body, in_specs=ins, out_specs=[vmem] * len(outs), out_shap...]
  transfers between devices with their start and end apart: 3 -> 1, of which waited for: 3 -> 1; matrix products, arithmetic and copies ran while one was open for 0% -> 0% of each run, Pallas kernels for 2% -> 0%
where the time goes in v5:
time: 54.9 us; the launch traced here: 54.5 us
  blocking collectives  35.1 us (64%)
  Pallas kernels  9.03 us (16%)
  starting transfers between devices  7.31 us (13%)
  waiting for transfers between devices  2.16 us (4%)
  between operations  0.77 us (1%)
    all_to_all x3, blocking collectives, per_device(): lax.all_to_all(send, 'src' if last else ('src', 'rcv'), 0, 0, tiled=True)  29.7 us
    pallas_call x5, Pallas kernels, call(): pl.pallas_call(body, in_specs=ins, out_specs=[vmem] * len(outs), out_shap...  9.03 us
    all_to_all x1, starting transfers between devices, per_device(): recv = lax.all_to_all(send, ('src', 'rcv'), 0, 0, tiled=True)  7.31 us
    all_gather x1, blocking collectives, per_device(): fields = lax.all_gather(jnp.stack(own_fields), 'rcv', axis=1, tiled=True)  5.47 us
    all_to_all x1, waiting for transfers between devices, per_device(): recv = lax.all_to_all(send, ('src', 'rcv'), 0, 0, tiled=True)  2.16 us
  transfers between devices with their start and end apart: 1, of which 1 were waited for; matrix products, arithmetic and copies ran while one was open for 0% of the time, Pallas kernels for 0%

profile of v5, /device:TPU:0, one launch (start us, length us, event | category | flops | bytes accessed | tf_op | source)
XLA Modules:
  0.0 54.5 jit_solution(2415118734581616325)
XLA Ops:
  0.6 0.0 copy-start.4
  0.6 0.0 copy-start
  0.7 0.0 copy-start.1
  0.7 0.0 copy-start.2
  0.7 0.0 copy-start.3
  0.7 5.2 %older.1 = (bf16[32,4,384]{2,1,0:T(4,128)(2,1)}, f32[3,96,128]{2,1,0:T(8,128)S(1)}, f32[24,128]{1,0:T(8,128)S(1)}, bf16[3,24,64,128]{3,2,1,0:T(8,128)(2,1)S(1)},...) custom-call(bf16[12,24,64,128]{3,2,1,0:T(8,128)(2,1)} %bitcast.12, ...), custom_call_target="tpu_custom_call" | custom-call | flops 188743680 | bytes 2949120 | tf_op jit(solution)/shard_map/older/pallas_call | solution.py:300
  5.9 7.3 %all-to-all-start = ((bf16[32,4,384]{2,1,0:T(4,128)(2,1)}), bf16[32,4,384]{2,1,0:T(4,128)(2,1)S(1)}, u32[]{:S(2)}, u32[]{:S(2)}) async-start(bf16[32,4,384]{2,1,0:T(4,128)(2,1)} %get-tuple-element.22), calls=%async_computation | async-start | bytes 196608 | tf_op jit(solution)/shard_map/all_to_all | solution.py:345
  13.3 0.0 copy-done.4
  13.3 0.0 copy-done
  13.3 0.0 copy-done.1
  13.3 0.0 copy-done.2
  13.3 0.0 copy-done.3
  13.4 5.5 %all_gather.3 = f32[5,24,128]{2,0,1:T(8,128)S(1)} all-gather(f32[5,6,128]{2,0,1:T(8,128)S(1)} %stack.3), channel_id=1, replica_groups=mesh['src'=8,'rcv'=4] {'rcv'}, dimensions={1}, use_global_device_ids=true | all-gather | bytes 76800 | tf_op jit(solution)/shard_map/all_gather | solution.py:310
  18.9 2.2 %all-to-all-done.recv = bf16[32,4,384]{2,1,0:T(4,128)(2,1)S(1)} async-done(((bf16[32,4,384]{2,1,0:T(4,128)(2,1)}), bf16[32,4,384]{2,1,0:T(4,128)(2,1)S(1)}, u32[]{:S(2)}, u32[]{:S(2)}) %all-to-all-start) | async-done | bytes 98336 | tf_op jit(solution)/shard_map/all_to_all | solution.py:345
  21.1 1.2 %step.3 = (bf16[32,4,384]{2,1,0:T(4,128)(2,1)S(1)}, f32[24,128]{1,0:T(8,128)S(1)}, f32[24,128]{1,0:T(8,128)S(1)}, f32[2,96,128]{2,1,0:T(8,128)S(1)}) custom-call(bf16[32,4,384]{2,1,0:T(4,128)(2,1)S(1)} %all-to-all-done.recv, f32[5,24,128]{2,1,0:T(8,128)S(1)} %copy.13.fields, f32[24,128]{1,0:T(8,128)S(1)} %get-tuple-element.23.guess, ...), custom_call_target="tpu_custom_call" | custom-call | flops 3145728 | bytes 49152 | tf_op jit(solution)/shard_map/step/pallas_call | solution.py:300
  22.3 11.2 %all_to_all.20.recv = bf16[32,4,384]{2,1,0:T(4,128)(2,1)S(1)} all-to-all(bf16[32,4,384]{2,1,0:T(4,128)(2,1)S(1)} %get-tuple-element.29), channel_id=1, replica_groups=mesh['src'=8,'rcv'=4] {'src','rcv'}, dimensions={0} | all-to-all | bytes 196608 | tf_op jit(solution)/shard_map/all_to_all | solution.py:371
  33.4 1.0 %step.4 = (bf16[32,4,384]{2,1,0:T(4,128)(2,1)S(1)}, f32[24,128]{1,0:T(8,128)S(1)}, f32[24,128]{1,0:T(8,128)S(1)}, f32[1,96,128]{2,1,0:T(8,128)S(1)}) custom-call(bf16[32,4,384]{2,1,0:T(4,128)(2,1)S(1)} %all_to_all.20.recv, f32[5,24,128]{2,1,0:T(8,128)S(1)} %copy.13.fields, f32[24,128]{1,0:T(8,128)S(1)} %get-tuple-element.30.guess.refs_0_, ...), custom_call_target="tpu_custom_call" | custom-call | flops 3145728 | bytes 49152 | tf_op jit(solution)/shard_map/step/pallas_call | solution.py:300
  34.4 9.5 %all_to_all.21.recv = bf16[32,4,384]{2,1,0:T(4,128)(2,1)S(1)} all-to-all(bf16[32,4,384]{2,1,0:T(4,128)(2,1)S(1)} %get-tuple-element.33), channel_id=1, replica_groups=mesh['src'=8,'rcv'=4] {'src','rcv'}, dimensions={0} | all-to-all | bytes 196608 | tf_op jit(solution)/shard_map/all_to_all | solution.py:371
  43.9 0.8 %step.5 = (bf16[8,4,384]{2,1,0:T(4,128)(2,1)S(1)}, f32[24,128]{1,0:T(8,128)S(1)}, f32[24,128]{1,0:T(8,128)S(1)}) custom-call(bf16[32,4,384]{2,1,0:T(4,128)(2,1)S(1)} %all_to_all.21.recv, f32[5,24,128]{2,1,0:T(8,128)S(1)} %copy.13.fields, f32[24,128]{1,0:T(8,128)S(1)} %get-tuple-element.34.guess.refs_1_, f32[24,128]{1,0:T(8,128)S(1)} %get-tuple-element.35.state_in, ...), custom_call_target="tpu_custom_call" | custom-call | flops 3145728 | bytes 49152 | tf_op jit(solution)/shard_map/step/pallas_call | solution.py:300
  44.7 9.0 %all_to_all.22.recv = bf16[8,4,384]{2,1,0:T(4,128)(2,1)S(1)} all-to-all(bf16[8,4,384]{2,1,0:T(4,128)(2,1)S(1)} %get-tuple-element.37), channel_id=1, replica_groups=mesh['src'=8,'rcv'=4] {'src'}, dimensions={0} | all-to-all | bytes 49152 | tf_op jit(solution)/shard_map/all_to_all | solution.py:371
  53.7 0.8 %last.1 = (f32[4,768]{1,0:T(4,128)}, f32[6,128]{1,0:T(8,128)}) custom-call(bf16[8,4,384]{2,1,0:T(4,128)(2,1)S(1)} %all_to_all.22.recv, f32[6,128]{1,0:T(8,128)S(1)} %bitcast.8, f32[6,128]{1,0:T(8,128)S(1)} %bitcast.9, f32[6,128]{1,0:T(8,128)S(1)} %bitcast.10, f32[6,128]{1,0:T(8,128)S(1)} %bitcast.11, f32[24,128]{1,0:T(8,128)S(1)} %get-tuple-element.38.state_in, ...), custom_call_target="tpu_custom_call" | custom-call | flops 1000000 | bytes 15625 | tf_op jit(solution)/shard_map/last/pallas_call | solution.py:300
  (8 shorter events, 0.1 us)
Async XLA Ops:
  0.6 12.6 %copy-start.4 = (f32[768]{0:T(1024)S(1)}, f32[768]{0:T(1024)}, u32[]{:S(2)}) copy-start(f32[768]{0:T(1024)} %param.19) | copy-start | bytes 9220
  0.6 12.6 %copy-start = (f32[768]{0:T(1024)S(1)}, f32[768]{0:T(1024)}, u32[]{:S(2)}) copy-start(f32[768]{0:T(1024)} %param.15) | copy-start | bytes 9220
  0.7 12.7 %copy-start.1 = (f32[768]{0:T(1024)S(1)}, f32[768]{0:T(1024)}, u32[]{:S(2)}) copy-start(f32[768]{0:T(1024)} %param.16) | copy-start | bytes 9220
  0.7 12.7 %copy-start.2 = (f32[768]{0:T(1024)S(1)}, f32[768]{0:T(1024)}, u32[]{:S(2)}) copy-start(f32[768]{0:T(1024)} %param.17) | copy-start | bytes 9220
  0.7 12.7 %copy-start.3 = (f32[768]{0:T(1024)S(1)}, f32[768]{0:T(1024)}, u32[]{:S(2)}) copy-start(f32[768]{0:T(1024)} %param.18) | copy-start | bytes 9220
  5.9 15.1 %all-to-all-start = ((bf16[32,4,384]{2,1,0:T(4,128)(2,1)}), bf16[32,4,384]{2,1,0:T(4,128)(2,1)S(1)}, u32[]{:S(2)}, u32[]{:S(2)}) async-start(bf16[32,4,384]{2,1,0:T(4,128)(2,1)} %get-tuple-element.22), calls=%async_computation | async-start | bytes 196608 | tf_op jit(solution)/shard_map/all_to_all | solution.py:345

commit v6 on v5

--- a/solution.py
+++ b/solution.py
@@ -119,8 +119,8 @@
 def older_kernel(
     panels, history, rows_in, cols_in, scales_in,
     send, rest, guess, recent, gather, scatter, weights,
-    panel_buf, history_buf, rows, cols, scales, rows_now, cols_now, scales_now, sources, acc,
-    sems, small_sems, out_sem,
+    panel_buf, history_buf, rows, cols, scales, rows_now, cols_now, scales_now, sources, acc, messages,
+    sems, small_sems, out_sems,
     *, lags, slots, n_src, n_rcv, own_blocks,
 ):
     src_blocks = n_rcv * own_blocks
@@ -154,8 +154,6 @@
             sources[base + lags:base + TAPS, :] = tail
     for copy in smalls[1:]:
         copy.wait()
-    make_tables(rows_now, cols_now, scales_now, gather, scatter, weights)
-
     top = lax.broadcasted_iota(jnp.int32, (8, LANES), 0) < STEPS
     match = top == (lax.broadcasted_iota(jnp.int32, (8, LANES), 1) < HALF)
     zero = jnp.zeros((8, LANES), jnp.float32)
@@ -192,20 +190,25 @@
         return carry
 
     lax.fori_loop(0, lags, one_lag, 0)
-    handed_on = pltpu.make_async_copy(panel_buf.at[recent_lags], recent, out_sem)
-    handed_on.start()
-
     def partials(first_row, count, step):
         low, high = [
             acc[pl.ds(first_row * 8 + start, count, stride=8), :] for start in (step, STEPS + step)
         ]
         return low + high
 
-    pack_messages(send, lambda first, count: partials(first, count, 0), own_blocks, n_src, n_rcv)
+    pack_messages(messages, lambda first, count: partials(first, count, 0), own_blocks, n_src, 1)
+    outgoing = [
+        pltpu.make_async_copy(messages, send.at[:, dup], out_sems.at[dup]) for dup in range(n_rcv)
+    ]
+    outgoing.append(pltpu.make_async_copy(panel_buf.at[recent_lags], recent, out_sems.at[n_rcv]))
+    for copy in outgoing:
+        copy.start()
+    make_tables(rows_now, cols_now, scales_now, gather, scatter, weights)
     for step in range(1, STEPS):
         rest[step - 1] = partials(0, recv_blocks, step)
     guess[...] = sources[pl.ds(LEAD + lags - 1, src_blocks // 2, stride=2 * TAPS), :]
-    handed_on.wait()
+    for copy in outgoing:
+        copy.wait()
 
 
 def spread_sources(slip_rate, sources):
@@ -296,9 +299,9 @@
     def shape(*dims, dtype=f32):
         return jax.ShapeDtypeStruct(dims, dtype)
 
-    def call(body, ins, outs, scratch, name, args, flops, limit=VMEM_LIMIT):
+    def call(body, ins, outs, scratch, name, args, flops, limit=VMEM_LIMIT, out_specs=None):
         return pl.pallas_call(
-            body, in_specs=ins, out_specs=[vmem] * len(outs), out_shape=outs, scratch_shapes=scratch,
+            body, in_specs=ins, out_specs=out_specs or [vmem] * len(outs), out_shape=outs, scratch_shapes=scratch,
             compiler_params=pltpu.CompilerParams(vmem_limit_bytes=limit), name=name,
             cost_estimate=pl.CostEstimate(flops=flops, bytes_accessed=flops // 64, transcendentals=0),
         )(*args)
@@ -318,7 +321,7 @@
         functools.partial(older_kernel, lags=lags, **sizes),
         [hbm] * 5,
         [
-            shape(n_src * n_rcv, *message, dtype=jnp.bfloat16),
+            shape(n_src, n_rcv, *message, dtype=jnp.bfloat16),
             shape(STEPS - 1, recv_rows, LANES),
             shape(src_blocks // 2, LANES),
             shape(STEPS - 1, slots, width, 2 * width, dtype=panels.dtype),
@@ -333,16 +336,18 @@
             *[pltpu.VMEM((STEPS - 1, *array.shape[1:]), array.dtype) for array in table],
             pltpu.VMEM((LEAD + src_blocks * TAPS, LANES), f32),
             pltpu.VMEM((recv_rows * 8, LANES), f32),
+            pltpu.VMEM((n_src, *message), jnp.bfloat16),
             pltpu.SemaphoreType.DMA((lags,)),
             pltpu.SemaphoreType.DMA((7,)),
-            pltpu.SemaphoreType.DMA,
+            pltpu.SemaphoreType.DMA((n_rcv + 1,)),
         ],
         "older", [panels, history, *table], 60 * one_lag, limit=32 * 1024 * 1024,
+        out_specs=[hbm] + [vmem] * 6,
     )
 
     state = fields[4]
     slips = []
-    recv = lax.all_to_all(send, ("src", "rcv"), 0, 0, tiled=True)
+    recv = lax.all_to_all(send.reshape(n_src * n_rcv, *message), ("src", "rcv"), 0, 0, tiled=True)
     for step_no in range(STEPS - 1):
         last = step_no == STEPS - 2
         dups = 1 if last else n_rcv

time: 54.9 us -> 54.4 us (level)
  no operation moved by 1% of the time
where the time goes in v6:
time: 54.4 us; the launch traced here: 54.1 us
  blocking collectives  35.1 us (65%)
  Pallas kernels  8.56 us (16%)
  starting transfers between devices  7.31 us (13%)
  waiting for transfers between devices  2.16 us (4%)
  between operations  0.77 us (1%)
    all_to_all x3, blocking collectives, per_device(): lax.all_to_all(send, 'src' if last else ('src', 'rcv'), 0, 0, tiled=True)  29.7 us
    pallas_call x5, Pallas kernels, call(): pl.pallas_call(body, in_specs=ins, out_specs=out_specs or [vmem] * len(ou...  8.56 us
    all_to_all x1, starting transfers between devices, per_device(): lax.all_to_all(send.reshape(n_src * n_rcv, *message), ('src', 'rcv'), 0,...  7.31 us
    all_gather x1, blocking collectives, per_device(): fields = lax.all_gather(jnp.stack(own_fields), 'rcv', axis=1, tiled=True)  5.47 us
    all_to_all x1, waiting for transfers between devices, per_device(): lax.all_to_all(send.reshape(n_src * n_rcv, *message), ('src', 'rcv'), 0,...  2.16 us
  transfers between devices with their start and end apart: 1, of which 1 were waited for; matrix products, arithmetic and copies ran while one was open for 0% of the time, Pallas kernels for 0%

profile of v6, /device:TPU:0, one launch (start us, length us, event | category | flops | bytes accessed | tf_op | source)
XLA Modules:
  0.0 54.1 jit_solution(16753259687714785867)
XLA Ops:
  0.6 0.0 copy-start.4
  0.6 0.0 copy-start
  0.7 0.0 copy-start.1
  0.7 0.0 copy-start.2
  0.7 0.0 copy-start.3
  0.7 4.8 %older.1 = (bf16[8,4,4,384]{3,2,1,0:T(4,128)(2,1)}, f32[3,96,128]{2,1,0:T(8,128)S(1)}, f32[24,128]{1,0:T(8,128)S(1)}, bf16[3,24,64,128]{3,2,1,0:T(8,128)(2,1)S(1...) custom-call(bf16[12,24,64,128]{3,2,1,0:T(8,128)(2,1)} %bitcast.13, ...), custom_call_target="tpu_custom_call" | custom-call | flops 188743680 | bytes 2949120 | tf_op jit(solution)/shard_map/older/pallas_call | solution.py:303
  5.5 7.3 %all-to-all-start = ((bf16[32,4,384]{2,1,0:T(4,128)(2,1)}), bf16[32,4,384]{2,1,0:T(4,128)(2,1)S(1)}, u32[]{:S(2)}, u32[]{:S(2)}) async-start(bf16[32,4,384]{2,1,0:T(4,128)(2,1)} %bitcast.1), calls=%async_computation | async-start | bytes 196608 | tf_op jit(solution)/shard_map/all_to_all | solution.py:350
  12.8 0.0 copy-done.4
  12.8 0.0 copy-done
  12.8 0.0 copy-done.1
  12.8 0.0 copy-done.2
  12.9 0.0 copy-done.3
  12.9 5.5 %all_gather.3 = f32[5,24,128]{2,0,1:T(8,128)S(1)} all-gather(f32[5,6,128]{2,0,1:T(8,128)S(1)} %stack.3), channel_id=1, replica_groups=mesh['src'=8,'rcv'=4] {'rcv'}, dimensions={1}, use_global_device_ids=true | all-gather | bytes 76800 | tf_op jit(solution)/shard_map/all_gather | solution.py:313
  18.4 2.2 %all-to-all-done.recv = bf16[32,4,384]{2,1,0:T(4,128)(2,1)S(1)} async-done(((bf16[32,4,384]{2,1,0:T(4,128)(2,1)}), bf16[32,4,384]{2,1,0:T(4,128)(2,1)S(1)}, u32[]{:S(2)}, u32[]{:S(2)}) %all-to-all-start) | async-done | bytes 98336 | tf_op jit(solution)/shard_map/all_to_all | solution.py:350
  20.6 1.2 %step.3 = (bf16[32,4,384]{2,1,0:T(4,128)(2,1)S(1)}, f32[24,128]{1,0:T(8,128)S(1)}, f32[24,128]{1,0:T(8,128)S(1)}, f32[2,96,128]{2,1,0:T(8,128)S(1)}) custom-call(bf16[32,4,384]{2,1,0:T(4,128)(2,1)S(1)} %all-to-all-done.recv, f32[5,24,128]{2,1,0:T(8,128)S(1)} %copy.13.fields, f32[24,128]{1,0:T(8,128)S(1)} %get-tuple-element.23.guess, ...), custom_call_target="tpu_custom_call" | custom-call | flops 3145728 | bytes 49152 | tf_op jit(solution)/shard_map/step/pallas_call | solution.py:303
  21.8 11.2 %all_to_all.20.recv = bf16[32,4,384]{2,1,0:T(4,128)(2,1)S(1)} all-to-all(bf16[32,4,384]{2,1,0:T(4,128)(2,1)S(1)} %get-tuple-element.29), channel_id=1, replica_groups=mesh['src'=8,'rcv'=4] {'src','rcv'}, dimensions={0} | all-to-all | bytes 196608 | tf_op jit(solution)/shard_map/all_to_all | solution.py:376
  32.9 1.0 %step.4 = (bf16[32,4,384]{2,1,0:T(4,128)(2,1)S(1)}, f32[24,128]{1,0:T(8,128)S(1)}, f32[24,128]{1,0:T(8,128)S(1)}, f32[1,96,128]{2,1,0:T(8,128)S(1)}) custom-call(bf16[32,4,384]{2,1,0:T(4,128)(2,1)S(1)} %all_to_all.20.recv, f32[5,24,128]{2,1,0:T(8,128)S(1)} %copy.13.fields, f32[24,128]{1,0:T(8,128)S(1)} %get-tuple-element.30.guess.refs_0_, ...), custom_call_target="tpu_custom_call" | custom-call | flops 3145728 | bytes 49152 | tf_op jit(solution)/shard_map/step/pallas_call | solution.py:303
  33.9 9.5 %all_to_all.21.recv = bf16[32,4,384]{2,1,0:T(4,128)(2,1)S(1)} all-to-all(bf16[32,4,384]{2,1,0:T(4,128)(2,1)S(1)} %get-tuple-element.33), channel_id=1, replica_groups=mesh['src'=8,'rcv'=4] {'src','rcv'}, dimensions={0} | all-to-all | bytes 196608 | tf_op jit(solution)/shard_map/all_to_all | solution.py:376
  43.4 0.8 %step.5 = (bf16[8,4,384]{2,1,0:T(4,128)(2,1)S(1)}, f32[24,128]{1,0:T(8,128)S(1)}, f32[24,128]{1,0:T(8,128)S(1)}) custom-call(bf16[32,4,384]{2,1,0:T(4,128)(2,1)S(1)} %all_to_all.21.recv, f32[5,24,128]{2,1,0:T(8,128)S(1)} %copy.13.fields, f32[24,128]{1,0:T(8,128)S(1)} %get-tuple-element.34.guess.refs_1_, f32[24,128]{1,0:T(8,128)S(1)} %get-tuple-element.35.state_in, ...), custom_call_target="tpu_custom_call" | custom-call | flops 3145728 | bytes 49152 | tf_op jit(solution)/shard_map/step/pallas_call | solution.py:303
  44.2 9.0 %all_to_all.22.recv = bf16[8,4,384]{2,1,0:T(4,128)(2,1)S(1)} all-to-all(bf16[8,4,384]{2,1,0:T(4,128)(2,1)S(1)} %get-tuple-element.37), channel_id=1, replica_groups=mesh['src'=8,'rcv'=4] {'src'}, dimensions={0} | all-to-all | bytes 49152 | tf_op jit(solution)/shard_map/all_to_all | solution.py:376
  53.2 0.8 %last.1 = (f32[4,768]{1,0:T(4,128)}, f32[6,128]{1,0:T(8,128)}) custom-call(bf16[8,4,384]{2,1,0:T(4,128)(2,1)S(1)} %all_to_all.22.recv, f32[6,128]{1,0:T(8,128)S(1)} %bitcast.9, f32[6,128]{1,0:T(8,128)S(1)} %bitcast.10, f32[6,128]{1,0:T(8,128)S(1)} %bitcast.11, f32[6,128]{1,0:T(8,128)S(1)} %bitcast.12, f32[24,128]{1,0:T(8,128)S(1)} %get-tuple-element.38.state_in, ...), custom_call_target="tpu_custom_call" | custom-call | flops 1000000 | bytes 15625 | tf_op jit(solution)/shard_map/last/pallas_call | solution.py:303
  (8 shorter events, 0.1 us)
Async XLA Ops:
  0.6 12.1 %copy-start.4 = (f32[768]{0:T(1024)S(1)}, f32[768]{0:T(1024)}, u32[]{:S(2)}) copy-start(f32[768]{0:T(1024)} %param.19) | copy-start | bytes 9220
  0.6 12.2 %copy-start = (f32[768]{0:T(1024)S(1)}, f32[768]{0:T(1024)}, u32[]{:S(2)}) copy-start(f32[768]{0:T(1024)} %param.15) | copy-start | bytes 9220
  0.7 12.2 %copy-start.1 = (f32[768]{0:T(1024)S(1)}, f32[768]{0:T(1024)}, u32[]{:S(2)}) copy-start(f32[768]{0:T(1024)} %param.16) | copy-start | bytes 9220
  0.7 12.2 %copy-start.2 = (f32[768]{0:T(1024)S(1)}, f32[768]{0:T(1024)}, u32[]{:S(2)}) copy-start(f32[768]{0:T(1024)} %param.17) | copy-start | bytes 9220
  0.7 12.2 %copy-start.3 = (f32[768]{0:T(1024)S(1)}, f32[768]{0:T(1024)}, u32[]{:S(2)}) copy-start(f32[768]{0:T(1024)} %param.18) | copy-start | bytes 9220
  5.5 15.1 %all-to-all-start = ((bf16[32,4,384]{2,1,0:T(4,128)(2,1)}), bf16[32,4,384]{2,1,0:T(4,128)(2,1)S(1)}, u32[]{:S(2)}, u32[]{:S(2)}) async-start(bf16[32,4,384]{2,1,0:T(4,128)(2,1)} %bitcast.1), calls=%async_computation | async-start | bytes 196608 | tf_op jit(solution)/shard_map/all_to_all | solution.py:350

commit v7 on v6

--- a/solution.py
+++ b/solution.py
@@ -111,8 +111,8 @@
             row_ids = jnp.where(at, pltpu.roll(widened(rows[lag, 0]), part * SLOT_ROWS, 1), row_ids)
         row_ids = jnp.where(one_row < PARTS * SLOT_ROWS, row_ids, -1.0)
         scatter[lag] = (block == row_ids).astype(jnp.float32).astype(jnp.bfloat16)
-        picks = column(widened(cols[lag, 0])) == lane.astype(jnp.float32)
-        gather[lag] = picks.astype(jnp.float32).astype(jnp.bfloat16)
+        picks = jnp.maximum(column(widened(cols[lag, 0])), 0.0).astype(jnp.int32)
+        gather[lag] = jnp.broadcast_to(picks, gather.shape[1:])
         weights[lag] = jnp.broadcast_to(column(widened(scales[lag, 0])), weights.shape[1:])
 
 
@@ -219,25 +219,47 @@
     sources[pl.ds(1, pairs, stride=2), :] = jnp.where(low, turned, slip_rate)
 
 
-def new_terms(lag, panels, sources, gather, scatter, weights):
+def take_rows(groups, rows):
+    taken = []
+    for first in range(0, rows.shape[0], 8):
+        row = rows[first:first + 8]
+        within = row & 7
+        block = row - within
+        piece = jnp.zeros(groups[0].shape, jnp.float32)
+        for at, group in enumerate(groups):
+            found = jnp.take_along_axis(group, within, axis=0, mode="promise_in_bounds")
+            piece = jnp.where(block == 8 * at, found, piece)
+        taken.append(piece)
+    return jnp.concatenate(taken, axis=0)
+
+
+def new_terms(lags, panels, sources, gather, scatter, weights):
     slots, width, wide = panels.shape[1:]
-    rounded = sources[...].astype(jnp.bfloat16)
-    picked = jnp.dot(gather[lag][:, :rounded.shape[0]], rounded, preferred_element_type=jnp.float32)
-    lane = lax.broadcasted_iota(jnp.int32, picked.shape, 1)
-    row = lax.broadcasted_iota(jnp.int32, picked.shape, 0)
+    groups = [sources[at:at + 8, :] for at in range(0, sources.shape[0], 8)]
+    picked = [take_rows(groups, gather[lag]) for lag in lags]
+    lane = lax.broadcasted_iota(jnp.int32, picked[0].shape, 1)
+    row = lax.broadcasted_iota(jnp.int32, picked[0].shape, 0)
     first = row - jnp.where(lane < HALF, 0, 1)
-    tiles = [
-        jnp.where(first == slot, picked, 0.0).astype(jnp.bfloat16) for slot in range(0, slots, 2)
-    ]
-    panel = panels[lag].reshape(slots * width, wide)
-    terms = jnp.dot(jnp.concatenate(tiles, axis=1), panel, preferred_element_type=jnp.float32)
-    left = terms * weights[lag]
-    parts = []
-    for part in range(PARTS):
-        parts.append(left.astype(jnp.bfloat16))
-        left = left - parts[-1].astype(jnp.float32)
-    stacked = jnp.concatenate(parts, axis=0)
-    return jnp.dot(scatter[lag][:, :stacked.shape[0]], stacked, preferred_element_type=jnp.float32)
+    terms = []
+    for lag, rates in zip(lags, picked):
+        tiles = [
+            jnp.where(first == slot, rates, 0.0).astype(jnp.bfloat16) for slot in range(0, slots, 2)
+        ]
+        panel = panels[lag].reshape(slots * width, wide)
+        terms.append(
+            jnp.dot(jnp.concatenate(tiles, axis=1), panel, preferred_element_type=jnp.float32)
+        )
+    sums = []
+    for lag, left in zip(lags, terms):
+        left = left * weights[lag]
+        parts = []
+        for part in range(PARTS):
+            parts.append(left.astype(jnp.bfloat16))
+            left = left - parts[-1].astype(jnp.float32)
+        stacked = jnp.concatenate(parts, axis=0)
+        table = scatter[lag][:, :stacked.shape[0]]
+        sums.append(jnp.dot(table, stacked, preferred_element_type=jnp.float32))
+    return sums
 
 
 def step_kernel(
@@ -250,13 +272,13 @@
         shear, normal, step_no, guess[...], state_in[...], [fields[kind] for kind in range(4)]
     )
     spread_sources(slip_rate, sources)
-    acc[...] = rest[0] + new_terms(0, panels, sources, gather, scatter, weights)
+    terms = new_terms(range(later + 1), panels, sources, gather, scatter, weights)
+    acc[...] = rest[0] + terms[0]
     pack_messages(send, lambda first, count: acc[pl.ds(first, count), :], own_blocks, n_src, dups)
     slip_out[...] = slip_rate
     state_out[...] = next_state
     for at in range(later):
-        terms = new_terms(at + 1, panels, sources, gather, scatter, weights)
-        rest_out[0][at] = rest[at + 1] + terms
+        rest_out[0][at] = rest[at + 1] + terms[at + 1]
 
 
 def last_kernel(
@@ -325,7 +347,7 @@
             shape(STEPS - 1, recv_rows, LANES),
             shape(src_blocks // 2, LANES),
             shape(STEPS - 1, slots, width, 2 * width, dtype=panels.dtype),
-            shape(STEPS - 1, SLOT_ROWS, LANES, dtype=jnp.bfloat16),
+            shape(STEPS - 1, SLOT_ROWS, LANES, dtype=jnp.int32),
             shape(STEPS - 1, recv_rows, LANES, dtype=jnp.bfloat16),
             shape(STEPS - 1, SLOT_ROWS, LANES),
         ],

time: 54.4 us -> 53.6 us (0.985)
  Pallas kernels: 8.56 us -> 7.8 us
    pallas_call x5, Pallas kernels: 8.56 us -> 7.8 us  [call(): pl.pallas_call(body, in_specs=ins, out_specs=out_specs or [vmem] * len(ou...]
where the time goes in v7:
time: 53.6 us; the launch traced here: 53.3 us
  blocking collectives  35.1 us (65%)
  Pallas kernels  7.8 us (15%)
  starting transfers between devices  7.31 us (14%)
  waiting for transfers between devices  2.16 us (4%)
  between operations  0.77 us (1%)
    all_to_all x3, blocking collectives, per_device(): lax.all_to_all(send, 'src' if last else ('src', 'rcv'), 0, 0, tiled=True)  29.7 us
    pallas_call x5, Pallas kernels, call(): pl.pallas_call(body, in_specs=ins, out_specs=out_specs or [vmem] * len(ou...  7.8 us
    all_to_all x1, starting transfers between devices, per_device(): lax.all_to_all(send.reshape(n_src * n_rcv, *message), ('src', 'rcv'), 0,...  7.31 us
    all_gather x1, blocking collectives, per_device(): fields = lax.all_gather(jnp.stack(own_fields), 'rcv', axis=1, tiled=True)  5.47 us
    all_to_all x1, waiting for transfers between devices, per_device(): lax.all_to_all(send.reshape(n_src * n_rcv, *message), ('src', 'rcv'), 0,...  2.16 us
  transfers between devices with their start and end apart: 1, of which 1 were waited for; matrix products, arithmetic and copies ran while one was open for 0% of the time, Pallas kernels for 0%

profile of v7, /device:TPU:0, one launch (start us, length us, event | category | flops | bytes accessed | tf_op | source)
XLA Modules:
  0.0 53.3 jit_solution(16524416701035918603)
XLA Ops:
  0.6 0.0 copy-start.4
  0.6 0.0 copy-start
  0.7 0.0 copy-start.1
  0.7 0.0 copy-start.2
  0.7 0.0 copy-start.3
  0.7 4.8 %older.1 = (bf16[8,4,4,384]{3,2,1,0:T(4,128)(2,1)}, f32[3,96,128]{2,1,0:T(8,128)S(1)}, f32[24,128]{1,0:T(8,128)S(1)}, bf16[3,24,64,128]{3,2,1,0:T(8,128)(2,1)S(1...) custom-call(bf16[12,24,64,128]{3,2,1,0:T(8,128)(2,1)} %bitcast.13, ...), custom_call_target="tpu_custom_call" | custom-call | flops 188743680 | bytes 2949120 | tf_op jit(solution)/shard_map/older/pallas_call | solution.py:325
  5.5 7.3 %all-to-all-start = ((bf16[32,4,384]{2,1,0:T(4,128)(2,1)}), bf16[32,4,384]{2,1,0:T(4,128)(2,1)S(1)}, u32[]{:S(2)}, u32[]{:S(2)}) async-start(bf16[32,4,384]{2,1,0:T(4,128)(2,1)} %bitcast.1), calls=%async_computation | async-start | bytes 196608 | tf_op jit(solution)/shard_map/all_to_all | solution.py:372
  12.8 0.0 copy-done.4
  12.8 0.0 copy-done
  12.8 0.0 copy-done.1
  12.8 0.0 copy-done.2
  12.9 0.0 copy-done.3
  12.9 5.5 %all_gather.3 = f32[5,24,128]{2,0,1:T(8,128)S(1)} all-gather(f32[5,6,128]{2,0,1:T(8,128)S(1)} %stack.3), channel_id=1, replica_groups=mesh['src'=8,'rcv'=4] {'rcv'}, dimensions={1}, use_global_device_ids=true | all-gather | bytes 76800 | tf_op jit(solution)/shard_map/all_gather | solution.py:335
  18.4 2.2 %all-to-all-done.recv = bf16[32,4,384]{2,1,0:T(4,128)(2,1)S(1)} async-done(((bf16[32,4,384]{2,1,0:T(4,128)(2,1)}), bf16[32,4,384]{2,1,0:T(4,128)(2,1)S(1)}, u32[]{:S(2)}, u32[]{:S(2)}) %all-to-all-start) | async-done | bytes 98336 | tf_op jit(solution)/shard_map/all_to_all | solution.py:372
  20.6 0.8 %step.3 = (bf16[32,4,384]{2,1,0:T(4,128)(2,1)S(1)}, f32[24,128]{1,0:T(8,128)S(1)}, f32[24,128]{1,0:T(8,128)S(1)}, f32[2,96,128]{2,1,0:T(8,128)S(1)}) custom-call(bf16[32,4,384]{2,1,0:T(4,128)(2,1)S(1)} %all-to-all-done.recv, f32[5,24,128]{2,1,0:T(8,128)S(1)} %copy.13.fields, f32[24,128]{1,0:T(8,128)S(1)} %get-tuple-element.23.guess, ...), custom_call_target="tpu_custom_call" | custom-call | flops 3145728 | bytes 49152 | tf_op jit(solution)/shard_map/step/pallas_call | solution.py:325
  21.4 11.2 %all_to_all.20.recv = bf16[32,4,384]{2,1,0:T(4,128)(2,1)S(1)} all-to-all(bf16[32,4,384]{2,1,0:T(4,128)(2,1)S(1)} %get-tuple-element.29), channel_id=1, replica_groups=mesh['src'=8,'rcv'=4] {'src','rcv'}, dimensions={0} | all-to-all | bytes 196608 | tf_op jit(solution)/shard_map/all_to_all | solution.py:398
  32.5 0.7 %step.4 = (bf16[32,4,384]{2,1,0:T(4,128)(2,1)S(1)}, f32[24,128]{1,0:T(8,128)S(1)}, f32[24,128]{1,0:T(8,128)S(1)}, f32[1,96,128]{2,1,0:T(8,128)S(1)}) custom-call(bf16[32,4,384]{2,1,0:T(4,128)(2,1)S(1)} %all_to_all.20.recv, f32[5,24,128]{2,1,0:T(8,128)S(1)} %copy.13.fields, f32[24,128]{1,0:T(8,128)S(1)} %get-tuple-element.30.guess.refs_0_, ...), custom_call_target="tpu_custom_call" | custom-call | flops 3145728 | bytes 49152 | tf_op jit(solution)/shard_map/step/pallas_call | solution.py:325
  33.3 9.5 %all_to_all.21.recv = bf16[32,4,384]{2,1,0:T(4,128)(2,1)S(1)} all-to-all(bf16[32,4,384]{2,1,0:T(4,128)(2,1)S(1)} %get-tuple-element.33), channel_id=1, replica_groups=mesh['src'=8,'rcv'=4] {'src','rcv'}, dimensions={0} | all-to-all | bytes 196608 | tf_op jit(solution)/shard_map/all_to_all | solution.py:398
  42.8 0.7 %step.5 = (bf16[8,4,384]{2,1,0:T(4,128)(2,1)S(1)}, f32[24,128]{1,0:T(8,128)S(1)}, f32[24,128]{1,0:T(8,128)S(1)}) custom-call(bf16[32,4,384]{2,1,0:T(4,128)(2,1)S(1)} %all_to_all.21.recv, f32[5,24,128]{2,1,0:T(8,128)S(1)} %copy.13.fields, f32[24,128]{1,0:T(8,128)S(1)} %get-tuple-element.34.guess.refs_1_, f32[24,128]{1,0:T(8,128)S(1)} %get-tuple-element.35.state_in, ...), custom_call_target="tpu_custom_call" | custom-call | flops 3145728 | bytes 49152 | tf_op jit(solution)/shard_map/step/pallas_call | solution.py:325
  43.5 9.0 %all_to_all.22.recv = bf16[8,4,384]{2,1,0:T(4,128)(2,1)S(1)} all-to-all(bf16[8,4,384]{2,1,0:T(4,128)(2,1)S(1)} %get-tuple-element.37), channel_id=1, replica_groups=mesh['src'=8,'rcv'=4] {'src'}, dimensions={0} | all-to-all | bytes 49152 | tf_op jit(solution)/shard_map/all_to_all | solution.py:398
  52.5 0.8 %last.1 = (f32[4,768]{1,0:T(4,128)}, f32[6,128]{1,0:T(8,128)}) custom-call(bf16[8,4,384]{2,1,0:T(4,128)(2,1)S(1)} %all_to_all.22.recv, f32[6,128]{1,0:T(8,128)S(1)} %bitcast.9, f32[6,128]{1,0:T(8,128)S(1)} %bitcast.10, f32[6,128]{1,0:T(8,128)S(1)} %bitcast.11, f32[6,128]{1,0:T(8,128)S(1)} %bitcast.12, f32[24,128]{1,0:T(8,128)S(1)} %get-tuple-element.38.state_in, ...), custom_call_target="tpu_custom_call" | custom-call | flops 1000000 | bytes 15625 | tf_op jit(solution)/shard_map/last/pallas_call | solution.py:325
  (8 shorter events, 0.1 us)
Async XLA Ops:
  0.6 12.1 %copy-start.4 = (f32[768]{0:T(1024)S(1)}, f32[768]{0:T(1024)}, u32[]{:S(2)}) copy-start(f32[768]{0:T(1024)} %param.19) | copy-start | bytes 9220
  0.6 12.2 %copy-start = (f32[768]{0:T(1024)S(1)}, f32[768]{0:T(1024)}, u32[]{:S(2)}) copy-start(f32[768]{0:T(1024)} %param.15) | copy-start | bytes 9220
  0.7 12.2 %copy-start.1 = (f32[768]{0:T(1024)S(1)}, f32[768]{0:T(1024)}, u32[]{:S(2)}) copy-start(f32[768]{0:T(1024)} %param.16) | copy-start | bytes 9220
  0.7 12.2 %copy-start.2 = (f32[768]{0:T(1024)S(1)}, f32[768]{0:T(1024)}, u32[]{:S(2)}) copy-start(f32[768]{0:T(1024)} %param.17) | copy-start | bytes 9220
  0.7 12.2 %copy-start.3 = (f32[768]{0:T(1024)S(1)}, f32[768]{0:T(1024)}, u32[]{:S(2)}) copy-start(f32[768]{0:T(1024)} %param.18) | copy-start | bytes 9220
  5.5 15.1 %all-to-all-start = ((bf16[32,4,384]{2,1,0:T(4,128)(2,1)}), bf16[32,4,384]{2,1,0:T(4,128)(2,1)S(1)}, u32[]{:S(2)}, u32[]{:S(2)}) async-start(bf16[32,4,384]{2,1,0:T(4,128)(2,1)} %bitcast.1), calls=%async_computation | async-start | bytes 196608 | tf_op jit(solution)/shard_map/all_to_all | solution.py:372

commit v8 on v7

--- a/solution.py
+++ b/solution.py
@@ -117,12 +117,15 @@
 
 
 def older_kernel(
-    panels, history, rows_in, cols_in, scales_in,
-    send, rest, guess, recent, gather, scatter, weights,
-    panel_buf, history_buf, rows, cols, scales, rows_now, cols_now, scales_now, sources, acc, messages,
-    sems, small_sems, out_sems,
-    *, lags, slots, n_src, n_rcv, own_blocks,
+    panels, history, rows_in, cols_in, scales_in, *refs,
+    lags, slots, n_src, n_rcv, own_blocks, n_fields,
 ):
+    own_fields, refs = refs[:n_fields], refs[n_fields:]
+    send, rest, guess, recent, gather, scatter, weights, fields, *refs = refs
+    (
+        panel_buf, history_buf, rows, cols, scales, rows_now, cols_now, scales_now, sources, acc, messages,
+        sems, small_sems, out_sems,
+    ) = refs
     src_blocks = n_rcv * own_blocks
     recv_blocks = n_src * own_blocks
     recent_lags = pl.ds(0, STEPS - 1)
@@ -132,6 +135,7 @@
             (history, history_buf), (cols_in, cols), (rows_in, rows), (scales_in, scales),
             (rows_in.at[recent_lags], rows_now), (cols_in.at[recent_lags], cols_now),
             (scales_in.at[recent_lags], scales_now),
+            *[(field, fields.at[at]) for at, field in enumerate(own_fields)],
         ])
     ]
 
@@ -152,7 +156,7 @@
             base = LEAD + (2 * pair + half) * TAPS
             sources[base:base + lags, :] = tile if half == 0 else pltpu.roll(tile, HALF, 1)
             sources[base + lags:base + TAPS, :] = tail
-    for copy in smalls[1:]:
+    for copy in smalls[1:7]:
         copy.wait()
     top = lax.broadcasted_iota(jnp.int32, (8, LANES), 0) < STEPS
     match = top == (lax.broadcasted_iota(jnp.int32, (8, LANES), 1) < HALF)
@@ -207,7 +211,7 @@
     for step in range(1, STEPS):
         rest[step - 1] = partials(0, recv_blocks, step)
     guess[...] = sources[pl.ds(LEAD + lags - 1, src_blocks // 2, stride=2 * TAPS), :]
-    for copy in outgoing:
+    for copy in outgoing + smalls[7:]:
         copy.wait()
 
 
@@ -262,10 +266,27 @@
     return sums
 
 
+def order_fields(parts, fields):
+    here = lax.axis_index("rcv")
+    pairs = parts[0].shape[1]
+    for owner in range(len(parts)):
+        chosen = parts[0][...]
+        for turn in range(1, len(parts)):
+            chosen = jnp.where(here ^ owner == turn, parts[turn][...], chosen)
+        for kind in range(fields.shape[0]):
+            fields[kind, owner * pairs:(owner + 1) * pairs, :] = chosen[kind]
+
+
 def step_kernel(
-    recv, fields, guess, state_in, rest, panels, gather, scatter, weights,
-    send, slip_out, state_out, *refs, step_no, n_src, n_rcv, own_blocks, dups, later,
+    recv, guess, rest, panels, gather, scatter, weights, *refs,
+    step_no, n_src, n_rcv, own_blocks, dups, later,
 ):
+    if step_no == 0:
+        parts, (send, slip_out, state_out, fields), refs = refs[:n_rcv], refs[n_rcv:n_rcv + 4], refs[n_rcv + 4:]
+        order_fields(parts, fields)
+        state_in = fields.at[4]
+    else:
+        (fields, state_in, send, slip_out, state_out), refs = refs[:5], refs[5:]
     rest_out, (total, sources, acc) = refs[:-3], refs[-3:]
     shear, normal = split_stress(*sum_messages(recv, total, own_blocks, n_src, n_rcv))
     slip_rate, next_state = friction_solve(
@@ -332,16 +353,16 @@
         field.reshape(pairs, LANES)
         for field in (shear_pre, sigma_pre, friction_a, state_rate, state_init)
     ]
-    fields = lax.all_gather(jnp.stack(own_fields), "rcv", axis=1, tiled=True)
+    own_hbm = [pltpu.with_memory_space_constraint(field, pltpu.HBM) for field in own_fields]
 
     panels, history, *table = [
         pltpu.with_memory_space_constraint(array, pltpu.HBM)
         for array in (panels, history, block_rows, block_cols, scales)
     ]
     one_lag = 2 * slots * width * 2 * width * 8
-    send, rest, guess, recent, *tables = call(
-        functools.partial(older_kernel, lags=lags, **sizes),
-        [hbm] * 5,
+    send, rest, guess, recent, *tables, mine = call(
+        functools.partial(older_kernel, lags=lags, n_fields=len(own_fields), **sizes),
+        [hbm] * (5 + len(own_fields)),
         [
             shape(n_src, n_rcv, *message, dtype=jnp.bfloat16),
             shape(STEPS - 1, recv_rows, LANES),
@@ -350,6 +371,7 @@
             shape(STEPS - 1, SLOT_ROWS, LANES, dtype=jnp.int32),
             shape(STEPS - 1, recv_rows, LANES, dtype=jnp.bfloat16),
             shape(STEPS - 1, SLOT_ROWS, LANES),
+            shape(len(own_fields), pairs, LANES),
         ],
         [
             pltpu.VMEM(panels.shape, panels.dtype),
@@ -360,40 +382,44 @@
             pltpu.VMEM((recv_rows * 8, LANES), f32),
             pltpu.VMEM((n_src, *message), jnp.bfloat16),
             pltpu.SemaphoreType.DMA((lags,)),
-            pltpu.SemaphoreType.DMA((7,)),
+            pltpu.SemaphoreType.DMA((7 + len(own_fields),)),
             pltpu.SemaphoreType.DMA((n_rcv + 1,)),
         ],
-        "older", [panels, history, *table], 60 * one_lag, limit=32 * 1024 * 1024,
-        out_specs=[hbm] + [vmem] * 6,
-    )
-
-    state = fields[4]
+        "older", [panels, history, *table, *own_hbm], 60 * one_lag, limit=32 * 1024 * 1024,
+        out_specs=[hbm] + [vmem] * 7,
+    )
+
+    parts = [mine] + [
+        lax.ppermute(mine, "rcv", [(at, at ^ turn) for at in range(n_rcv)]) for turn in range(1, n_rcv)
+    ]
     slips = []
     recv = lax.all_to_all(send.reshape(n_src * n_rcv, *message), ("src", "rcv"), 0, 0, tiled=True)
     for step_no in range(STEPS - 1):
         last = step_no == STEPS - 2
         dups = 1 if last else n_rcv
         later = STEPS - 2 - step_no
-        send, slip_rate, state, *rest_out = call(
+        first = step_no == 0
+        solve_inputs = parts if first else [fields, state]
+        packed = shape(src_blocks // 2, LANES)
+        send, slip_rate, state, *more = call(
             functools.partial(
                 step_kernel, step_no=step_no, dups=dups, later=later,
                 n_src=n_src, n_rcv=n_rcv, own_blocks=own_blocks,
             ),
-            [vmem] * 9,
-            [
-                shape(n_src * dups, *message, dtype=jnp.bfloat16),
-                shape(src_blocks // 2, LANES),
-                shape(src_blocks // 2, LANES),
-            ] + [shape(later, recv_rows, LANES)] * bool(later),
+            [vmem] * (7 + len(solve_inputs)),
+            [shape(n_src * dups, *message, dtype=jnp.bfloat16), packed, packed]
+            + [shape(len(own_fields), src_blocks // 2, LANES)] * first
+            + [shape(later, recv_rows, LANES)] * bool(later),
             [
                 pltpu.VMEM((src_blocks, LANES), f32),
                 pltpu.VMEM((src_blocks, LANES), f32),
                 pltpu.VMEM((recv_rows, LANES), f32),
             ],
-            "step", [recv, fields, guess, state, rest, recent, *tables], one_lag,
+            "step", [recv, guess, rest, recent, *tables, *solve_inputs], one_lag,
         )
+        fields = more.pop(0) if first else fields
         guess = slip_rate
-        rest = rest_out[0] if later else rest
+        rest = more[0] if later else rest
         slips.append(slip_rate)
         recv = lax.all_to_all(send, "src" if last else ("src", "rcv"), 0, 0, tiled=True)
 

time: 53.6 us -> 52.2 us (0.974)
  blocking collectives: 35.1 us -> 28.3 us
  waiting for transfers between devices: 2.16 us -> 5.84 us
  starting transfers between devices: 7.31 us -> 9.27 us
    all_gather x1 -> x0, blocking collectives: 5.47 us -> none  [per_device(): fields = lax.all_gather(jnp.stack(own_fields), 'rcv', axis=1, tiled=True)]
    ppermute x0 -> x3, waiting for transfers between devices: none -> 3.49 us  [per_device(): lax.ppermute(mine, 'rcv', [(at, at ^ turn) for at in range(n_rcv)])]
    ppermute x0 -> x3, starting transfers between devices: none -> 1.96 us  [per_device(): lax.ppermute(mine, 'rcv', [(at, at ^ turn) for at in range(n_rcv)])]
    all_to_all x3, blocking collectives: 29.7 us -> 28.3 us  [per_device(): lax.all_to_all(send, 'src' if last else ('src', 'rcv'), 0, 0, tiled=True)]
  transfers between devices with their start and end apart: 1 -> 4, of which waited for: 1 -> 3; matrix products, arithmetic and copies ran while one was open for 0% -> 0% of each run, Pallas kernels for 0% -> 0%
where the time goes in v8:
time: 52.2 us; the launch traced here: 51.9 us
  blocking collectives  28.3 us (54%)
  starting transfers between devices  9.27 us (18%)
  Pallas kernels  7.77 us (15%)
  waiting for transfers between devices  5.84 us (11%)
  between operations  0.71 us (1%)
    all_to_all x3, blocking collectives, per_device(): lax.all_to_all(send, 'src' if last else ('src', 'rcv'), 0, 0, tiled=True)  28.3 us
    pallas_call x5, Pallas kernels, call(): pl.pallas_call(body, in_specs=ins, out_specs=out_specs or [vmem] * len(ou...  7.77 us
    all_to_all x1, starting transfers between devices, per_device(): lax.all_to_all(send.reshape(n_src * n_rcv, *message), ('src', 'rcv'), 0,...  7.3 us
    ppermute x3, waiting for transfers between devices, per_device(): lax.ppermute(mine, 'rcv', [(at, at ^ turn) for at in range(n_rcv)])  3.49 us
    all_to_all x1, waiting for transfers between devices, per_device(): lax.all_to_all(send.reshape(n_src * n_rcv, *message), ('src', 'rcv'), 0,...  2.36 us
    ppermute x3, starting transfers between devices, per_device(): lax.ppermute(mine, 'rcv', [(at, at ^ turn) for at in range(n_rcv)])  1.96 us
  transfers between devices with their start and end apart: 4, of which 3 were waited for; matrix products, arithmetic and copies ran while one was open for 0% of the time, Pallas kernels for 0%

profile of v8, /device:TPU:0, one launch (start us, length us, event | category | flops | bytes accessed | tf_op | source)
XLA Modules:
  0.0 51.9 jit_solution(9620646784275363027)
XLA Ops:
  0.6 0.0 copy-start
  0.6 0.0 copy-start.1
  0.7 0.0 copy-start.2
  0.7 0.0 copy-start.3
  0.7 4.7 %older.1 = (bf16[8,4,4,384]{3,2,1,0:T(4,128)(2,1)}, f32[3,96,128]{2,1,0:T(8,128)S(1)}, f32[24,128]{1,0:T(8,128)S(1)}, bf16[3,24,64,128]{3,2,1,0:T(8,128)(2,1)S(1...) custom-call(bf16[12,24,64,128]{3,2,1,0:T(8,128)(2,1)} %bitcast.16, ...), custom_call_target="tpu_custom_call" | custom-call | flops 188743680 | bytes 2949120 | tf_op jit(solution)/shard_map/older/pallas_call | solution.py:346
  5.4 7.3 %all-to-all-start = ((bf16[32,4,384]{2,1,0:T(4,128)(2,1)}), bf16[32,4,384]{2,1,0:T(4,128)(2,1)S(1)}, u32[]{:S(2)}, u32[]{:S(2)}) async-start(bf16[32,4,384]{2,1,0:T(4,128)(2,1)} %bitcast.6), calls=%async_computation | async-start | bytes 196608 | tf_op jit(solution)/shard_map/all_to_all | solution.py:396
  12.7 1.6 %collective-permute-start.2 = (f32[5,6,128]{2,1,0:T(8,128)S(1)}, f32[5,6,128]{2,1,0:T(8,128)S(1)}, u32[]{:S(2)}, u32[]{:S(2)}) collective-permute-start(f32[5,6,128]{2,1,0:T(8,128)S(1)} %get-tuple-element.31.refs_0_), channel_id=1, source_target_pairs={{0,3},{1,2},{2,1},{3,0},{4,7},{5,6},{6,5},{7,4},{8,11},{9,10},{10,... | collective-permute-start | bytes 46088 | tf_op jit(solution)/shard_map/ppermute | solution.py:393
  14.3 0.4 collective-permute-start.1
  14.7 0.0 collective-permute-start
  14.7 1.3 %collective-permute-done.2.refs_3_ = f32[5,6,128]{2,1,0:T(8,128)S(1)} collective-permute-done((f32[5,6,128]{2,1,0:T(8,128)S(1)}, f32[5,6,128]{2,1,0:T(8,128)S(1)}, u32[]{:S(2)}, u32[]{:S(2)}) %collective-permute-start.2) | collective-permute-done | bytes 15392 | tf_op jit(solution)/shard_map/ppermute | solution.py:393
  16.0 2.2 %collective-permute-done.1.refs_2_ = f32[5,6,128]{2,1,0:T(8,128)S(1)} collective-permute-done((f32[5,6,128]{2,1,0:T(8,128)S(1)}, f32[5,6,128]{2,1,0:T(8,128)S(1)}, u32[]{:S(2)}, u32[]{:S(2)}) %collective-permute-start.1) | collective-permute-done | bytes 15392 | tf_op jit(solution)/shard_map/ppermute | solution.py:393
  18.2 0.0 collective-permute-done.refs_1_
  18.2 2.4 %all-to-all-done.recv = bf16[32,4,384]{2,1,0:T(4,128)(2,1)S(1)} async-done(((bf16[32,4,384]{2,1,0:T(4,128)(2,1)}), bf16[32,4,384]{2,1,0:T(4,128)(2,1)S(1)}, u32[]{:S(2)}, u32[]{:S(2)}) %all-to-all-start) | async-done | bytes 98336 | tf_op jit(solution)/shard_map/all_to_all | solution.py:396
  20.5 0.8 %step.3 = (bf16[32,4,384]{2,1,0:T(4,128)(2,1)S(1)}, f32[24,128]{1,0:T(8,128)S(1)}, f32[24,128]{1,0:T(8,128)S(1)}, f32[5,24,128]{2,1,0:T(8,128)S(1)}, f32[2,96,128]{2,1,0:T(8,128)S(1)}) custom-call(bf16[32,4,384]{2,1,0:T(4,128)(2,1)S(1)} %all-to-all-done.recv, f32[24,128]{1,0:T(8,128)S(1)} %get-tuple-element.25.guess, ...), custom_call_target="tpu_custom_call" | custom-call | flops 3145728 | bytes 49152 | tf_op jit(solution)/shard_map/step/pallas_call | solution.py:346
  21.3 9.8 %all_to_all.20.recv = bf16[32,4,384]{2,1,0:T(4,128)(2,1)S(1)} all-to-all(bf16[32,4,384]{2,1,0:T(4,128)(2,1)S(1)} %get-tuple-element.32), channel_id=1, replica_groups=mesh['src'=8,'rcv'=4] {'src','rcv'}, dimensions={0} | all-to-all | bytes 196608 | tf_op jit(solution)/shard_map/all_to_all | solution.py:424
  31.1 0.7 %step.4 = (bf16[32,4,384]{2,1,0:T(4,128)(2,1)S(1)}, f32[24,128]{1,0:T(8,128)S(1)}, f32[24,128]{1,0:T(8,128)S(1)}, f32[1,96,128]{2,1,0:T(8,128)S(1)}) custom-call(bf16[32,4,384]{2,1,0:T(4,128)(2,1)S(1)} %all_to_all.20.recv, f32[24,128]{1,0:T(8,128)S(1)} %get-tuple-element.33.guess.refs_0_, f32[2,96,128]{2,1,0:T(8,128)S(1)} %get-tuple-element.34.rest, ...), custom_call_target="tpu_custom_call" | custom-call | flops 3145728 | bytes 49152 | tf_op jit(solution)/shard_map/step/pallas_call | solution.py:346
  31.9 9.5 %all_to_all.21.recv = bf16[32,4,384]{2,1,0:T(4,128)(2,1)S(1)} all-to-all(bf16[32,4,384]{2,1,0:T(4,128)(2,1)S(1)} %get-tuple-element.37), channel_id=1, replica_groups=mesh['src'=8,'rcv'=4] {'src','rcv'}, dimensions={0} | all-to-all | bytes 196608 | tf_op jit(solution)/shard_map/all_to_all | solution.py:424
  41.4 0.7 %step.5 = (bf16[8,4,384]{2,1,0:T(4,128)(2,1)S(1)}, f32[24,128]{1,0:T(8,128)S(1)}, f32[24,128]{1,0:T(8,128)S(1)}) custom-call(bf16[32,4,384]{2,1,0:T(4,128)(2,1)S(1)} %all_to_all.21.recv, f32[24,128]{1,0:T(8,128)S(1)} %get-tuple-element.38.guess.refs_1_, f32[1,96,128]{2,1,0:T(8,128)S(1)} %get-tuple-element.39.rest, ...), custom_call_target="tpu_custom_call" | custom-call | flops 3145728 | bytes 49152 | tf_op jit(solution)/shard_map/step/pallas_call | solution.py:346
  42.1 9.0 %all_to_all.22.recv = bf16[8,4,384]{2,1,0:T(4,128)(2,1)S(1)} all-to-all(bf16[8,4,384]{2,1,0:T(4,128)(2,1)S(1)} %get-tuple-element.41), channel_id=1, replica_groups=mesh['src'=8,'rcv'=4] {'src'}, dimensions={0} | all-to-all | bytes 49152 | tf_op jit(solution)/shard_map/all_to_all | solution.py:424
  51.1 0.0 copy-done
  51.1 0.0 copy-done.1
  51.1 0.0 copy-done.2
  51.1 0.0 copy-done.3
  51.1 0.8 %last.1 = (f32[4,768]{1,0:T(4,128)}, f32[6,128]{1,0:T(8,128)}) custom-call(bf16[8,4,384]{2,1,0:T(4,128)(2,1)S(1)} %all_to_all.22.recv, f32[6,128]{1,0:T(8,128)S(1)} %bitcast.9, f32[6,128]{1,0:T(8,128)S(1)} %bitcast.11, f32[6,128]{1,0:T(8,128)S(1)} %bitcast.13, f32[6,128]{1,0:T(8,128)S(1)} %bitcast.15, f32[24,128]{1,0:T(8,128)S(1)} %get-tuple-element.42.state_in, ...), custom_call_target="tpu_custom_call" | custom-call | flops 1000000 | bytes 15625 | tf_op jit(solution)/shard_map/last/pallas_call | solution.py:346
Async XLA Ops:
  0.6 50.5 %copy-start = (f32[768]{0:T(1024)S(1)}, f32[768]{0:T(1024)}, u32[]{:S(2)}) copy-start(f32[768]{0:T(1024)} %param.15) | copy-start | bytes 9220
  0.6 50.5 %copy-start.1 = (f32[768]{0:T(1024)S(1)}, f32[768]{0:T(1024)}, u32[]{:S(2)}) copy-start(f32[768]{0:T(1024)} %param.16) | copy-start | bytes 9220
  0.7 50.5 %copy-start.2 = (f32[768]{0:T(1024)S(1)}, f32[768]{0:T(1024)}, u32[]{:S(2)}) copy-start(f32[768]{0:T(1024)} %param.17) | copy-start | bytes 9220
  0.7 50.4 %copy-start.3 = (f32[768]{0:T(1024)S(1)}, f32[768]{0:T(1024)}, u32[]{:S(2)}) copy-start(f32[768]{0:T(1024)} %param.18) | copy-start | bytes 9220
  5.4 15.1 %all-to-all-start = ((bf16[32,4,384]{2,1,0:T(4,128)(2,1)}), bf16[32,4,384]{2,1,0:T(4,128)(2,1)S(1)}, u32[]{:S(2)}, u32[]{:S(2)}) async-start(bf16[32,4,384]{2,1,0:T(4,128)(2,1)} %bitcast.6), calls=%async_computation | async-start | bytes 196608 | tf_op jit(solution)/shard_map/all_to_all | solution.py:396
  12.7 3.3 %collective-permute-start.2 = (f32[5,6,128]{2,1,0:T(8,128)S(1)}, f32[5,6,128]{2,1,0:T(8,128)S(1)}, u32[]{:S(2)}, u32[]{:S(2)}) collective-permute-start(f32[5,6,128]{2,1,0:T(8,128)S(1)} %get-tuple-element.31.refs_0_), channel_id=1, source_target_pairs={{0,3},{1,2},{2,1},{3,0},{4,7},{5,6},{6,5},{7,4},{8,11},{9,10},{10,... | collective-permute-start | bytes 46088 | tf_op jit(solution)/shard_map/ppermute | solution.py:393
  14.3 3.9 %collective-permute-start.1 = (f32[5,6,128]{2,1,0:T(8,128)S(1)}, f32[5,6,128]{2,1,0:T(8,128)S(1)}, u32[]{:S(2)}, u32[]{:S(2)}) collective-permute-start(f32[5,6,128]{2,1,0:T(8,128)S(1)} %get-tuple-element.31.refs_0_), channel_id=1, source_target_pairs={{0,2},{1,3},{2,0},{3,1},{4,6},{5,7},{6,4},{7,5},{8,10},{9,11},{10,... | collective-permute-start | bytes 46088 | tf_op jit(solution)/shard_map/ppermute | solution.py:393
  14.7 3.5 %collective-permute-start = (f32[5,6,128]{2,1,0:T(8,128)S(1)}, f32[5,6,128]{2,1,0:T(8,128)S(1)}, u32[]{:S(2)}, u32[]{:S(2)}) collective-permute-start(f32[5,6,128]{2,1,0:T(8,128)S(1)} %get-tuple-element.31.refs_0_), channel_id=1, source_target_pairs={{0,1},{1,0},{2,3},{3,2},{4,5},{5,4},{6,7},{7,6},{8,9},{9,8},{10,11... | collective-permute-start | bytes 46088 | tf_op jit(solution)/shard_map/ppermute | solution.py:393

commit v9 on v8

--- a/solution.py
+++ b/solution.py
@@ -15,7 +15,7 @@
 LANES = 128
 HALF = LANES // 2
 ROWS = 4
-IN_FLIGHT = 5
+IN_FLIGHT = 6
 GROUP = 4
 SLOT_ROWS = 32
 PARTS = 3
@@ -25,9 +25,8 @@
 VMEM_LIMIT = 16 * 1024 * 1024
 
 
-def inverse_sinh(value):
-    magnitude = jnp.abs(value)
-    result = jnp.log(magnitude + jnp.sqrt(1.0 + magnitude * magnitude))
+def inverse_sinh(value, root):
+    result = jnp.log(jnp.abs(value) + root)
     return jnp.where(value < 0.0, -result, result)
 
 
@@ -40,8 +39,9 @@
     slip_rate = guess
     for attempt in range(NEWTON_ITERS):
         scaled = slip_rate * factor
-        misfit = shear_total - DAMPING * slip_rate - strength * inverse_sinh(scaled)
-        derivative = -DAMPING - strength * factor / jnp.sqrt(1.0 + scaled * scaled)
+        root = jnp.sqrt(1.0 + scaled * scaled)
+        misfit = shear_total - DAMPING * slip_rate - strength * inverse_sinh(scaled, root)
+        derivative = -DAMPING - strength * factor / root
         slip_rate = slip_rate - misfit / derivative
     next_state = state_now + TIME_STEP * state_rate * jnp.tanh(
         jnp.exp(-state_now) - jnp.abs(slip_rate)
@@ -123,7 +123,7 @@
     own_fields, refs = refs[:n_fields], refs[n_fields:]
     send, rest, guess, recent, gather, scatter, weights, fields, *refs = refs
     (
-        panel_buf, history_buf, rows, cols, scales, rows_now, cols_now, scales_now, sources, acc, messages,
+        panel_buf, history_buf, rows, cols, scales, rows_now, cols_now, scales_now, sources, acc_low, acc_high, messages,
         sems, small_sems, out_sems,
     ) = refs
     src_blocks = n_rcv * own_blocks
@@ -146,7 +146,9 @@
         copy.start()
     for lag in range(IN_FLIGHT):
         panel_copy(lag).start()
-    acc[...] = jnp.zeros_like(acc)
+    accs = (acc_low, acc_high)
+    for acc in accs:
+        acc[...] = jnp.zeros_like(acc)
     tail = jnp.zeros((TAPS - lags, LANES), jnp.float32)
     sources[0:LEAD, :] = jnp.zeros((LEAD, LANES), jnp.float32)
     smalls[0].wait()
@@ -188,15 +190,16 @@
                 slot = group + 2 * pair
                 scale = jnp.where(top, scales[lag, 0, 0, slot], scales[lag, 0, 0, slot + 1])
                 term = terms[8 * pair:8 * pair + 8] * scale
-                for part, addend in enumerate([jnp.where(top, term, 0.0), jnp.where(top, 0.0, term)]):
+                for part, acc in enumerate(accs):
                     at = pl.ds(pl.multiple_of(rows[lag, 0, 0, slot + part] * 8, 8), 8)
-                    acc[at, :] = acc[at, :] + addend
+                    acc[at, :] = acc[at, :] + term
         return carry
 
     lax.fori_loop(0, lags, one_lag, 0)
     def partials(first_row, count, step):
         low, high = [
-            acc[pl.ds(first_row * 8 + start, count, stride=8), :] for start in (step, STEPS + step)
+            acc[pl.ds(first_row * 8 + part * STEPS + step, count, stride=8), :]
+            for part, acc in enumerate(accs)
         ]
         return low + high
 
@@ -379,6 +382,7 @@
             *[pltpu.SMEM(array.shape, array.dtype) for array in table],
             *[pltpu.VMEM((STEPS - 1, *array.shape[1:]), array.dtype) for array in table],
             pltpu.VMEM((LEAD + src_blocks * TAPS, LANES), f32),
+            pltpu.VMEM((recv_rows * 8, LANES), f32),
             pltpu.VMEM((recv_rows * 8, LANES), f32),
             pltpu.VMEM((n_src, *message), jnp.bfloat16),
             pltpu.SemaphoreType.DMA((lags,)),

time: 52.2 us -> 51.9 us (level)
  no operation moved by 1% of the time
where the time goes in v9:
time: 51.9 us; the launch traced here: 51.6 us
  blocking collectives  28.3 us (55%)
  starting transfers between devices  9.25 us (18%)
  Pallas kernels  7.43 us (14%)
  waiting for transfers between devices  5.84 us (11%)
  between operations  0.71 us (1%)
    all_to_all x3, blocking collectives, per_device(): lax.all_to_all(send, 'src' if last else ('src', 'rcv'), 0, 0, tiled=True)  28.3 us
    pallas_call x5, Pallas kernels, call(): pl.pallas_call(body, in_specs=ins, out_specs=out_specs or [vmem] * len(ou...  7.43 us
    all_to_all x1, starting transfers between devices, per_device(): lax.all_to_all(send.reshape(n_src * n_rcv, *message), ('src', 'rcv'), 0,...  7.29 us
    ppermute x3, waiting for transfers between devices, per_device(): lax.ppermute(mine, 'rcv', [(at, at ^ turn) for at in range(n_rcv)])  3.49 us
    all_to_all x1, waiting for transfers between devices, per_device(): lax.all_to_all(send.reshape(n_src * n_rcv, *message), ('src', 'rcv'), 0,...  2.36 us
    ppermute x3, starting transfers between devices, per_device(): lax.ppermute(mine, 'rcv', [(at, at ^ turn) for at in range(n_rcv)])  1.96 us
  transfers between devices with their start and end apart: 4, of which 3 were waited for; matrix products, arithmetic and copies ran while one was open for 0% of the time, Pallas kernels for 0%

profile of v9, /device:TPU:0, one launch (start us, length us, event | category | flops | bytes accessed | tf_op | source)
XLA Modules:
  0.0 51.6 jit_solution(15425605903467342312)
XLA Ops:
  0.6 0.0 copy-start
  0.6 0.0 copy-start.1
  0.7 0.0 copy-start.2
  0.7 0.0 copy-start.3
  0.7 4.4 %older.1 = (bf16[8,4,4,384]{3,2,1,0:T(4,128)(2,1)}, f32[3,96,128]{2,1,0:T(8,128)S(1)}, f32[24,128]{1,0:T(8,128)S(1)}, bf16[3,24,64,128]{3,2,1,0:T(8,128)(2,1)S(1...) custom-call(bf16[12,24,64,128]{3,2,1,0:T(8,128)(2,1)} %bitcast.16, ...), custom_call_target="tpu_custom_call" | custom-call | flops 188743680 | bytes 2949120 | tf_op jit(solution)/shard_map/older/pallas_call | solution.py:349
  5.1 7.3 %all-to-all-start = ((bf16[32,4,384]{2,1,0:T(4,128)(2,1)}), bf16[32,4,384]{2,1,0:T(4,128)(2,1)S(1)}, u32[]{:S(2)}, u32[]{:S(2)}) async-start(bf16[32,4,384]{2,1,0:T(4,128)(2,1)} %bitcast.6), calls=%async_computation | async-start | bytes 196608 | tf_op jit(solution)/shard_map/all_to_all | solution.py:400
  12.4 1.6 %collective-permute-start.2 = (f32[5,6,128]{2,1,0:T(8,128)S(1)}, f32[5,6,128]{2,1,0:T(8,128)S(1)}, u32[]{:S(2)}, u32[]{:S(2)}) collective-permute-start(f32[5,6,128]{2,1,0:T(8,128)S(1)} %get-tuple-element.31.refs_0_), channel_id=1, source_target_pairs={{0,3},{1,2},{2,1},{3,0},{4,7},{5,6},{6,5},{7,4},{8,11},{9,10},{10,... | collective-permute-start | bytes 46088 | tf_op jit(solution)/shard_map/ppermute | solution.py:397
  13.9 0.4 collective-permute-start.1
  14.3 0.0 collective-permute-start
  14.3 1.3 %collective-permute-done.2.refs_3_ = f32[5,6,128]{2,1,0:T(8,128)S(1)} collective-permute-done((f32[5,6,128]{2,1,0:T(8,128)S(1)}, f32[5,6,128]{2,1,0:T(8,128)S(1)}, u32[]{:S(2)}, u32[]{:S(2)}) %collective-permute-start.2) | collective-permute-done | bytes 15392 | tf_op jit(solution)/shard_map/ppermute | solution.py:397
  15.6 2.2 %collective-permute-done.1.refs_2_ = f32[5,6,128]{2,1,0:T(8,128)S(1)} collective-permute-done((f32[5,6,128]{2,1,0:T(8,128)S(1)}, f32[5,6,128]{2,1,0:T(8,128)S(1)}, u32[]{:S(2)}, u32[]{:S(2)}) %collective-permute-start.1) | collective-permute-done | bytes 15392 | tf_op jit(solution)/shard_map/ppermute | solution.py:397
  17.8 0.0 collective-permute-done.refs_1_
  17.8 2.4 %all-to-all-done.recv = bf16[32,4,384]{2,1,0:T(4,128)(2,1)S(1)} async-done(((bf16[32,4,384]{2,1,0:T(4,128)(2,1)}), bf16[32,4,384]{2,1,0:T(4,128)(2,1)S(1)}, u32[]{:S(2)}, u32[]{:S(2)}) %all-to-all-start) | async-done | bytes 98336 | tf_op jit(solution)/shard_map/all_to_all | solution.py:400
  20.2 0.8 %step.3 = (bf16[32,4,384]{2,1,0:T(4,128)(2,1)S(1)}, f32[24,128]{1,0:T(8,128)S(1)}, f32[24,128]{1,0:T(8,128)S(1)}, f32[5,24,128]{2,1,0:T(8,128)S(1)}, f32[2,96,128]{2,1,0:T(8,128)S(1)}) custom-call(bf16[32,4,384]{2,1,0:T(4,128)(2,1)S(1)} %all-to-all-done.recv, f32[24,128]{1,0:T(8,128)S(1)} %get-tuple-element.25.guess, ...), custom_call_target="tpu_custom_call" | custom-call | flops 3145728 | bytes 49152 | tf_op jit(solution)/shard_map/step/pallas_call | solution.py:349
  21.0 9.8 %all_to_all.20.recv = bf16[32,4,384]{2,1,0:T(4,128)(2,1)S(1)} all-to-all(bf16[32,4,384]{2,1,0:T(4,128)(2,1)S(1)} %get-tuple-element.32), channel_id=1, replica_groups=mesh['src'=8,'rcv'=4] {'src','rcv'}, dimensions={0} | all-to-all | bytes 196608 | tf_op jit(solution)/shard_map/all_to_all | solution.py:428
  30.8 0.7 %step.4 = (bf16[32,4,384]{2,1,0:T(4,128)(2,1)S(1)}, f32[24,128]{1,0:T(8,128)S(1)}, f32[24,128]{1,0:T(8,128)S(1)}, f32[1,96,128]{2,1,0:T(8,128)S(1)}) custom-call(bf16[32,4,384]{2,1,0:T(4,128)(2,1)S(1)} %all_to_all.20.recv, f32[24,128]{1,0:T(8,128)S(1)} %get-tuple-element.33.guess.refs_0_, f32[2,96,128]{2,1,0:T(8,128)S(1)} %get-tuple-element.34.rest, ...), custom_call_target="tpu_custom_call" | custom-call | flops 3145728 | bytes 49152 | tf_op jit(solution)/shard_map/step/pallas_call | solution.py:349
  31.5 9.5 %all_to_all.21.recv = bf16[32,4,384]{2,1,0:T(4,128)(2,1)S(1)} all-to-all(bf16[32,4,384]{2,1,0:T(4,128)(2,1)S(1)} %get-tuple-element.37), channel_id=1, replica_groups=mesh['src'=8,'rcv'=4] {'src','rcv'}, dimensions={0} | all-to-all | bytes 196608 | tf_op jit(solution)/shard_map/all_to_all | solution.py:428
  41.0 0.7 %step.5 = (bf16[8,4,384]{2,1,0:T(4,128)(2,1)S(1)}, f32[24,128]{1,0:T(8,128)S(1)}, f32[24,128]{1,0:T(8,128)S(1)}) custom-call(bf16[32,4,384]{2,1,0:T(4,128)(2,1)S(1)} %all_to_all.21.recv, f32[24,128]{1,0:T(8,128)S(1)} %get-tuple-element.38.guess.refs_1_, f32[1,96,128]{2,1,0:T(8,128)S(1)} %get-tuple-element.39.rest, ...), custom_call_target="tpu_custom_call" | custom-call | flops 3145728 | bytes 49152 | tf_op jit(solution)/shard_map/step/pallas_call | solution.py:349
  41.7 9.0 %all_to_all.22.recv = bf16[8,4,384]{2,1,0:T(4,128)(2,1)S(1)} all-to-all(bf16[8,4,384]{2,1,0:T(4,128)(2,1)S(1)} %get-tuple-element.41), channel_id=1, replica_groups=mesh['src'=8,'rcv'=4] {'src'}, dimensions={0} | all-to-all | bytes 49152 | tf_op jit(solution)/shard_map/all_to_all | solution.py:428
  50.7 0.0 copy-done
  50.7 0.0 copy-done.1
  50.7 0.0 copy-done.2
  50.8 0.0 copy-done.3
  50.8 0.8 %last.1 = (f32[4,768]{1,0:T(4,128)}, f32[6,128]{1,0:T(8,128)}) custom-call(bf16[8,4,384]{2,1,0:T(4,128)(2,1)S(1)} %all_to_all.22.recv, f32[6,128]{1,0:T(8,128)S(1)} %bitcast.9, f32[6,128]{1,0:T(8,128)S(1)} %bitcast.11, f32[6,128]{1,0:T(8,128)S(1)} %bitcast.13, f32[6,128]{1,0:T(8,128)S(1)} %bitcast.15, f32[24,128]{1,0:T(8,128)S(1)} %get-tuple-element.42.state_in, ...), custom_call_target="tpu_custom_call" | custom-call | flops 1000000 | bytes 15625 | tf_op jit(solution)/shard_map/last/pallas_call | solution.py:349
Async XLA Ops:
  0.6 50.1 %copy-start = (f32[768]{0:T(1024)S(1)}, f32[768]{0:T(1024)}, u32[]{:S(2)}) copy-start(f32[768]{0:T(1024)} %param.15) | copy-start | bytes 9220
  0.6 50.1 %copy-start.1 = (f32[768]{0:T(1024)S(1)}, f32[768]{0:T(1024)}, u32[]{:S(2)}) copy-start(f32[768]{0:T(1024)} %param.16) | copy-start | bytes 9220
  0.7 50.1 %copy-start.2 = (f32[768]{0:T(1024)S(1)}, f32[768]{0:T(1024)}, u32[]{:S(2)}) copy-start(f32[768]{0:T(1024)} %param.17) | copy-start | bytes 9220
  0.7 50.1 %copy-start.3 = (f32[768]{0:T(1024)S(1)}, f32[768]{0:T(1024)}, u32[]{:S(2)}) copy-start(f32[768]{0:T(1024)} %param.18) | copy-start | bytes 9220
  5.1 15.1 %all-to-all-start = ((bf16[32,4,384]{2,1,0:T(4,128)(2,1)}), bf16[32,4,384]{2,1,0:T(4,128)(2,1)S(1)}, u32[]{:S(2)}, u32[]{:S(2)}) async-start(bf16[32,4,384]{2,1,0:T(4,128)(2,1)} %bitcast.6), calls=%async_computation | async-start | bytes 196608 | tf_op jit(solution)/shard_map/all_to_all | solution.py:400
  12.4 3.3 %collective-permute-start.2 = (f32[5,6,128]{2,1,0:T(8,128)S(1)}, f32[5,6,128]{2,1,0:T(8,128)S(1)}, u32[]{:S(2)}, u32[]{:S(2)}) collective-permute-start(f32[5,6,128]{2,1,0:T(8,128)S(1)} %get-tuple-element.31.refs_0_), channel_id=1, source_target_pairs={{0,3},{1,2},{2,1},{3,0},{4,7},{5,6},{6,5},{7,4},{8,11},{9,10},{10,... | collective-permute-start | bytes 46088 | tf_op jit(solution)/shard_map/ppermute | solution.py:397
  13.9 3.9 %collective-permute-start.1 = (f32[5,6,128]{2,1,0:T(8,128)S(1)}, f32[5,6,128]{2,1,0:T(8,128)S(1)}, u32[]{:S(2)}, u32[]{:S(2)}) collective-permute-start(f32[5,6,128]{2,1,0:T(8,128)S(1)} %get-tuple-element.31.refs_0_), channel_id=1, source_target_pairs={{0,2},{1,3},{2,0},{3,1},{4,6},{5,7},{6,4},{7,5},{8,10},{9,11},{10,... | collective-permute-start | bytes 46088 | tf_op jit(solution)/shard_map/ppermute | solution.py:397
  14.3 3.5 %collective-permute-start = (f32[5,6,128]{2,1,0:T(8,128)S(1)}, f32[5,6,128]{2,1,0:T(8,128)S(1)}, u32[]{:S(2)}, u32[]{:S(2)}) collective-permute-start(f32[5,6,128]{2,1,0:T(8,128)S(1)} %get-tuple-element.31.refs_0_), channel_id=1, source_target_pairs={{0,1},{1,0},{2,3},{3,2},{4,5},{5,4},{6,7},{7,6},{8,9},{9,8},{10,11... | collective-permute-start | bytes 46088 | tf_op jit(solution)/shard_map/ppermute | solution.py:397

commit v10 on v9

--- a/solution.py
+++ b/solution.py
@@ -15,11 +15,12 @@
 LANES = 128
 HALF = LANES // 2
 ROWS = 4
-IN_FLIGHT = 6
+IN_FLIGHT = 8
 GROUP = 4
 SLOT_ROWS = 32
 PARTS = 3
-MESSAGE_SCALE = 2.0 ** 22
+MESSAGE_BITS = 22
+MESSAGE_SCALE = 2.0 ** MESSAGE_BITS
 TAPS = 24
 LEAD = 8
 VMEM_LIMIT = 16 * 1024 * 1024
@@ -58,21 +59,19 @@
 
 def encode(partial):
     scaled = partial * (1.0 / MESSAGE_SCALE)
-    return (scaled * scaled * scaled).astype(jnp.bfloat16)
+    return scaled * scaled * scaled
 
 
 def decode(message):
     cube = message.astype(jnp.float32)
-    magnitude = jnp.abs(cube)
-    root = jnp.exp2(jnp.log2(jnp.maximum(magnitude, 1e-38)) * (1.0 / 3.0)) * MESSAGE_SCALE
-    root = jnp.where(cube < 0.0, -root, root)
-    return jnp.where(magnitude > 0.0, root, 0.0)
+    root = jnp.exp2(jnp.log2(jnp.abs(cube)) * (1.0 / 3.0) + MESSAGE_BITS)
+    return jnp.where(cube < 0.0, -root, root)
 
 
 def pack_messages(send, partials, own_blocks, n_dest, dups):
     for dest in range(n_dest):
         for tile in range(own_blocks // ROWS):
-            piece = encode(partials(dest * own_blocks + tile * ROWS, ROWS))
+            piece = partials(dest * own_blocks + tile * ROWS, ROWS).astype(jnp.bfloat16)
             for dup in range(dups):
                 send[dest * dups + dup, :, tile * LANES:(tile + 1) * LANES] = piece
 
@@ -203,7 +202,7 @@
         ]
         return low + high
 
-    pack_messages(messages, lambda first, count: partials(first, count, 0), own_blocks, n_src, 1)
+    pack_messages(messages, lambda first, count: encode(partials(first, count, 0)), own_blocks, n_src, 1)
     outgoing = [
         pltpu.make_async_copy(messages, send.at[:, dup], out_sems.at[dup]) for dup in range(n_rcv)
     ]
@@ -297,7 +296,7 @@
     )
     spread_sources(slip_rate, sources)
     terms = new_terms(range(later + 1), panels, sources, gather, scatter, weights)
-    acc[...] = rest[0] + terms[0]
+    acc[...] = encode(rest[0] + terms[0])
     pack_messages(send, lambda first, count: acc[pl.ds(first, count), :], own_blocks, n_src, dups)
     slip_out[...] = slip_rate
     state_out[...] = next_state

time: 51.9 us -> 51.7 us (level)
  no operation moved by 1% of the time
where the time goes in v10:
time: 51.7 us; the launch traced here: 51.5 us
  blocking collectives  28.3 us (55%)
  starting transfers between devices  9.26 us (18%)
  Pallas kernels  7.32 us (14%)
  waiting for transfers between devices  5.84 us (11%)
  between operations  0.71 us (1%)
    all_to_all x3, blocking collectives, per_device(): lax.all_to_all(send, 'src' if last else ('src', 'rcv'), 0, 0, tiled=True)  28.3 us
    pallas_call x5, Pallas kernels, call(): pl.pallas_call(body, in_specs=ins, out_specs=out_specs or [vmem] * len(ou...  7.32 us
    all_to_all x1, starting transfers between devices, per_device(): lax.all_to_all(send.reshape(n_src * n_rcv, *message), ('src', 'rcv'), 0,...  7.29 us
    ppermute x3, waiting for transfers between devices, per_device(): lax.ppermute(mine, 'rcv', [(at, at ^ turn) for at in range(n_rcv)])  3.49 us
    all_to_all x1, waiting for transfers between devices, per_device(): lax.all_to_all(send.reshape(n_src * n_rcv, *message), ('src', 'rcv'), 0,...  2.36 us
    ppermute x3, starting transfers between devices, per_device(): lax.ppermute(mine, 'rcv', [(at, at ^ turn) for at in range(n_rcv)])  1.96 us
  transfers between devices with their start and end apart: 4, of which 3 were waited for; matrix products, arithmetic and copies ran while one was open for 0% of the time, Pallas kernels for 0%

profile of v10, /device:TPU:0, one launch (start us, length us, event | category | flops | bytes accessed | tf_op | source)
XLA Modules:
  0.0 51.5 jit_solution(3927080736045636494)
XLA Ops:
  0.6 0.0 copy-start
  0.6 0.0 copy-start.1
  0.7 0.0 copy-start.2
  0.7 0.0 copy-start.3
  0.7 4.4 %older.1 = (bf16[8,4,4,384]{3,2,1,0:T(4,128)(2,1)}, f32[3,96,128]{2,1,0:T(8,128)S(1)}, f32[24,128]{1,0:T(8,128)S(1)}, bf16[3,24,64,128]{3,2,1,0:T(8,128)(2,1)S(1...) custom-call(bf16[12,24,64,128]{3,2,1,0:T(8,128)(2,1)} %bitcast.16, ...), custom_call_target="tpu_custom_call" | custom-call | flops 188743680 | bytes 2949120 | tf_op jit(solution)/shard_map/older/pallas_call | solution.py:348
  5.0 7.3 %all-to-all-start = ((bf16[32,4,384]{2,1,0:T(4,128)(2,1)}), bf16[32,4,384]{2,1,0:T(4,128)(2,1)S(1)}, u32[]{:S(2)}, u32[]{:S(2)}) async-start(bf16[32,4,384]{2,1,0:T(4,128)(2,1)} %bitcast.6), calls=%async_computation | async-start | bytes 196608 | tf_op jit(solution)/shard_map/all_to_all | solution.py:399
  12.4 1.6 %collective-permute-start.2 = (f32[5,6,128]{2,1,0:T(8,128)S(1)}, f32[5,6,128]{2,1,0:T(8,128)S(1)}, u32[]{:S(2)}, u32[]{:S(2)}) collective-permute-start(f32[5,6,128]{2,1,0:T(8,128)S(1)} %get-tuple-element.31.refs_0_), channel_id=1, source_target_pairs={{0,3},{1,2},{2,1},{3,0},{4,7},{5,6},{6,5},{7,4},{8,11},{9,10},{10,... | collective-permute-start | bytes 46088 | tf_op jit(solution)/shard_map/ppermute | solution.py:396
  13.9 0.4 collective-permute-start.1
  14.3 0.0 collective-permute-start
  14.3 1.3 %collective-permute-done.2.refs_3_ = f32[5,6,128]{2,1,0:T(8,128)S(1)} collective-permute-done((f32[5,6,128]{2,1,0:T(8,128)S(1)}, f32[5,6,128]{2,1,0:T(8,128)S(1)}, u32[]{:S(2)}, u32[]{:S(2)}) %collective-permute-start.2) | collective-permute-done | bytes 15392 | tf_op jit(solution)/shard_map/ppermute | solution.py:396
  15.6 2.2 %collective-permute-done.1.refs_2_ = f32[5,6,128]{2,1,0:T(8,128)S(1)} collective-permute-done((f32[5,6,128]{2,1,0:T(8,128)S(1)}, f32[5,6,128]{2,1,0:T(8,128)S(1)}, u32[]{:S(2)}, u32[]{:S(2)}) %collective-permute-start.1) | collective-permute-done | bytes 15392 | tf_op jit(solution)/shard_map/ppermute | solution.py:396
  17.8 0.0 collective-permute-done.refs_1_
  17.8 2.4 %all-to-all-done.recv = bf16[32,4,384]{2,1,0:T(4,128)(2,1)S(1)} async-done(((bf16[32,4,384]{2,1,0:T(4,128)(2,1)}), bf16[32,4,384]{2,1,0:T(4,128)(2,1)S(1)}, u32[]{:S(2)}, u32[]{:S(2)}) %all-to-all-start) | async-done | bytes 98336 | tf_op jit(solution)/shard_map/all_to_all | solution.py:399
  20.2 0.8 %step.3 = (bf16[32,4,384]{2,1,0:T(4,128)(2,1)S(1)}, f32[24,128]{1,0:T(8,128)S(1)}, f32[24,128]{1,0:T(8,128)S(1)}, f32[5,24,128]{2,1,0:T(8,128)S(1)}, f32[2,96,128]{2,1,0:T(8,128)S(1)}) custom-call(bf16[32,4,384]{2,1,0:T(4,128)(2,1)S(1)} %all-to-all-done.recv, f32[24,128]{1,0:T(8,128)S(1)} %get-tuple-element.25.guess, ...), custom_call_target="tpu_custom_call" | custom-call | flops 3145728 | bytes 49152 | tf_op jit(solution)/shard_map/step/pallas_call | solution.py:348
  20.9 9.8 %all_to_all.20.recv = bf16[32,4,384]{2,1,0:T(4,128)(2,1)S(1)} all-to-all(bf16[32,4,384]{2,1,0:T(4,128)(2,1)S(1)} %get-tuple-element.32), channel_id=1, replica_groups=mesh['src'=8,'rcv'=4] {'src','rcv'}, dimensions={0} | all-to-all | bytes 196608 | tf_op jit(solution)/shard_map/all_to_all | solution.py:427
  30.8 0.7 %step.4 = (bf16[32,4,384]{2,1,0:T(4,128)(2,1)S(1)}, f32[24,128]{1,0:T(8,128)S(1)}, f32[24,128]{1,0:T(8,128)S(1)}, f32[1,96,128]{2,1,0:T(8,128)S(1)}) custom-call(bf16[32,4,384]{2,1,0:T(4,128)(2,1)S(1)} %all_to_all.20.recv, f32[24,128]{1,0:T(8,128)S(1)} %get-tuple-element.33.guess.refs_0_, f32[2,96,128]{2,1,0:T(8,128)S(1)} %get-tuple-element.34.rest, ...), custom_call_target="tpu_custom_call" | custom-call | flops 3145728 | bytes 49152 | tf_op jit(solution)/shard_map/step/pallas_call | solution.py:348
  31.5 9.5 %all_to_all.21.recv = bf16[32,4,384]{2,1,0:T(4,128)(2,1)S(1)} all-to-all(bf16[32,4,384]{2,1,0:T(4,128)(2,1)S(1)} %get-tuple-element.37), channel_id=1, replica_groups=mesh['src'=8,'rcv'=4] {'src','rcv'}, dimensions={0} | all-to-all | bytes 196608 | tf_op jit(solution)/shard_map/all_to_all | solution.py:427
  41.0 0.7 %step.5 = (bf16[8,4,384]{2,1,0:T(4,128)(2,1)S(1)}, f32[24,128]{1,0:T(8,128)S(1)}, f32[24,128]{1,0:T(8,128)S(1)}) custom-call(bf16[32,4,384]{2,1,0:T(4,128)(2,1)S(1)} %all_to_all.21.recv, f32[24,128]{1,0:T(8,128)S(1)} %get-tuple-element.38.guess.refs_1_, f32[1,96,128]{2,1,0:T(8,128)S(1)} %get-tuple-element.39.rest, ...), custom_call_target="tpu_custom_call" | custom-call | flops 3145728 | bytes 49152 | tf_op jit(solution)/shard_map/step/pallas_call | solution.py:348
  41.6 9.0 %all_to_all.22.recv = bf16[8,4,384]{2,1,0:T(4,128)(2,1)S(1)} all-to-all(bf16[8,4,384]{2,1,0:T(4,128)(2,1)S(1)} %get-tuple-element.41), channel_id=1, replica_groups=mesh['src'=8,'rcv'=4] {'src'}, dimensions={0} | all-to-all | bytes 49152 | tf_op jit(solution)/shard_map/all_to_all | solution.py:427
  50.6 0.0 copy-done
  50.6 0.0 copy-done.1
  50.6 0.0 copy-done.2
  50.7 0.0 copy-done.3
  50.7 0.8 %last.1 = (f32[4,768]{1,0:T(4,128)}, f32[6,128]{1,0:T(8,128)}) custom-call(bf16[8,4,384]{2,1,0:T(4,128)(2,1)S(1)} %all_to_all.22.recv, f32[6,128]{1,0:T(8,128)S(1)} %bitcast.9, f32[6,128]{1,0:T(8,128)S(1)} %bitcast.11, f32[6,128]{1,0:T(8,128)S(1)} %bitcast.13, f32[6,128]{1,0:T(8,128)S(1)} %bitcast.15, f32[24,128]{1,0:T(8,128)S(1)} %get-tuple-element.42.state_in, ...), custom_call_target="tpu_custom_call" | custom-call | flops 1000000 | bytes 15625 | tf_op jit(solution)/shard_map/last/pallas_call | solution.py:348
Async XLA Ops:
  0.6 50.0 %copy-start = (f32[768]{0:T(1024)S(1)}, f32[768]{0:T(1024)}, u32[]{:S(2)}) copy-start(f32[768]{0:T(1024)} %param.15) | copy-start | bytes 9220
  0.6 50.0 %copy-start.1 = (f32[768]{0:T(1024)S(1)}, f32[768]{0:T(1024)}, u32[]{:S(2)}) copy-start(f32[768]{0:T(1024)} %param.16) | copy-start | bytes 9220
  0.7 50.0 %copy-start.2 = (f32[768]{0:T(1024)S(1)}, f32[768]{0:T(1024)}, u32[]{:S(2)}) copy-start(f32[768]{0:T(1024)} %param.17) | copy-start | bytes 9220
  0.7 50.0 %copy-start.3 = (f32[768]{0:T(1024)S(1)}, f32[768]{0:T(1024)}, u32[]{:S(2)}) copy-start(f32[768]{0:T(1024)} %param.18) | copy-start | bytes 9220
  5.0 15.1 %all-to-all-start = ((bf16[32,4,384]{2,1,0:T(4,128)(2,1)}), bf16[32,4,384]{2,1,0:T(4,128)(2,1)S(1)}, u32[]{:S(2)}, u32[]{:S(2)}) async-start(bf16[32,4,384]{2,1,0:T(4,128)(2,1)} %bitcast.6), calls=%async_computation | async-start | bytes 196608 | tf_op jit(solution)/shard_map/all_to_all | solution.py:399
  12.4 3.3 %collective-permute-start.2 = (f32[5,6,128]{2,1,0:T(8,128)S(1)}, f32[5,6,128]{2,1,0:T(8,128)S(1)}, u32[]{:S(2)}, u32[]{:S(2)}) collective-permute-start(f32[5,6,128]{2,1,0:T(8,128)S(1)} %get-tuple-element.31.refs_0_), channel_id=1, source_target_pairs={{0,3},{1,2},{2,1},{3,0},{4,7},{5,6},{6,5},{7,4},{8,11},{9,10},{10,... | collective-permute-start | bytes 46088 | tf_op jit(solution)/shard_map/ppermute | solution.py:396
  13.9 3.9 %collective-permute-start.1 = (f32[5,6,128]{2,1,0:T(8,128)S(1)}, f32[5,6,128]{2,1,0:T(8,128)S(1)}, u32[]{:S(2)}, u32[]{:S(2)}) collective-permute-start(f32[5,6,128]{2,1,0:T(8,128)S(1)} %get-tuple-element.31.refs_0_), channel_id=1, source_target_pairs={{0,2},{1,3},{2,0},{3,1},{4,6},{5,7},{6,4},{7,5},{8,10},{9,11},{10,... | collective-permute-start | bytes 46088 | tf_op jit(solution)/shard_map/ppermute | solution.py:396
  14.3 3.5 %collective-permute-start = (f32[5,6,128]{2,1,0:T(8,128)S(1)}, f32[5,6,128]{2,1,0:T(8,128)S(1)}, u32[]{:S(2)}, u32[]{:S(2)}) collective-permute-start(f32[5,6,128]{2,1,0:T(8,128)S(1)} %get-tuple-element.31.refs_0_), channel_id=1, source_target_pairs={{0,1},{1,0},{2,3},{3,2},{4,5},{5,4},{6,7},{7,6},{8,9},{9,8},{10,11... | collective-permute-start | bytes 46088 | tf_op jit(solution)/shard_map/ppermute | solution.py:396

commit v11 on v10

--- a/solution.py
+++ b/solution.py
@@ -194,7 +194,7 @@
                     acc[at, :] = acc[at, :] + term
         return carry
 
-    lax.fori_loop(0, lags, one_lag, 0)
+    lax.fori_loop(0, lags, one_lag, 0, unroll=2)
     def partials(first_row, count, step):
         low, high = [
             acc[pl.ds(first_row * 8 + part * STEPS + step, count, stride=8), :]

time: 51.7 us -> 51.7 us (level)
  no operation moved by 1% of the time
where the time goes in v11:
time: 51.7 us; the launch traced here: 51.4 us
  blocking collectives  28.3 us (55%)
  starting transfers between devices  9.27 us (18%)
  Pallas kernels  7.26 us (14%)
  waiting for transfers between devices  5.84 us (11%)
  between operations  0.71 us (1%)
    all_to_all x3, blocking collectives, per_device(): lax.all_to_all(send, 'src' if last else ('src', 'rcv'), 0, 0, tiled=True)  28.3 us
    all_to_all x1, starting transfers between devices, per_device(): lax.all_to_all(send.reshape(n_src * n_rcv, *message), ('src', 'rcv'), 0,...  7.31 us
    pallas_call x5, Pallas kernels, call(): pl.pallas_call(body, in_specs=ins, out_specs=out_specs or [vmem] * len(ou...  7.26 us
    ppermute x3, waiting for transfers between devices, per_device(): lax.ppermute(mine, 'rcv', [(at, at ^ turn) for at in range(n_rcv)])  3.49 us
    all_to_all x1, waiting for transfers between devices, per_device(): lax.all_to_all(send.reshape(n_src * n_rcv, *message), ('src', 'rcv'), 0,...  2.36 us
    ppermute x3, starting transfers between devices, per_device(): lax.ppermute(mine, 'rcv', [(at, at ^ turn) for at in range(n_rcv)])  1.96 us
  transfers between devices with their start and end apart: 4, of which 3 were waited for; matrix products, arithmetic and copies ran while one was open for 0% of the time, Pallas kernels for 0%

profile of v11, /device:TPU:0, one launch (start us, length us, event | category | flops | bytes accessed | tf_op | source)
XLA Modules:
  0.0 51.4 jit_solution(2959677224919030640)
XLA Ops:
  0.6 0.0 copy-start
  0.6 0.0 copy-start.1
  0.7 0.0 copy-start.2
  0.7 0.0 copy-start.3
  0.7 4.3 %older.1 = (bf16[8,4,4,384]{3,2,1,0:T(4,128)(2,1)}, f32[3,96,128]{2,1,0:T(8,128)S(1)}, f32[24,128]{1,0:T(8,128)S(1)}, bf16[3,24,64,128]{3,2,1,0:T(8,128)(2,1)S(1...) custom-call(bf16[12,24,64,128]{3,2,1,0:T(8,128)(2,1)} %bitcast.16, ...), custom_call_target="tpu_custom_call" | custom-call | flops 188743680 | bytes 2949120 | tf_op jit(solution)/shard_map/older/pallas_call | solution.py:348
  5.0 7.3 %all-to-all-start = ((bf16[32,4,384]{2,1,0:T(4,128)(2,1)}), bf16[32,4,384]{2,1,0:T(4,128)(2,1)S(1)}, u32[]{:S(2)}, u32[]{:S(2)}) async-start(bf16[32,4,384]{2,1,0:T(4,128)(2,1)} %bitcast.6), calls=%async_computation | async-start | bytes 196608 | tf_op jit(solution)/shard_map/all_to_all | solution.py:399
  12.3 1.6 %collective-permute-start.2 = (f32[5,6,128]{2,1,0:T(8,128)S(1)}, f32[5,6,128]{2,1,0:T(8,128)S(1)}, u32[]{:S(2)}, u32[]{:S(2)}) collective-permute-start(f32[5,6,128]{2,1,0:T(8,128)S(1)} %get-tuple-element.31.refs_0_), channel_id=1, source_target_pairs={{0,3},{1,2},{2,1},{3,0},{4,7},{5,6},{6,5},{7,4},{8,11},{9,10},{10,... | collective-permute-start | bytes 46088 | tf_op jit(solution)/shard_map/ppermute | solution.py:396
  13.9 0.4 collective-permute-start.1
  14.3 0.0 collective-permute-start
  14.3 1.3 %collective-permute-done.2.refs_3_ = f32[5,6,128]{2,1,0:T(8,128)S(1)} collective-permute-done((f32[5,6,128]{2,1,0:T(8,128)S(1)}, f32[5,6,128]{2,1,0:T(8,128)S(1)}, u32[]{:S(2)}, u32[]{:S(2)}) %collective-permute-start.2) | collective-permute-done | bytes 15392 | tf_op jit(solution)/shard_map/ppermute | solution.py:396
  15.6 2.2 %collective-permute-done.1.refs_2_ = f32[5,6,128]{2,1,0:T(8,128)S(1)} collective-permute-done((f32[5,6,128]{2,1,0:T(8,128)S(1)}, f32[5,6,128]{2,1,0:T(8,128)S(1)}, u32[]{:S(2)}, u32[]{:S(2)}) %collective-permute-start.1) | collective-permute-done | bytes 15392 | tf_op jit(solution)/shard_map/ppermute | solution.py:396
  17.8 0.0 collective-permute-done.refs_1_
  17.8 2.4 %all-to-all-done.recv = bf16[32,4,384]{2,1,0:T(4,128)(2,1)S(1)} async-done(((bf16[32,4,384]{2,1,0:T(4,128)(2,1)}), bf16[32,4,384]{2,1,0:T(4,128)(2,1)S(1)}, u32[]{:S(2)}, u32[]{:S(2)}) %all-to-all-start) | async-done | bytes 98336 | tf_op jit(solution)/shard_map/all_to_all | solution.py:399
  20.1 0.8 %step.3 = (bf16[32,4,384]{2,1,0:T(4,128)(2,1)S(1)}, f32[24,128]{1,0:T(8,128)S(1)}, f32[24,128]{1,0:T(8,128)S(1)}, f32[5,24,128]{2,1,0:T(8,128)S(1)}, f32[2,96,128]{2,1,0:T(8,128)S(1)}) custom-call(bf16[32,4,384]{2,1,0:T(4,128)(2,1)S(1)} %all-to-all-done.recv, f32[24,128]{1,0:T(8,128)S(1)} %get-tuple-element.25.guess, ...), custom_call_target="tpu_custom_call" | custom-call | flops 3145728 | bytes 49152 | tf_op jit(solution)/shard_map/step/pallas_call | solution.py:348
  20.9 9.8 %all_to_all.20.recv = bf16[32,4,384]{2,1,0:T(4,128)(2,1)S(1)} all-to-all(bf16[32,4,384]{2,1,0:T(4,128)(2,1)S(1)} %get-tuple-element.32), channel_id=1, replica_groups=mesh['src'=8,'rcv'=4] {'src','rcv'}, dimensions={0} | all-to-all | bytes 196608 | tf_op jit(solution)/shard_map/all_to_all | solution.py:427
  30.7 0.7 %step.4 = (bf16[32,4,384]{2,1,0:T(4,128)(2,1)S(1)}, f32[24,128]{1,0:T(8,128)S(1)}, f32[24,128]{1,0:T(8,128)S(1)}, f32[1,96,128]{2,1,0:T(8,128)S(1)}) custom-call(bf16[32,4,384]{2,1,0:T(4,128)(2,1)S(1)} %all_to_all.20.recv, f32[24,128]{1,0:T(8,128)S(1)} %get-tuple-element.33.guess.refs_0_, f32[2,96,128]{2,1,0:T(8,128)S(1)} %get-tuple-element.34.rest, ...), custom_call_target="tpu_custom_call" | custom-call | flops 3145728 | bytes 49152 | tf_op jit(solution)/shard_map/step/pallas_call | solution.py:348
  31.4 9.5 %all_to_all.21.recv = bf16[32,4,384]{2,1,0:T(4,128)(2,1)S(1)} all-to-all(bf16[32,4,384]{2,1,0:T(4,128)(2,1)S(1)} %get-tuple-element.37), channel_id=1, replica_groups=mesh['src'=8,'rcv'=4] {'src','rcv'}, dimensions={0} | all-to-all | bytes 196608 | tf_op jit(solution)/shard_map/all_to_all | solution.py:427
  40.9 0.7 %step.5 = (bf16[8,4,384]{2,1,0:T(4,128)(2,1)S(1)}, f32[24,128]{1,0:T(8,128)S(1)}, f32[24,128]{1,0:T(8,128)S(1)}) custom-call(bf16[32,4,384]{2,1,0:T(4,128)(2,1)S(1)} %all_to_all.21.recv, f32[24,128]{1,0:T(8,128)S(1)} %get-tuple-element.38.guess.refs_1_, f32[1,96,128]{2,1,0:T(8,128)S(1)} %get-tuple-element.39.rest, ...), custom_call_target="tpu_custom_call" | custom-call | flops 3145728 | bytes 49152 | tf_op jit(solution)/shard_map/step/pallas_call | solution.py:348
  41.6 9.0 %all_to_all.22.recv = bf16[8,4,384]{2,1,0:T(4,128)(2,1)S(1)} all-to-all(bf16[8,4,384]{2,1,0:T(4,128)(2,1)S(1)} %get-tuple-element.41), channel_id=1, replica_groups=mesh['src'=8,'rcv'=4] {'src'}, dimensions={0} | all-to-all | bytes 49152 | tf_op jit(solution)/shard_map/all_to_all | solution.py:427
  50.6 0.0 copy-done
  50.6 0.0 copy-done.1
  50.6 0.0 copy-done.2
  50.6 0.0 copy-done.3
  50.6 0.8 %last.1 = (f32[4,768]{1,0:T(4,128)}, f32[6,128]{1,0:T(8,128)}) custom-call(bf16[8,4,384]{2,1,0:T(4,128)(2,1)S(1)} %all_to_all.22.recv, f32[6,128]{1,0:T(8,128)S(1)} %bitcast.9, f32[6,128]{1,0:T(8,128)S(1)} %bitcast.11, f32[6,128]{1,0:T(8,128)S(1)} %bitcast.13, f32[6,128]{1,0:T(8,128)S(1)} %bitcast.15, f32[24,128]{1,0:T(8,128)S(1)} %get-tuple-element.42.state_in, ...), custom_call_target="tpu_custom_call" | custom-call | flops 1000000 | bytes 15625 | tf_op jit(solution)/shard_map/last/pallas_call | solution.py:348
Async XLA Ops:
  0.6 50.0 %copy-start = (f32[768]{0:T(1024)S(1)}, f32[768]{0:T(1024)}, u32[]{:S(2)}) copy-start(f32[768]{0:T(1024)} %param.15) | copy-start | bytes 9220
  0.6 50.0 %copy-start.1 = (f32[768]{0:T(1024)S(1)}, f32[768]{0:T(1024)}, u32[]{:S(2)}) copy-start(f32[768]{0:T(1024)} %param.16) | copy-start | bytes 9220
  0.7 49.9 %copy-start.2 = (f32[768]{0:T(1024)S(1)}, f32[768]{0:T(1024)}, u32[]{:S(2)}) copy-start(f32[768]{0:T(1024)} %param.17) | copy-start | bytes 9220
  0.7 49.9 %copy-start.3 = (f32[768]{0:T(1024)S(1)}, f32[768]{0:T(1024)}, u32[]{:S(2)}) copy-start(f32[768]{0:T(1024)} %param.18) | copy-start | bytes 9220
  5.0 15.1 %all-to-all-start = ((bf16[32,4,384]{2,1,0:T(4,128)(2,1)}), bf16[32,4,384]{2,1,0:T(4,128)(2,1)S(1)}, u32[]{:S(2)}, u32[]{:S(2)}) async-start(bf16[32,4,384]{2,1,0:T(4,128)(2,1)} %bitcast.6), calls=%async_computation | async-start | bytes 196608 | tf_op jit(solution)/shard_map/all_to_all | solution.py:399
  12.3 3.3 %collective-permute-start.2 = (f32[5,6,128]{2,1,0:T(8,128)S(1)}, f32[5,6,128]{2,1,0:T(8,128)S(1)}, u32[]{:S(2)}, u32[]{:S(2)}) collective-permute-start(f32[5,6,128]{2,1,0:T(8,128)S(1)} %get-tuple-element.31.refs_0_), channel_id=1, source_target_pairs={{0,3},{1,2},{2,1},{3,0},{4,7},{5,6},{6,5},{7,4},{8,11},{9,10},{10,... | collective-permute-start | bytes 46088 | tf_op jit(solution)/shard_map/ppermute | solution.py:396
  13.9 3.9 %collective-permute-start.1 = (f32[5,6,128]{2,1,0:T(8,128)S(1)}, f32[5,6,128]{2,1,0:T(8,128)S(1)}, u32[]{:S(2)}, u32[]{:S(2)}) collective-permute-start(f32[5,6,128]{2,1,0:T(8,128)S(1)} %get-tuple-element.31.refs_0_), channel_id=1, source_target_pairs={{0,2},{1,3},{2,0},{3,1},{4,6},{5,7},{6,4},{7,5},{8,10},{9,11},{10,... | collective-permute-start | bytes 46088 | tf_op jit(solution)/shard_map/ppermute | solution.py:396
  14.3 3.5 %collective-permute-start = (f32[5,6,128]{2,1,0:T(8,128)S(1)}, f32[5,6,128]{2,1,0:T(8,128)S(1)}, u32[]{:S(2)}, u32[]{:S(2)}) collective-permute-start(f32[5,6,128]{2,1,0:T(8,128)S(1)} %get-tuple-element.31.refs_0_), channel_id=1, source_target_pairs={{0,1},{1,0},{2,3},{3,2},{4,5},{5,4},{6,7},{7,6},{8,9},{9,8},{10,11... | collective-permute-start | bytes 46088 | tf_op jit(solution)/shard_map/ppermute | solution.py:396

commit v12 on v11

--- a/solution.py
+++ b/solution.py
@@ -40,9 +40,10 @@
     slip_rate = guess
     for attempt in range(NEWTON_ITERS):
         scaled = slip_rate * factor
-        root = jnp.sqrt(1.0 + scaled * scaled)
-        misfit = shear_total - DAMPING * slip_rate - strength * inverse_sinh(scaled, root)
-        derivative = -DAMPING - strength * factor / root
+        square = 1.0 + scaled * scaled
+        inverse_root = lax.rsqrt(square)
+        misfit = shear_total - DAMPING * slip_rate - strength * inverse_sinh(scaled, square * inverse_root)
+        derivative = -DAMPING - strength * factor * inverse_root
         slip_rate = slip_rate - misfit / derivative
     next_state = state_now + TIME_STEP * state_rate * jnp.tanh(
         jnp.exp(-state_now) - jnp.abs(slip_rate)

time: 51.7 us -> 51.7 us (level)
  no operation moved by 1% of the time
where the time goes in v12:
time: 51.7 us; the launch traced here: 51.4 us
  blocking collectives  28.3 us (55%)
  starting transfers between devices  9.26 us (18%)
  Pallas kernels  7.23 us (14%)
  waiting for transfers between devices  5.84 us (11%)
  between operations  0.71 us (1%)
    all_to_all x3, blocking collectives, per_device(): lax.all_to_all(send, 'src' if last else ('src', 'rcv'), 0, 0, tiled=True)  28.3 us
    all_to_all x1, starting transfers between devices, per_device(): lax.all_to_all(send.reshape(n_src * n_rcv, *message), ('src', 'rcv'), 0,...  7.29 us
    pallas_call x5, Pallas kernels, call(): pl.pallas_call(body, in_specs=ins, out_specs=out_specs or [vmem] * len(ou...  7.23 us
    ppermute x3, waiting for transfers between devices, per_device(): lax.ppermute(mine, 'rcv', [(at, at ^ turn) for at in range(n_rcv)])  3.49 us
    all_to_all x1, waiting for transfers between devices, per_device(): lax.all_to_all(send.reshape(n_src * n_rcv, *message), ('src', 'rcv'), 0,...  2.36 us
    ppermute x3, starting transfers between devices, per_device(): lax.ppermute(mine, 'rcv', [(at, at ^ turn) for at in range(n_rcv)])  1.96 us
  transfers between devices with their start and end apart: 4, of which 3 were waited for; matrix products, arithmetic and copies ran while one was open for 0% of the time, Pallas kernels for 0%

profile of v12, /device:TPU:0, one launch (start us, length us, event | category | flops | bytes accessed | tf_op | source)
XLA Modules:
  0.0 51.4 jit_solution(11860748508261823679)
XLA Ops:
  0.6 0.0 copy-start
  0.6 0.0 copy-start.1
  0.7 0.0 copy-start.2
  0.7 0.0 copy-start.3
  0.7 4.3 %older.1 = (bf16[8,4,4,384]{3,2,1,0:T(4,128)(2,1)}, f32[3,96,128]{2,1,0:T(8,128)S(1)}, f32[24,128]{1,0:T(8,128)S(1)}, bf16[3,24,64,128]{3,2,1,0:T(8,128)(2,1)S(1...) custom-call(bf16[12,24,64,128]{3,2,1,0:T(8,128)(2,1)} %bitcast.16, ...), custom_call_target="tpu_custom_call" | custom-call | flops 188743680 | bytes 2949120 | tf_op jit(solution)/shard_map/older/pallas_call | solution.py:349
  5.0 7.3 %all-to-all-start = ((bf16[32,4,384]{2,1,0:T(4,128)(2,1)}), bf16[32,4,384]{2,1,0:T(4,128)(2,1)S(1)}, u32[]{:S(2)}, u32[]{:S(2)}) async-start(bf16[32,4,384]{2,1,0:T(4,128)(2,1)} %bitcast.6), calls=%async_computation | async-start | bytes 196608 | tf_op jit(solution)/shard_map/all_to_all | solution.py:400
  12.3 1.6 %collective-permute-start.2 = (f32[5,6,128]{2,1,0:T(8,128)S(1)}, f32[5,6,128]{2,1,0:T(8,128)S(1)}, u32[]{:S(2)}, u32[]{:S(2)}) collective-permute-start(f32[5,6,128]{2,1,0:T(8,128)S(1)} %get-tuple-element.31.refs_0_), channel_id=1, source_target_pairs={{0,3},{1,2},{2,1},{3,0},{4,7},{5,6},{6,5},{7,4},{8,11},{9,10},{10,... | collective-permute-start | bytes 46088 | tf_op jit(solution)/shard_map/ppermute | solution.py:397
  13.9 0.4 collective-permute-start.1
  14.2 0.0 collective-permute-start
  14.3 1.3 %collective-permute-done.2.refs_3_ = f32[5,6,128]{2,1,0:T(8,128)S(1)} collective-permute-done((f32[5,6,128]{2,1,0:T(8,128)S(1)}, f32[5,6,128]{2,1,0:T(8,128)S(1)}, u32[]{:S(2)}, u32[]{:S(2)}) %collective-permute-start.2) | collective-permute-done | bytes 15392 | tf_op jit(solution)/shard_map/ppermute | solution.py:397
  15.6 2.2 %collective-permute-done.1.refs_2_ = f32[5,6,128]{2,1,0:T(8,128)S(1)} collective-permute-done((f32[5,6,128]{2,1,0:T(8,128)S(1)}, f32[5,6,128]{2,1,0:T(8,128)S(1)}, u32[]{:S(2)}, u32[]{:S(2)}) %collective-permute-start.1) | collective-permute-done | bytes 15392 | tf_op jit(solution)/shard_map/ppermute | solution.py:397
  17.7 0.0 collective-permute-done.refs_1_
  17.7 2.4 %all-to-all-done.recv = bf16[32,4,384]{2,1,0:T(4,128)(2,1)S(1)} async-done(((bf16[32,4,384]{2,1,0:T(4,128)(2,1)}), bf16[32,4,384]{2,1,0:T(4,128)(2,1)S(1)}, u32[]{:S(2)}, u32[]{:S(2)}) %all-to-all-start) | async-done | bytes 98336 | tf_op jit(solution)/shard_map/all_to_all | solution.py:400
  20.1 0.8 %step.3 = (bf16[32,4,384]{2,1,0:T(4,128)(2,1)S(1)}, f32[24,128]{1,0:T(8,128)S(1)}, f32[24,128]{1,0:T(8,128)S(1)}, f32[5,24,128]{2,1,0:T(8,128)S(1)}, f32[2,96,128]{2,1,0:T(8,128)S(1)}) custom-call(bf16[32,4,384]{2,1,0:T(4,128)(2,1)S(1)} %all-to-all-done.recv, f32[24,128]{1,0:T(8,128)S(1)} %get-tuple-element.25.guess, ...), custom_call_target="tpu_custom_call" | custom-call | flops 3145728 | bytes 49152 | tf_op jit(solution)/shard_map/step/pallas_call | solution.py:349
  20.9 9.8 %all_to_all.20.recv = bf16[32,4,384]{2,1,0:T(4,128)(2,1)S(1)} all-to-all(bf16[32,4,384]{2,1,0:T(4,128)(2,1)S(1)} %get-tuple-element.32), channel_id=1, replica_groups=mesh['src'=8,'rcv'=4] {'src','rcv'}, dimensions={0} | all-to-all | bytes 196608 | tf_op jit(solution)/shard_map/all_to_all | solution.py:428
  30.7 0.7 %step.4 = (bf16[32,4,384]{2,1,0:T(4,128)(2,1)S(1)}, f32[24,128]{1,0:T(8,128)S(1)}, f32[24,128]{1,0:T(8,128)S(1)}, f32[1,96,128]{2,1,0:T(8,128)S(1)}) custom-call(bf16[32,4,384]{2,1,0:T(4,128)(2,1)S(1)} %all_to_all.20.recv, f32[24,128]{1,0:T(8,128)S(1)} %get-tuple-element.33.guess.refs_0_, f32[2,96,128]{2,1,0:T(8,128)S(1)} %get-tuple-element.34.rest, ...), custom_call_target="tpu_custom_call" | custom-call | flops 3145728 | bytes 49152 | tf_op jit(solution)/shard_map/step/pallas_call | solution.py:349
  31.4 9.5 %all_to_all.21.recv = bf16[32,4,384]{2,1,0:T(4,128)(2,1)S(1)} all-to-all(bf16[32,4,384]{2,1,0:T(4,128)(2,1)S(1)} %get-tuple-element.37), channel_id=1, replica_groups=mesh['src'=8,'rcv'=4] {'src','rcv'}, dimensions={0} | all-to-all | bytes 196608 | tf_op jit(solution)/shard_map/all_to_all | solution.py:428
  40.9 0.7 %step.5 = (bf16[8,4,384]{2,1,0:T(4,128)(2,1)S(1)}, f32[24,128]{1,0:T(8,128)S(1)}, f32[24,128]{1,0:T(8,128)S(1)}) custom-call(bf16[32,4,384]{2,1,0:T(4,128)(2,1)S(1)} %all_to_all.21.recv, f32[24,128]{1,0:T(8,128)S(1)} %get-tuple-element.38.guess.refs_1_, f32[1,96,128]{2,1,0:T(8,128)S(1)} %get-tuple-element.39.rest, ...), custom_call_target="tpu_custom_call" | custom-call | flops 3145728 | bytes 49152 | tf_op jit(solution)/shard_map/step/pallas_call | solution.py:349
  41.6 9.0 %all_to_all.22.recv = bf16[8,4,384]{2,1,0:T(4,128)(2,1)S(1)} all-to-all(bf16[8,4,384]{2,1,0:T(4,128)(2,1)S(1)} %get-tuple-element.41), channel_id=1, replica_groups=mesh['src'=8,'rcv'=4] {'src'}, dimensions={0} | all-to-all | bytes 49152 | tf_op jit(solution)/shard_map/all_to_all | solution.py:428
  50.6 0.0 copy-done
  50.6 0.0 copy-done.1
  50.6 0.0 copy-done.2
  50.6 0.0 copy-done.3
  50.6 0.8 %last.1 = (f32[4,768]{1,0:T(4,128)}, f32[6,128]{1,0:T(8,128)}) custom-call(bf16[8,4,384]{2,1,0:T(4,128)(2,1)S(1)} %all_to_all.22.recv, f32[6,128]{1,0:T(8,128)S(1)} %bitcast.9, f32[6,128]{1,0:T(8,128)S(1)} %bitcast.11, f32[6,128]{1,0:T(8,128)S(1)} %bitcast.13, f32[6,128]{1,0:T(8,128)S(1)} %bitcast.15, f32[24,128]{1,0:T(8,128)S(1)} %get-tuple-element.42.state_in, ...), custom_call_target="tpu_custom_call" | custom-call | flops 1000000 | bytes 15625 | tf_op jit(solution)/shard_map/last/pallas_call | solution.py:349
Async XLA Ops:
  0.6 49.9 %copy-start = (f32[768]{0:T(1024)S(1)}, f32[768]{0:T(1024)}, u32[]{:S(2)}) copy-start(f32[768]{0:T(1024)} %param.15) | copy-start | bytes 9220
  0.6 49.9 %copy-start.1 = (f32[768]{0:T(1024)S(1)}, f32[768]{0:T(1024)}, u32[]{:S(2)}) copy-start(f32[768]{0:T(1024)} %param.16) | copy-start | bytes 9220
  0.7 49.9 %copy-start.2 = (f32[768]{0:T(1024)S(1)}, f32[768]{0:T(1024)}, u32[]{:S(2)}) copy-start(f32[768]{0:T(1024)} %param.17) | copy-start | bytes 9220
  0.7 49.9 %copy-start.3 = (f32[768]{0:T(1024)S(1)}, f32[768]{0:T(1024)}, u32[]{:S(2)}) copy-start(f32[768]{0:T(1024)} %param.18) | copy-start | bytes 9220
  5.0 15.1 %all-to-all-start = ((bf16[32,4,384]{2,1,0:T(4,128)(2,1)}), bf16[32,4,384]{2,1,0:T(4,128)(2,1)S(1)}, u32[]{:S(2)}, u32[]{:S(2)}) async-start(bf16[32,4,384]{2,1,0:T(4,128)(2,1)} %bitcast.6), calls=%async_computation | async-start | bytes 196608 | tf_op jit(solution)/shard_map/all_to_all | solution.py:400
  12.3 3.3 %collective-permute-start.2 = (f32[5,6,128]{2,1,0:T(8,128)S(1)}, f32[5,6,128]{2,1,0:T(8,128)S(1)}, u32[]{:S(2)}, u32[]{:S(2)}) collective-permute-start(f32[5,6,128]{2,1,0:T(8,128)S(1)} %get-tuple-element.31.refs_0_), channel_id=1, source_target_pairs={{0,3},{1,2},{2,1},{3,0},{4,7},{5,6},{6,5},{7,4},{8,11},{9,10},{10,... | collective-permute-start | bytes 46088 | tf_op jit(solution)/shard_map/ppermute | solution.py:397
  13.9 3.9 %collective-permute-start.1 = (f32[5,6,128]{2,1,0:T(8,128)S(1)}, f32[5,6,128]{2,1,0:T(8,128)S(1)}, u32[]{:S(2)}, u32[]{:S(2)}) collective-permute-start(f32[5,6,128]{2,1,0:T(8,128)S(1)} %get-tuple-element.31.refs_0_), channel_id=1, source_target_pairs={{0,2},{1,3},{2,0},{3,1},{4,6},{5,7},{6,4},{7,5},{8,10},{9,11},{10,... | collective-permute-start | bytes 46088 | tf_op jit(solution)/shard_map/ppermute | solution.py:397
  14.2 3.5 %collective-permute-start = (f32[5,6,128]{2,1,0:T(8,128)S(1)}, f32[5,6,128]{2,1,0:T(8,128)S(1)}, u32[]{:S(2)}, u32[]{:S(2)}) collective-permute-start(f32[5,6,128]{2,1,0:T(8,128)S(1)} %get-tuple-element.31.refs_0_), channel_id=1, source_target_pairs={{0,1},{1,0},{2,3},{3,2},{4,5},{5,4},{6,7},{7,6},{8,9},{9,8},{10,11... | collective-permute-start | bytes 46088 | tf_op jit(solution)/shard_map/ppermute | solution.py:397

commit v13 on v11

--- a/solution.py
+++ b/solution.py
@@ -163,8 +163,14 @@
     match = top == (lax.broadcasted_iota(jnp.int32, (8, LANES), 1) < HALF)
     zero = jnp.zeros((8, LANES), jnp.float32)
 
+    handed_on = pltpu.make_async_copy(panels.at[recent_lags], recent, out_sems.at[n_rcv])
+
     def one_lag(lag, carry):
         panel_copy(lag).wait()
+
+        @pl.when(lag == STEPS)
+        def _():
+            handed_on.start()
 
         @pl.when(lag + IN_FLIGHT < lags)
         def _():
@@ -206,14 +212,13 @@
     outgoing = [
         pltpu.make_async_copy(messages, send.at[:, dup], out_sems.at[dup]) for dup in range(n_rcv)
     ]
-    outgoing.append(pltpu.make_async_copy(panel_buf.at[recent_lags], recent, out_sems.at[n_rcv]))
     for copy in outgoing:
         copy.start()
     make_tables(rows_now, cols_now, scales_now, gather, scatter, weights)
     for step in range(1, STEPS):
         rest[step - 1] = partials(0, recv_blocks, step)
     guess[...] = sources[pl.ds(LEAD + lags - 1, src_blocks // 2, stride=2 * TAPS), :]
-    for copy in outgoing + smalls[7:]:
+    for copy in outgoing + smalls[7:] + [handed_on]:
         copy.wait()
 
 

time: 51.7 us -> 51.7 us (level)
  no operation moved by 1% of the time
where the time goes in v13:
time: 51.7 us; the launch traced here: 51.5 us
  blocking collectives  28.3 us (55%)
  starting transfers between devices  9.28 us (18%)
  Pallas kernels  7.31 us (14%)
  waiting for transfers between devices  5.84 us (11%)
  between operations  0.71 us (1%)
    all_to_all x3, blocking collectives, per_device(): lax.all_to_all(send, 'src' if last else ('src', 'rcv'), 0, 0, tiled=True)  28.3 us
    all_to_all x1, starting transfers between devices, per_device(): lax.all_to_all(send.reshape(n_src * n_rcv, *message), ('src', 'rcv'), 0,...  7.32 us
    pallas_call x5, Pallas kernels, call(): pl.pallas_call(body, in_specs=ins, out_specs=out_specs or [vmem] * len(ou...  7.31 us
    ppermute x3, waiting for transfers between devices, per_device(): lax.ppermute(mine, 'rcv', [(at, at ^ turn) for at in range(n_rcv)])  3.49 us
    all_to_all x1, waiting for transfers between devices, per_device(): lax.all_to_all(send.reshape(n_src * n_rcv, *message), ('src', 'rcv'), 0,...  2.36 us
    ppermute x3, starting transfers between devices, per_device(): lax.ppermute(mine, 'rcv', [(at, at ^ turn) for at in range(n_rcv)])  1.96 us
  transfers between devices with their start and end apart: 4, of which 3 were waited for; matrix products, arithmetic and copies ran while one was open for 0% of the time, Pallas kernels for 0%

profile of v13, /device:TPU:0, one launch (start us, length us, event | category | flops | bytes accessed | tf_op | source)
XLA Modules:
  0.0 51.5 jit_solution(716749146336854135)
XLA Ops:
  0.6 0.0 copy-start
  0.6 0.0 copy-start.1
  0.7 0.0 copy-start.2
  0.7 0.0 copy-start.3
  0.7 4.4 %older.1 = (bf16[8,4,4,384]{3,2,1,0:T(4,128)(2,1)}, f32[3,96,128]{2,1,0:T(8,128)S(1)}, f32[24,128]{1,0:T(8,128)S(1)}, bf16[3,24,64,128]{3,2,1,0:T(8,128)(2,1)S(1...) custom-call(bf16[12,24,64,128]{3,2,1,0:T(8,128)(2,1)} %bitcast.16, ...), custom_call_target="tpu_custom_call" | custom-call | flops 188743680 | bytes 2949120 | tf_op jit(solution)/shard_map/older/pallas_call | solution.py:353
  5.0 7.3 %all-to-all-start = ((bf16[32,4,384]{2,1,0:T(4,128)(2,1)}), bf16[32,4,384]{2,1,0:T(4,128)(2,1)S(1)}, u32[]{:S(2)}, u32[]{:S(2)}) async-start(bf16[32,4,384]{2,1,0:T(4,128)(2,1)} %bitcast.6), calls=%async_computation | async-start | bytes 196608 | tf_op jit(solution)/shard_map/all_to_all | solution.py:404
  12.4 1.6 %collective-permute-start.2 = (f32[5,6,128]{2,1,0:T(8,128)S(1)}, f32[5,6,128]{2,1,0:T(8,128)S(1)}, u32[]{:S(2)}, u32[]{:S(2)}) collective-permute-start(f32[5,6,128]{2,1,0:T(8,128)S(1)} %get-tuple-element.31.refs_0_), channel_id=1, source_target_pairs={{0,3},{1,2},{2,1},{3,0},{4,7},{5,6},{6,5},{7,4},{8,11},{9,10},{10,... | collective-permute-start | bytes 46088 | tf_op jit(solution)/shard_map/ppermute | solution.py:401
  14.0 0.4 collective-permute-start.1
  14.3 0.0 collective-permute-start
  14.3 1.3 %collective-permute-done.2.refs_3_ = f32[5,6,128]{2,1,0:T(8,128)S(1)} collective-permute-done((f32[5,6,128]{2,1,0:T(8,128)S(1)}, f32[5,6,128]{2,1,0:T(8,128)S(1)}, u32[]{:S(2)}, u32[]{:S(2)}) %collective-permute-start.2) | collective-permute-done | bytes 15392 | tf_op jit(solution)/shard_map/ppermute | solution.py:401
  15.6 2.2 %collective-permute-done.1.refs_2_ = f32[5,6,128]{2,1,0:T(8,128)S(1)} collective-permute-done((f32[5,6,128]{2,1,0:T(8,128)S(1)}, f32[5,6,128]{2,1,0:T(8,128)S(1)}, u32[]{:S(2)}, u32[]{:S(2)}) %collective-permute-start.1) | collective-permute-done | bytes 15392 | tf_op jit(solution)/shard_map/ppermute | solution.py:401
  17.8 0.0 collective-permute-done.refs_1_
  17.8 2.4 %all-to-all-done.recv = bf16[32,4,384]{2,1,0:T(4,128)(2,1)S(1)} async-done(((bf16[32,4,384]{2,1,0:T(4,128)(2,1)}), bf16[32,4,384]{2,1,0:T(4,128)(2,1)S(1)}, u32[]{:S(2)}, u32[]{:S(2)}) %all-to-all-start) | async-done | bytes 98336 | tf_op jit(solution)/shard_map/all_to_all | solution.py:404
  20.2 0.8 %step.3 = (bf16[32,4,384]{2,1,0:T(4,128)(2,1)S(1)}, f32[24,128]{1,0:T(8,128)S(1)}, f32[24,128]{1,0:T(8,128)S(1)}, f32[5,24,128]{2,1,0:T(8,128)S(1)}, f32[2,96,128]{2,1,0:T(8,128)S(1)}) custom-call(bf16[32,4,384]{2,1,0:T(4,128)(2,1)S(1)} %all-to-all-done.recv, f32[24,128]{1,0:T(8,128)S(1)} %get-tuple-element.25.guess, ...), custom_call_target="tpu_custom_call" | custom-call | flops 3145728 | bytes 49152 | tf_op jit(solution)/shard_map/step/pallas_call | solution.py:353
  20.9 9.8 %all_to_all.20.recv = bf16[32,4,384]{2,1,0:T(4,128)(2,1)S(1)} all-to-all(bf16[32,4,384]{2,1,0:T(4,128)(2,1)S(1)} %get-tuple-element.32), channel_id=1, replica_groups=mesh['src'=8,'rcv'=4] {'src','rcv'}, dimensions={0} | all-to-all | bytes 196608 | tf_op jit(solution)/shard_map/all_to_all | solution.py:432
  30.8 0.7 %step.4 = (bf16[32,4,384]{2,1,0:T(4,128)(2,1)S(1)}, f32[24,128]{1,0:T(8,128)S(1)}, f32[24,128]{1,0:T(8,128)S(1)}, f32[1,96,128]{2,1,0:T(8,128)S(1)}) custom-call(bf16[32,4,384]{2,1,0:T(4,128)(2,1)S(1)} %all_to_all.20.recv, f32[24,128]{1,0:T(8,128)S(1)} %get-tuple-element.33.guess.refs_0_, f32[2,96,128]{2,1,0:T(8,128)S(1)} %get-tuple-element.34.rest, ...), custom_call_target="tpu_custom_call" | custom-call | flops 3145728 | bytes 49152 | tf_op jit(solution)/shard_map/step/pallas_call | solution.py:353
  31.5 9.5 %all_to_all.21.recv = bf16[32,4,384]{2,1,0:T(4,128)(2,1)S(1)} all-to-all(bf16[32,4,384]{2,1,0:T(4,128)(2,1)S(1)} %get-tuple-element.37), channel_id=1, replica_groups=mesh['src'=8,'rcv'=4] {'src','rcv'}, dimensions={0} | all-to-all | bytes 196608 | tf_op jit(solution)/shard_map/all_to_all | solution.py:432
  41.0 0.7 %step.5 = (bf16[8,4,384]{2,1,0:T(4,128)(2,1)S(1)}, f32[24,128]{1,0:T(8,128)S(1)}, f32[24,128]{1,0:T(8,128)S(1)}) custom-call(bf16[32,4,384]{2,1,0:T(4,128)(2,1)S(1)} %all_to_all.21.recv, f32[24,128]{1,0:T(8,128)S(1)} %get-tuple-element.38.guess.refs_1_, f32[1,96,128]{2,1,0:T(8,128)S(1)} %get-tuple-element.39.rest, ...), custom_call_target="tpu_custom_call" | custom-call | flops 3145728 | bytes 49152 | tf_op jit(solution)/shard_map/step/pallas_call | solution.py:353
  41.7 9.0 %all_to_all.22.recv = bf16[8,4,384]{2,1,0:T(4,128)(2,1)S(1)} all-to-all(bf16[8,4,384]{2,1,0:T(4,128)(2,1)S(1)} %get-tuple-element.41), channel_id=1, replica_groups=mesh['src'=8,'rcv'=4] {'src'}, dimensions={0} | all-to-all | bytes 49152 | tf_op jit(solution)/shard_map/all_to_all | solution.py:432
  50.7 0.0 copy-done
  50.7 0.0 copy-done.1
  50.7 0.0 copy-done.2
  50.7 0.0 copy-done.3
  50.7 0.8 %last.1 = (f32[4,768]{1,0:T(4,128)}, f32[6,128]{1,0:T(8,128)}) custom-call(bf16[8,4,384]{2,1,0:T(4,128)(2,1)S(1)} %all_to_all.22.recv, f32[6,128]{1,0:T(8,128)S(1)} %bitcast.9, f32[6,128]{1,0:T(8,128)S(1)} %bitcast.11, f32[6,128]{1,0:T(8,128)S(1)} %bitcast.13, f32[6,128]{1,0:T(8,128)S(1)} %bitcast.15, f32[24,128]{1,0:T(8,128)S(1)} %get-tuple-element.42.state_in, ...), custom_call_target="tpu_custom_call" | custom-call | flops 1000000 | bytes 15625 | tf_op jit(solution)/shard_map/last/pallas_call | solution.py:353
Async XLA Ops:
  0.6 50.0 %copy-start = (f32[768]{0:T(1024)S(1)}, f32[768]{0:T(1024)}, u32[]{:S(2)}) copy-start(f32[768]{0:T(1024)} %param.15) | copy-start | bytes 9220
  0.6 50.0 %copy-start.1 = (f32[768]{0:T(1024)S(1)}, f32[768]{0:T(1024)}, u32[]{:S(2)}) copy-start(f32[768]{0:T(1024)} %param.16) | copy-start | bytes 9220
  0.7 50.0 %copy-start.2 = (f32[768]{0:T(1024)S(1)}, f32[768]{0:T(1024)}, u32[]{:S(2)}) copy-start(f32[768]{0:T(1024)} %param.17) | copy-start | bytes 9220
  0.7 50.0 %copy-start.3 = (f32[768]{0:T(1024)S(1)}, f32[768]{0:T(1024)}, u32[]{:S(2)}) copy-start(f32[768]{0:T(1024)} %param.18) | copy-start | bytes 9220
  5.0 15.1 %all-to-all-start = ((bf16[32,4,384]{2,1,0:T(4,128)(2,1)}), bf16[32,4,384]{2,1,0:T(4,128)(2,1)S(1)}, u32[]{:S(2)}, u32[]{:S(2)}) async-start(bf16[32,4,384]{2,1,0:T(4,128)(2,1)} %bitcast.6), calls=%async_computation | async-start | bytes 196608 | tf_op jit(solution)/shard_map/all_to_all | solution.py:404
  12.4 3.3 %collective-permute-start.2 = (f32[5,6,128]{2,1,0:T(8,128)S(1)}, f32[5,6,128]{2,1,0:T(8,128)S(1)}, u32[]{:S(2)}, u32[]{:S(2)}) collective-permute-start(f32[5,6,128]{2,1,0:T(8,128)S(1)} %get-tuple-element.31.refs_0_), channel_id=1, source_target_pairs={{0,3},{1,2},{2,1},{3,0},{4,7},{5,6},{6,5},{7,4},{8,11},{9,10},{10,... | collective-permute-start | bytes 46088 | tf_op jit(solution)/shard_map/ppermute | solution.py:401
  14.0 3.9 %collective-permute-start.1 = (f32[5,6,128]{2,1,0:T(8,128)S(1)}, f32[5,6,128]{2,1,0:T(8,128)S(1)}, u32[]{:S(2)}, u32[]{:S(2)}) collective-permute-start(f32[5,6,128]{2,1,0:T(8,128)S(1)} %get-tuple-element.31.refs_0_), channel_id=1, source_target_pairs={{0,2},{1,3},{2,0},{3,1},{4,6},{5,7},{6,4},{7,5},{8,10},{9,11},{10,... | collective-permute-start | bytes 46088 | tf_op jit(solution)/shard_map/ppermute | solution.py:401
  14.3 3.5 %collective-permute-start = (f32[5,6,128]{2,1,0:T(8,128)S(1)}, f32[5,6,128]{2,1,0:T(8,128)S(1)}, u32[]{:S(2)}, u32[]{:S(2)}) collective-permute-start(f32[5,6,128]{2,1,0:T(8,128)S(1)} %get-tuple-element.31.refs_0_), channel_id=1, source_target_pairs={{0,1},{1,0},{2,3},{3,2},{4,5},{5,4},{6,7},{7,6},{8,9},{9,8},{10,11... | collective-permute-start | bytes 46088 | tf_op jit(solution)/shard_map/ppermute | solution.py:401
